TPU v7x, 32 devices: a whole 2x2x4 slice. The times are simulated.
32 devices in a mesh: grp: 2 (over x), seq: 16 (over z, y, core).
Axes of the slice: x: 2, y: 2, z: 4, core: 2. Of those that a mesh axis runs over, the one named last changes fastest.
Arguments:
- tokens: bfloat16 [4, 3072, 768], P('grp', 'seq'), may hold values from -6 to 6
- valid_len: int32 [4], P('grp'), may hold values from 768 to 3072, as said below
- query_weight: bfloat16 [768, 768], P(('grp', 'seq')), may hold values from -0.21875 to 0.21875
- query_bias: bfloat16 [768], P(('grp', 'seq')), may hold values from -3 to 3
- key_weight: bfloat16 [768, 768], P(('grp', 'seq')), may hold values from -0.21875 to 0.21875
- value_weight: bfloat16 [768, 768], P(('grp', 'seq')), may hold values from -0.21875 to 0.21875
- value_bias: bfloat16 [768], P(('grp', 'seq')), may hold values from -3 to 3
- output_weight: bfloat16 [768, 768], P(('grp', 'seq')), may hold values from -6 to 6
- output_bias: bfloat16 [768], P(('grp', 'seq')), may hold values from -3 to 3
- first_gain: bfloat16 [768], P(('grp', 'seq')), may hold values from 0.099609375 to 1.8984375
- first_shift: bfloat16 [768], P(('grp', 'seq')), may hold values from -3 to 3
- inner_weight: bfloat16 [768, 3072], P(('grp', 'seq')), may hold values from -0.21875 to 0.21875
- inner_bias: bfloat16 [3072], P(('grp', 'seq')), may hold values from -3 to 3
- outer_weight: bfloat16 [3072, 768], P(('grp', 'seq')), may hold values from -0.109375 to 0.109375
- outer_bias: bfloat16 [768], P(('grp', 'seq')), may hold values from -3 to 3
- second_gain: bfloat16 [768], P(('grp', 'seq')), may hold values from 0.099609375 to 1.8984375
- second_shift: bfloat16 [768], P(('grp', 'seq')), may hold values from -3 to 3
- grad_out: bfloat16 [4, 3072, 768], P('grp', 'seq'), may hold values from -6 to 6
Outputs:
- layer_output: bfloat16 [4, 3072, 768], P('grp', 'seq')
- dtokens: bfloat16 [4, 3072, 768], P('grp', 'seq')
- dquery_weight: float32 [768, 768], P('seq')
- dquery_bias: float32 [768], P('seq')
- dkey_weight: float32 [768, 768], P('seq')
- dvalue_weight: float32 [768, 768], P('seq')
- dvalue_bias: float32 [768], P('seq')
- doutput_weight: float32 [768, 768], P('seq')
- doutput_bias: float32 [768], P('seq')
- dfirst_gain: float32 [768], P('seq')
- dfirst_shift: float32 [768], P('seq')
- dinner_weight: float32 [768, 3072], P('seq')
- dinner_bias: float32 [3072], P('seq')
- douter_weight: float32 [3072, 768], P('seq')
- douter_bias: float32 [768], P('seq')
- dsecond_gain: float32 [768], P('seq')
- dsecond_shift: float32 [768], P('seq')
Inputs may be any that keep to these rules, and one draw needn't show every extreme that they name: Sequence n takes only its first valid_len[n] positions as keys; in every draw some sequence takes all 3072.
All inputs are finite; a program needn't handle non-finite values.
Results may differ from a plain program's by a relative error of at most 0.023.
Values may be sent and summed in bfloat16 or wider, within the bound.
No kernel may reach another device: no remote copies, remote signals or barrier semaphores. Data moves between devices by JAX's collectives and lax.ppermute only.
A program may use at most 320 MiB of HBM per device.

v0:
```python
from functools import partial

import jax
import jax.numpy as jnp
from jax import lax
from jax.sharding import PartitionSpec as P

HEADS = 12
HEAD = 64


score_scale = 0.125
epsilon = 1e-12
masked_score = -1e30


def shortened(value):
    return jax.tree.map(lambda a: a.astype(jnp.bfloat16) if a.dtype == jnp.float32 else a, value)


def layer_norm(hidden, norm_gain, norm_shift):
    centred = hidden - jnp.mean(hidden, axis=-1, keepdims=True)
    spread = jnp.mean(centred * centred, axis=-1, keepdims=True)
    return centred * lax.rsqrt(spread + epsilon) * norm_gain + norm_shift


def block_scores(queries, key_block, block_start, valid_count):
    raw_scores = (
        jnp.einsum("qhd,khd->hqk", queries, key_block, preferred_element_type=jnp.float32)
        * score_scale
    )
    position = block_start + jnp.arange(key_block.shape[0], dtype=jnp.int32)
    return jnp.where((position < valid_count)[None, None, :], raw_scores, masked_score)


def key_layout(all_keys, all_values):
    length = all_keys.shape[0]
    block_rows = min(1024, length)
    block_count = length // block_rows
    key_blocks = all_keys.reshape(block_count, block_rows, HEADS, HEAD)
    value_blocks = all_values.reshape(block_count, block_rows, HEADS, HEAD)
    starts = jnp.arange(block_count, dtype=jnp.int32) * block_rows
    return (key_blocks, value_blocks, starts)


def unchanged(running):
    return running


def attend_forward(queries, all_keys, all_values, valid_count):
    key_blocks, value_blocks, starts = key_layout(all_keys, all_values)
    query_rows = queries.shape[0]

    def stats_step(running, pieces):
        key_block, block_start = pieces

        def stats_update(current):
            row_peak, row_total = current
            scores = block_scores(queries, key_block, block_start, valid_count)
            fresh_peak = jnp.maximum(row_peak, jnp.max(scores, axis=-1))
            row_total = row_total * jnp.exp(row_peak - fresh_peak) + jnp.sum(
                jnp.exp(scores - fresh_peak[..., None]), axis=-1
            )
            return (fresh_peak, row_total)

        return (lax.cond(block_start < valid_count, stats_update, unchanged, running), None)

    initial = (
        jnp.full((HEADS, query_rows), masked_score, jnp.float32),
        jnp.zeros((HEADS, query_rows), jnp.float32),
    )
    row_peak, row_total = lax.scan(stats_step, initial, (key_blocks, starts))[0]
    log_total = row_peak + jnp.log(row_total)

    def value_step(context, pieces):
        key_block, value_block, block_start = pieces

        def value_update(current):
            scores = block_scores(queries, key_block, block_start, valid_count)
            probs = jnp.exp(scores - log_total[..., None]).astype(jnp.bfloat16)
            return current + jnp.einsum(
                "hqk,khd->qhd", probs, value_block, preferred_element_type=jnp.float32
            )

        return (lax.cond(block_start < valid_count, value_update, unchanged, context), None)

    empty = jnp.zeros((query_rows, HEADS, HEAD), jnp.float32)
    context = lax.scan(value_step, empty, (key_blocks, value_blocks, starts))[0]
    return (context, log_total)


def attend_backward(queries, all_keys, all_values, valid_count, log_total, dcontext, delta):
    key_blocks, value_blocks, starts = key_layout(all_keys, all_values)
    length = all_keys.shape[0]

    def grad_step(dqueries, pieces):
        key_block, value_block, block_start = pieces

        def grad_update(current):
            scores = block_scores(queries, key_block, block_start, valid_count)
            probs = jnp.exp(scores - log_total[..., None])
            dprobs = jnp.einsum(
                "qhd,khd->hqk", dcontext, value_block, preferred_element_type=jnp.float32
            )
            dscores = (probs * (dprobs - delta[..., None])).astype(jnp.bfloat16)
            current = current + jnp.einsum(
                "hqk,khd->qhd", dscores, key_block, preferred_element_type=jnp.float32
            )
            dkey_block = jnp.einsum(
                "hqk,qhd->khd", dscores, queries, preferred_element_type=jnp.float32
            )
            dvalue_block = jnp.einsum(
                "hqk,qhd->khd",
                probs.astype(jnp.bfloat16),
                dcontext,
                preferred_element_type=jnp.float32,
            )
            return (current, (dkey_block, dvalue_block))

        def skipped(current):
            nothing = jnp.zeros(key_block.shape, jnp.float32)
            return (current, (nothing, nothing))

        return lax.cond(block_start < valid_count, grad_update, skipped, dqueries)

    empty = jnp.zeros(queries.shape, jnp.float32)
    dqueries, block_grads = lax.scan(grad_step, empty, (key_blocks, value_blocks, starts))
    dkey_all = block_grads[0].reshape(length, HEADS * HEAD) * score_scale
    dvalue_all = block_grads[1].reshape(length, HEADS * HEAD)
    return (dqueries * score_scale, dkey_all, dvalue_all)


def column_sums(matrix):
    return jnp.sum(matrix.astype(jnp.float32), axis=0)


def micro_step(weights, inputs, valid_count, cotangent):
    (
        query_weight,
        query_bias,
        key_weight,
        value_weight,
        value_bias,
        output_weight,
        output_bias,
        first_gain,
        first_shift,
        inner_weight,
        inner_bias,
        outer_weight,
        outer_bias,
        second_gain,
        second_shift,
    ) = weights
    token_rows, width = inputs.shape
    shaped = (token_rows, HEADS, HEAD)
    queries = (
        jnp.dot(inputs, query_weight, preferred_element_type=jnp.float32) + query_bias
    ).astype(jnp.bfloat16)
    key_rows = jnp.dot(inputs, key_weight, preferred_element_type=jnp.float32).astype(jnp.bfloat16)
    value_rows = (
        jnp.dot(inputs, value_weight, preferred_element_type=jnp.float32) + value_bias
    ).astype(jnp.bfloat16)
    all_keys, all_values = (
        lax.all_gather(key_rows, "seq", axis=0, tiled=True),
        lax.all_gather(value_rows, "seq", axis=0, tiled=True),
    )
    context_full, log_total = attend_forward(
        queries.reshape(shaped), all_keys, all_values, valid_count
    )
    context = context_full.reshape(token_rows, width).astype(jnp.bfloat16)
    hidden_one = (
        inputs.astype(jnp.float32)
        + jnp.dot(context, output_weight, preferred_element_type=jnp.float32)
        + output_bias
    )
    norm_one, norm_back_one = jax.vjp(
        layer_norm, hidden_one, first_gain.astype(jnp.float32), first_shift.astype(jnp.float32)
    )
    first_out = norm_one.astype(jnp.bfloat16)
    inner_pre = jnp.dot(first_out, inner_weight, preferred_element_type=jnp.float32) + inner_bias
    active_full, gelu_back = jax.vjp(partial(jax.nn.gelu, approximate=False), inner_pre)
    active = active_full.astype(jnp.bfloat16)
    hidden_two = (
        first_out.astype(jnp.float32)
        + jnp.dot(active, outer_weight, preferred_element_type=jnp.float32)
        + outer_bias
    )
    layer_out, norm_back_two = jax.vjp(
        layer_norm, hidden_two, second_gain.astype(jnp.float32), second_shift.astype(jnp.float32)
    )
    dhidden_two, dsecond_gain, dsecond_shift = norm_back_two(cotangent.astype(jnp.float32))
    douter = dhidden_two.astype(jnp.bfloat16)
    douter_bias = column_sums(douter)
    douter_weight = jnp.einsum("tf,td->fd", active, douter, preferred_element_type=jnp.float32)
    dactive = jnp.einsum("td,fd->tf", douter, outer_weight, preferred_element_type=jnp.float32)
    dinner = gelu_back(dactive)[0].astype(jnp.bfloat16)
    dinner_bias = column_sums(dinner)
    dinner_weight = jnp.einsum("td,tf->df", first_out, dinner, preferred_element_type=jnp.float32)
    dfirst = dhidden_two + jnp.einsum(
        "tf,df->td", dinner, inner_weight, preferred_element_type=jnp.float32
    )
    dhidden_one, dfirst_gain, dfirst_shift = norm_back_one(dfirst)
    dattend = dhidden_one.astype(jnp.bfloat16)
    doutput_bias = column_sums(dattend)
    doutput_weight = jnp.einsum("te,td->ed", context, dattend, preferred_element_type=jnp.float32)
    dcontext = jnp.einsum(
        "td,ed->te", dattend, output_weight, preferred_element_type=jnp.float32
    ).astype(jnp.bfloat16)
    dcontext_heads = dcontext.reshape(shaped)
    delta = jnp.einsum("qhd,qhd->hq", dcontext_heads.astype(jnp.float32), context_full)
    dqueries, dkey_all, dvalue_all = attend_backward(
        queries.reshape(shaped), all_keys, all_values, valid_count, log_total, dcontext_heads, delta
    )
    dkey_rows, dvalue_rows = (
        lax.psum_scatter(
            dkey_all.astype(jnp.bfloat16), "seq", scatter_dimension=0, tiled=True
        ).astype(jnp.float32),
        lax.psum_scatter(
            dvalue_all.astype(jnp.bfloat16), "seq", scatter_dimension=0, tiled=True
        ).astype(jnp.float32),
    )
    dquery_low = dqueries.reshape(token_rows, width).astype(jnp.bfloat16)
    dkey_low = dkey_rows.astype(jnp.bfloat16)
    dvalue_low = dvalue_rows.astype(jnp.bfloat16)
    dinputs = dhidden_one
    dinputs = dinputs + jnp.einsum(
        "te,de->td", dquery_low, query_weight, preferred_element_type=jnp.float32
    )
    dinputs = dinputs + jnp.einsum(
        "te,de->td", dkey_low, key_weight, preferred_element_type=jnp.float32
    )
    dinputs = dinputs + jnp.einsum(
        "te,de->td", dvalue_low, value_weight, preferred_element_type=jnp.float32
    )
    dquery_weight = jnp.einsum("td,te->de", inputs, dquery_low, preferred_element_type=jnp.float32)
    dkey_weight = jnp.einsum("td,te->de", inputs, dkey_low, preferred_element_type=jnp.float32)
    dvalue_weight = jnp.einsum("td,te->de", inputs, dvalue_low, preferred_element_type=jnp.float32)
    gradients = (
        dquery_weight,
        column_sums(dquery_low),
        dkey_weight,
        dvalue_weight,
        column_sums(dvalue_low),
        doutput_weight,
        doutput_bias,
        dfirst_gain,
        dfirst_shift,
        dinner_weight,
        dinner_bias,
        douter_weight,
        douter_bias,
        dsecond_gain,
        dsecond_shift,
    )
    return (layer_out.astype(jnp.bfloat16), dinputs.astype(jnp.bfloat16), gradients)


def per_device(
    tokens,
    valid_len,
    query_weight,
    query_bias,
    key_weight,
    value_weight,
    value_bias,
    output_weight,
    output_bias,
    first_gain,
    first_shift,
    inner_weight,
    inner_bias,
    outer_weight,
    outer_bias,
    second_gain,
    second_shift,
    grad_out,
):
    outputs = []
    input_grads = []
    totals = None
    for micro_index in range(tokens.shape[0]):
        gathered = (
            lax.all_gather(query_weight, ("grp", "seq"), axis=0, tiled=True),
            lax.all_gather(query_bias, ("grp", "seq"), axis=0, tiled=True),
            lax.all_gather(key_weight, ("grp", "seq"), axis=0, tiled=True),
            lax.all_gather(value_weight, ("grp", "seq"), axis=0, tiled=True),
            lax.all_gather(value_bias, ("grp", "seq"), axis=0, tiled=True),
            lax.all_gather(output_weight, ("grp", "seq"), axis=0, tiled=True),
            lax.all_gather(output_bias, ("grp", "seq"), axis=0, tiled=True),
            lax.all_gather(first_gain, ("grp", "seq"), axis=0, tiled=True),
            lax.all_gather(first_shift, ("grp", "seq"), axis=0, tiled=True),
            lax.all_gather(inner_weight, ("grp", "seq"), axis=0, tiled=True),
            lax.all_gather(inner_bias, ("grp", "seq"), axis=0, tiled=True),
            lax.all_gather(outer_weight, ("grp", "seq"), axis=0, tiled=True),
            lax.all_gather(outer_bias, ("grp", "seq"), axis=0, tiled=True),
            lax.all_gather(second_gain, ("grp", "seq"), axis=0, tiled=True),
            lax.all_gather(second_shift, ("grp", "seq"), axis=0, tiled=True),
        )
        layer_out, dinputs, gradients = micro_step(
            gathered, tokens[micro_index], valid_len[micro_index], grad_out[micro_index]
        )
        outputs.append(layer_out)
        input_grads.append(dinputs)
        if micro_index == 0:
            totals = gradients
        else:
            totals = jax.tree.map(jnp.add, totals, gradients)
    partial_rows = jax.tree.map(
        lambda part: part.astype(jnp.float32),
        lax.psum_scatter(shortened(totals), "seq", scatter_dimension=0, tiled=True),
    )
    finals = jax.tree.map(
        lambda part: part.astype(jnp.float32), lax.psum(shortened(partial_rows), "grp")
    )
    return (jnp.stack(outputs), jnp.stack(input_grads)) + tuple(finals)


def solution(mesh):
    in_specs = (
        P("grp", "seq", None),
        P("grp"),
        P(("grp", "seq"), None),
        P(("grp", "seq")),
        P(("grp", "seq"), None),
        P(("grp", "seq"), None),
        P(("grp", "seq")),
        P(("grp", "seq"), None),
        P(("grp", "seq")),
        P(("grp", "seq")),
        P(("grp", "seq")),
        P(("grp", "seq"), None),
        P(("grp", "seq")),
        P(("grp", "seq"), None),
        P(("grp", "seq")),
        P(("grp", "seq")),
        P(("grp", "seq")),
        P("grp", "seq", None),
    )
    out_specs = (
        P("grp", "seq", None),
        P("grp", "seq", None),
        P("seq", None),
        P("seq"),
        P("seq", None),
        P("seq", None),
        P("seq"),
        P("seq", None),
        P("seq"),
        P("seq"),
        P("seq"),
        P("seq", None),
        P("seq"),
        P("seq", None),
        P("seq"),
        P("seq"),
        P("seq"),
    )
    return jax.shard_map(
        per_device, mesh=mesh, in_specs=in_specs, out_specs=out_specs, check_vma=False
    )
```

profile of v0, /device:TPU:0, one launch (start us, length us, event | category | flops | bytes accessed | tf_op | source)
XLA Modules:
  0.0 1561.5 jit_solution(11960454667539289378)
XLA Ops:
  9.6 58.2 %all-gather.11.cloned.1.call-done = bf16[768,768]{1,0:T(8,128)(2,1)} async-done(((bf16[24,768]{1,0:T(8,128)(2,1)}), bf16[768,768]{1,0:T(8,128)(2,1)}) %all-gather.11.cloned.1.call-update) | async-done | bytes 1179664 | tf_op jit(solution)/shard_map/all_gather | solution.py:286
  75.0 39.6 %all-reduce.18 = (bf16[768]{0:T(1024)(128)(2,1)S(1)}, bf16[768]{0:T(1024)(128)(2,1)S(1)}, bf16[768]{0:T(1024)(128)(2,1)S(1)}, bf16[768]{0:T(1024)(128)(2,1)S(1)}...) all-reduce(bf16[768]{0:T(1024)(128)(2,1)S(1)} %dynamic-update-slice, ...), channel_id=1, replica_groups=mesh['grp'=2,'seq'=16] {'grp','seq'}, use_global_device_ids=true, to_apply=%add | all-reduce | flops 9216 | bytes 36864
  114.6 8.9 all-gather.17.cloned.1.call-done
  140.1 39.4 %all-gather.15.cloned.1.call-done = bf16[768,768]{1,0:T(8,128)(2,1)} async-done(((bf16[24,768]{1,0:T(8,128)(2,1)}), bf16[768,768]{1,0:T(8,128)(2,1)}) %all-gather.15.cloned.1.call-update) | async-done | bytes 1179664 | tf_op jit(solution)/shard_map/all_gather | solution.py:284
  182.1 52.2 %all-gather.13.cloned.1.call-done = bf16[3072,768]{1,0:T(8,128)(2,1)} async-done(((bf16[192,768]{1,0:T(8,128)(2,1)}), bf16[3072,768]{1,0:T(8,128)(2,1)}) %all-gather.13.cloned.1.call-update) | async-done | bytes 4718608 | tf_op jit(solution)/shard_map/all_gather | solution.py:165
  234.3 15.3 reshape.314
  249.6 13.6 copy.83
  263.2 25.5 %all-gather.27.cloned.1.call-done = bf16[3072,768]{1,0:T(8,128)(2,1)} async-done(((bf16[192,768]{1,0:T(8,128)(2,1)}), bf16[3072,768]{1,0:T(8,128)(2,1)}) %all-gather.27.cloned.1.call-update) | async-done | bytes 4718608 | tf_op jit(solution)/shard_map/all_gather | solution.py:165
  288.7 15.1 reshape.316
  303.8 13.6 copy.89
  317.4 25.7 %all-gather.19.cloned.1.call-done = bf16[3072,768]{1,0:T(8,128)(2,1)} async-done(((bf16[192,768]{1,0:T(8,128)(2,1)}), bf16[3072,768]{1,0:T(8,128)(2,1)}) %all-gather.19.cloned.1.call-update) | async-done | bytes 4718608 | tf_op jit(solution)/shard_map/all_gather | solution.py:166
  343.1 15.1 reshape.315
  358.2 13.6 copy.84
  371.8 27.4 %while.84 = (s32[]{:T(128)}, f32[12,192]{1,0:T(8,128)S(1)}, f32[12,192]{1,0:T(8,128)S(1)}, s32[3]{0:T(128)}, s32[]{:T(128)}, /*index=5*/bf16[3,1024,12,64]{1,3,2...) while((s32[]{:T(128)}, f32[12,192]{1,0:T(8,128)S(1)}, f32[12,192]{1,0:T(8,128)S(1)}, s32[3]{0:T(128)}, ...), condition=%wide.region_5.6_spmd, body=%wide.region_0.5_spmd.sunk | while | flops 318511616 | bytes 20865760 | solution.py:72
  399.3 28.4 %while.85 = (s32[]{:T(128)}, f32[192,12,64]{0,2,1:T(8,128)S(1)}, s32[3]{0:T(128)}, s32[]{:T(128)}, bf16[3,1024,12,64]{1,3,2,0:T(8,128)(2,1)}, /*index=5*/bf16[19...) while((s32[]{:T(128)}, f32[192,12,64]{0,2,1:T(8,128)S(1)}, ...), condition=%wide.region_9.10_spmd, body=%wide.region_6.9_spmd.sunk | while | flops 613566464 | bytes 4632783 | solution.py:88
  428.6 15.1 reshape.317
  443.7 13.6 copy.90
  457.3 21.2 %while.86 = (s32[]{:T(128)}, f32[12,192]{1,0:T(8,128)S(1)}, f32[12,192]{1,0:T(8,128)S(1)}, s32[3]{0:T(128)}, s32[]{:T(128)}, /*index=5*/bf16[3,1024,12,64]{1,3,2...) while((s32[]{:T(128)}, f32[12,192]{1,0:T(8,128)S(1)}, f32[12,192]{1,0:T(8,128)S(1)}, s32[3]{0:T(128)}, ...), condition=%wide.region_19.20_spmd, body=%wide.region_14.19_spmd.sunk | while | flops 318511616 | bytes 20865760 | solution.py:72
  478.7 21.5 %while.87 = (s32[]{:T(128)}, f32[192,12,64]{0,2,1:T(8,128)S(1)}, s32[3]{0:T(128)}, s32[]{:T(128)}, bf16[3,1024,12,64]{1,3,2,0:T(8,128)(2,1)}, /*index=5*/bf16[19...) while((s32[]{:T(128)}, f32[192,12,64]{0,2,1:T(8,128)S(1)}, ...), condition=%wide.region_23.24_spmd, body=%wide.region_20.23_spmd.sunk | while | flops 613566464 | bytes 4632783 | solution.py:88
  505.2 13.3 all-gather.23.cloned.1.call-done
  518.6 9.1 multiply_convert_fusion.5
  527.7 55.6 %all-gather.25.cloned.1.call-done = bf16[3072,768]{1,0:T(8,128)(2,1)} async-done(((bf16[96,768]{1,0:T(8,128)(2,1)}), bf16[3072,768]{1,0:T(8,128)(2,1)}) %all-gather.25.cloned.1.call-update) | async-done | bytes 4718608 | tf_op jit(solution)/shard_map/all_gather | solution.py:295
  587.6 7.5 multiply_convert_fusion.4
  623.6 65.6 %while.88 = (s32[]{:T(128)}, f32[192,12,64]{0,2,1:T(8,128)}, f32[3,1024,12,64]{1,3,2,0:T(8,128)}, bf16[3,1024,12,64]{1,3,2,0:T(8,128)(2,1)}, s32[3]{0:T(128)}, /...) while((s32[]{:T(128)}, f32[192,12,64]{0,2,1:T(8,128)}, ...), condition=%wide.region_35.36_spmd, body=%wide.region_32.35_spmd.sunk | while | flops 1533691904 | bytes 73306464 | solution.py:127
  626.3 16.5 %conditional.16 = (f32[192,12,64]{0,2,1:T(8,128)}, f32[1,1024,12,64]{1,3,2,0:T(8,128)S(1)}, f32[1,1024,12,64]{1,3,2,0:T(8,128)S(1)}) conditional(s32[]{:T(128)} %convert_element_type.630, f32[192,12,64]{0,2,1:T(8,128)} %get-tuple-element.1687, (s32[]{:T(128)}, s32[]{:T(128)}, bf16[3,1024,12,64]{1,3,2,0:T(8,128)(2,1)}, s32[]{:T(128)}, ...), branch_computations={%region_33.33_spmd, %region_34.34_spmd} | conditional | flops 1533691904 | bytes 60722804 | solution.py:124
  648.2 16.5 %conditional.16 = (f32[192,12,64]{0,2,1:T(8,128)}, f32[1,1024,12,64]{1,3,2,0:T(8,128)S(1)}, f32[1,1024,12,64]{1,3,2,0:T(8,128)S(1)}) conditional(s32[]{:T(128)} %convert_element_type.630, f32[192,12,64]{0,2,1:T(8,128)} %get-tuple-element.1687, (s32[]{:T(128)}, s32[]{:T(128)}, bf16[3,1024,12,64]{1,3,2,0:T(8,128)(2,1)}, s32[]{:T(128)}, ...), branch_computations={%region_33.33_spmd, %region_34.34_spmd} | conditional | flops 1533691904 | bytes 60722804 | solution.py:124
  670.0 16.5 %conditional.16 = (f32[192,12,64]{0,2,1:T(8,128)}, f32[1,1024,12,64]{1,3,2,0:T(8,128)S(1)}, f32[1,1024,12,64]{1,3,2,0:T(8,128)S(1)}) conditional(s32[]{:T(128)} %convert_element_type.630, f32[192,12,64]{0,2,1:T(8,128)} %get-tuple-element.1687, (s32[]{:T(128)}, s32[]{:T(128)}, bf16[3,1024,12,64]{1,3,2,0:T(8,128)(2,1)}, s32[]{:T(128)}, ...), branch_computations={%region_33.33_spmd, %region_34.34_spmd} | conditional | flops 1533691904 | bytes 60722804 | solution.py:124
  689.2 7.3 multiply_convert_fusion.3
  696.5 14.9 copy.143
  711.4 15.6 reshape.291
  738.6 50.1 %while.89 = (s32[]{:T(128)}, f32[192,12,64]{0,2,1:T(8,128)}, f32[3,1024,12,64]{1,3,2,0:T(8,128)}, bf16[3,1024,12,64]{1,3,2,0:T(8,128)(2,1)}, s32[3]{0:T(128)}, /...) while((s32[]{:T(128)}, f32[192,12,64]{0,2,1:T(8,128)}, ...), condition=%wide.region_45.46_spmd, body=%wide.region_42.45_spmd.sunk | while | flops 1533691904 | bytes 73306464 | solution.py:127
  741.2 16.6 %conditional.17 = (f32[192,12,64]{0,2,1:T(8,128)}, f32[1,1024,12,64]{1,3,2,0:T(8,128)S(1)}, f32[1,1024,12,64]{1,3,2,0:T(8,128)S(1)}) conditional(s32[]{:T(128)} %convert_element_type.631, f32[192,12,64]{0,2,1:T(8,128)} %get-tuple-element.1648, (s32[]{:T(128)}, s32[]{:T(128)}, bf16[3,1024,12,64]{1,3,2,0:T(8,128)(2,1)}, s32[]{:T(128)}, ...), branch_computations={%region_43.43_spmd, %region_44.44_spmd} | conditional | flops 1533691904 | bytes 60722804 | solution.py:124
  763.1 16.5 %conditional.17 = (f32[192,12,64]{0,2,1:T(8,128)}, f32[1,1024,12,64]{1,3,2,0:T(8,128)S(1)}, f32[1,1024,12,64]{1,3,2,0:T(8,128)S(1)}) conditional(s32[]{:T(128)} %convert_element_type.631, f32[192,12,64]{0,2,1:T(8,128)} %get-tuple-element.1648, (s32[]{:T(128)}, s32[]{:T(128)}, bf16[3,1024,12,64]{1,3,2,0:T(8,128)(2,1)}, s32[]{:T(128)}, ...), branch_computations={%region_43.43_spmd, %region_44.44_spmd} | conditional | flops 1533691904 | bytes 60722804 | solution.py:124
  796.1 14.9 copy.146
  811.0 15.6 reshape.295
  826.8 15.2 copy.144
  842.0 15.7 %reshape.293 = bf16[3072,768]{1,0:T(8,128)(2,1)} reshape(bf16[3,1024,12,64]{3,2,1,0:T(8,128)(2,1)} %copy.144) | data formatting | bytes 9437184
  857.8 14.9 copy.147
  872.7 15.6 reshape.297
  904.5 74.9 %reduce-scatter.33.cloned.1.call-done = bf16[192,768]{1,0:T(8,128)(2,1)} async-done(((bf16[3072,768]{1,0:T(8,128)(2,1)}), bf16[192,768]{1,0:T(8,128)(2,1)}) %reduce-scatter.33.cloned.1.call-update) | async-done | bytes 294928
  982.3 75.6 %reduce-scatter.37.cloned.1.call-done = bf16[192,768]{1,0:T(8,128)(2,1)} async-done(((bf16[3072,768]{1,0:T(8,128)(2,1)}), bf16[192,768]{1,0:T(8,128)(2,1)}) %reduce-scatter.37.cloned.1.call-update) | async-done | bytes 294928
  1087.7 31.1 %reduce-scatter.39.cloned.1.call-done = bf16[48,768]{1,0:T(8,128)(2,1)} async-done(((bf16[768,768]{1,0:T(8,128)(2,1)}), bf16[48,768]{1,0:T(8,128)(2,1)}) %reduce-scatter.39.cloned.1.call-update) | async-done | bytes 73744
  1123.6 55.7 %reduce-scatter.41.cloned.1.call-done = bf16[48,768]{1,0:T(8,128)(2,1)} async-done(((bf16[768,768]{1,0:T(8,128)(2,1)}), bf16[48,768]{1,0:T(8,128)(2,1)}) %reduce-scatter.41.cloned.1.call-update) | async-done | bytes 73744
  1181.1 58.9 %reduce-scatter.43.cloned.1.call-done = bf16[48,768]{1,0:T(8,128)(2,1)} async-done(((bf16[768,768]{1,0:T(8,128)(2,1)}), bf16[48,768]{1,0:T(8,128)(2,1)}) %reduce-scatter.43.cloned.1.call-update) | async-done | bytes 73744
  1241.7 59.1 %reduce-scatter.25.cloned.1.call-done = bf16[48,768]{1,0:T(8,128)(2,1)} async-done(((bf16[768,768]{1,0:T(8,128)(2,1)}), bf16[48,768]{1,0:T(8,128)(2,1)}) %reduce-scatter.25.cloned.1.call-update) | async-done | bytes 73744 | tf_op jit(solution)/shard_map/reduce_scatter | solution.py:311
  1300.8 78.5 %reduce-scatter.27.cloned.1.call-done = bf16[48,3072]{1,0:T(8,128)(2,1)} async-done(((bf16[768,3072]{1,0:T(8,128)(2,1)}), bf16[48,3072]{1,0:T(8,128)(2,1)}) %reduce-scatter.27.cloned.1.call-update) | async-done | bytes 294928 | tf_op jit(solution)/shard_map/reduce_scatter | solution.py:311
  1379.3 78.5 %reduce-scatter.29.cloned.1.call-done = bf16[192,768]{1,0:T(8,128)(2,1)} async-done(((bf16[3072,768]{1,0:T(8,128)(2,1)}), bf16[192,768]{1,0:T(8,128)(2,1)}) %reduce-scatter.29.cloned.1.call-update) | async-done | bytes 294928 | tf_op jit(solution)/shard_map/reduce_scatter | solution.py:311
  1458.4 58.0 %all-reduce.19 = (bf16[768]{0:T(1024)(128)(2,1)}, bf16[768]{0:T(1024)(128)(2,1)S(1)}, bf16[768]{0:T(1024)(128)(2,1)S(1)}, bf16[768]{0:T(1024)(128)(2,1)}, bf16[7...) all-reduce(bf16[768]{0:T(1024)(128)(2,1)} %convert_element_type.457, ...), channel_id=7, replica_groups=mesh['grp'=2,'seq'=16] {'seq'}, use_global_device_ids=true, to_apply=%region_52.53.clone | all-reduce | flops 9216 | bytes 36864
  (543 shorter events, 437.3 us)
Async XLA Ops:
  7.2 116.4 %copy-start.12 = (bf16[2,192,768]{2,1,0:T(8,128)(2,1)S(1)}, bf16[2,192,768]{2,1,0:T(8,128)(2,1)}, u32[]{:S(2)}) copy-start(bf16[2,192,768]{2,1,0:T(8,128)(2,1)} %param.42) | copy-start | bytes 1769476
  7.2 65.7 %copy-start.88 = (bf16[24]{0:T(256)(128)(2,1)S(1)}, bf16[24]{0:T(256)(128)(2,1)}, u32[]{:S(2)}) copy-start(bf16[24]{0:T(256)(128)(2,1)} %param.57) | copy-start | bytes 148
  7.2 65.9 %copy-start.89 = (bf16[24]{0:T(256)(128)(2,1)S(1)}, bf16[24]{0:T(256)(128)(2,1)}, u32[]{:S(2)}) copy-start(bf16[24]{0:T(256)(128)(2,1)} %param.56) | copy-start | bytes 148
  7.2 66.1 %copy-start.90 = (bf16[24]{0:T(256)(128)(2,1)S(1)}, bf16[24]{0:T(256)(128)(2,1)}, u32[]{:S(2)}) copy-start(bf16[24]{0:T(256)(128)(2,1)} %param.51) | copy-start | bytes 148
  7.2 66.4 %copy-start.91 = (bf16[24]{0:T(256)(128)(2,1)S(1)}, bf16[24]{0:T(256)(128)(2,1)}, u32[]{:S(2)}) copy-start(bf16[24]{0:T(256)(128)(2,1)} %param.52) | copy-start | bytes 148
  7.2 66.6 %copy-start.92 = (bf16[24]{0:T(256)(128)(2,1)S(1)}, bf16[24]{0:T(256)(128)(2,1)}, u32[]{:S(2)}) copy-start(bf16[24]{0:T(256)(128)(2,1)} %param.50) | copy-start | bytes 148
  7.3 66.8 %copy-start.93 = (bf16[24]{0:T(256)(128)(2,1)S(1)}, bf16[24]{0:T(256)(128)(2,1)}, u32[]{:S(2)}) copy-start(bf16[24]{0:T(256)(128)(2,1)} %param.48) | copy-start | bytes 148
  7.3 67.0 %copy-start.94 = (bf16[24]{0:T(256)(128)(2,1)S(1)}, bf16[24]{0:T(256)(128)(2,1)}, u32[]{:S(2)}) copy-start(bf16[24]{0:T(256)(128)(2,1)} %param.45) | copy-start | bytes 148
  7.3 67.3 %copy-start.95 = (bf16[24]{0:T(256)(128)(2,1)S(1)}, bf16[24]{0:T(256)(128)(2,1)}, u32[]{:S(2)}) copy-start(bf16[24]{0:T(256)(128)(2,1)} %param.58) | copy-start | bytes 148
  7.3 67.5 %copy-start.96 = (bf16[96]{0:T(256)(128)(2,1)S(1)}, bf16[96]{0:T(256)(128)(2,1)}, u32[]{:S(2)}) copy-start(bf16[96]{0:T(256)(128)(2,1)} %param.54) | copy-start | bytes 580
  7.3 60.4 %all-gather.11.cloned.1.call-start = ((), (), s32[]{:S(2)}) async-start(), calls=%async_computation.10 | async-start | bytes 1216512 | tf_op jit(solution)/shard_map/all_gather | solution.py:286
  8.0 115.5 %all-gather.17.cloned.1.call-start = ((), (), s32[]{:S(2)}) async-start(), calls=%async_computation.13 | async-start | bytes 1216512 | tf_op jit(solution)/shard_map/all_gather | solution.py:287
  8.8 170.7 %all-gather.15.cloned.1.call-start = ((), (), s32[]{:S(2)}) async-start(), calls=%async_computation.12 | async-start | bytes 1216512 | tf_op jit(solution)/shard_map/all_gather | solution.py:284
  9.5 224.8 %all-gather.13.cloned.1.call-start = ((), (), s32[]{:S(2)}) async-start(), calls=%async_computation.11 | async-start | bytes 5013504 | tf_op jit(solution)/shard_map/all_gather | solution.py:165
  70.2 218.4 %all-gather.27.cloned.1.call-start = ((), (), s32[]{:S(2)}) async-start(), calls=%async_computation.18 | async-start | bytes 5013504 | tf_op jit(solution)/shard_map/all_gather | solution.py:165
  72.8 270.3 %all-gather.19.cloned.1.call-start = ((), (), s32[]{:S(2)}) async-start(), calls=%async_computation.14 | async-start | bytes 5013504 | tf_op jit(solution)/shard_map/all_gather | solution.py:166
  126.0 302.6 %all-gather.29.cloned.1.call-start = ((), (), s32[]{:S(2)}) async-start(), calls=%async_computation.19 | async-start | bytes 5013504 | tf_op jit(solution)/shard_map/all_gather | solution.py:166
  128.4 372.7 %all-gather.21.cloned.1.call-start = ((), (), s32[]{:S(2)}) async-start(), calls=%async_computation.15 | async-start | bytes 1216512 | tf_op jit(solution)/shard_map/all_gather | solution.py:289
  129.2 389.4 %all-gather.23.cloned.1.call-start = ((), (), s32[]{:S(2)}) async-start(), calls=%async_computation.16 | async-start | bytes 4866048 | tf_op jit(solution)/shard_map/all_gather | solution.py:293
  129.9 453.3 %all-gather.25.cloned.1.call-start = ((), (), s32[]{:S(2)}) async-start(), calls=%async_computation.17 | async-start | bytes 4866048 | tf_op jit(solution)/shard_map/all_gather | solution.py:295
  130.5 761.9 %reduce-scatter.31.cloned.1.call-start = ((), (), s32[]{:S(2)}) async-start(), calls=%async_computation.23 | async-start | bytes 5013504
  427.7 16.0 %copy-start.16 = (f32[192,12,64]{0,2,1:T(8,128)}, f32[192,12,64]{0,2,1:T(8,128)S(1)}, u32[]{:S(2)}) copy-start(f32[192,12,64]{0,2,1:T(8,128)S(1)} %get-tuple-element.711) | copy-start | bytes 1769476
  478.7 22.6 %copy-start.61 = (f32[768]{0:T(1024)S(1)}, f32[768]{0:T(1024)}, u32[]{:S(2)}) copy-start(f32[768]{0:T(1024)} %convert_element_type.404) | copy-start | bytes 9220
  503.6 15.0 copy-start.73
  505.2 78.0 %copy-start.43 = (bf16[192,768]{1,0:T(8,128)(2,1)}, bf16[192,768]{1,0:T(8,128)(2,1)S(1)}, u32[]{:S(2)}) copy-start(bf16[192,768]{1,0:T(8,128)(2,1)S(1)} %get-tuple-element.1132) | copy-start | bytes 884740
  505.2 89.8 %copy-start.52 = (bf16[192,768]{1,0:T(8,128)(2,1)}, bf16[192,768]{1,0:T(8,128)(2,1)S(1)}, u32[]{:S(2)}) copy-start(bf16[192,768]{1,0:T(8,128)(2,1)S(1)} %get-tuple-element.1133) | copy-start | bytes 884740
  518.6 64.7 %copy-start.80 = (f32[768]{0:T(1024)S(1)}, f32[768]{0:T(1024)}, u32[]{:S(2)}) copy-start(f32[768]{0:T(1024)} %convert_element_type.411) | copy-start | bytes 9220
  583.3 11.8 slice-start
  614.6 9.0 copy-start.36
  727.0 173.6 %reduce-scatter.35.cloned.1.call-start = ((), (), s32[]{:S(2)}) async-start(), calls=%async_computation.25 | async-start | bytes 5013504
  826.6 152.8 %reduce-scatter.33.cloned.1.call-start = ((), (), s32[]{:S(2)}) async-start(), calls=%async_computation.24 | async-start | bytes 5013504
  857.7 200.2 %reduce-scatter.37.cloned.1.call-start = ((), (), s32[]{:S(2)}) async-start(), calls=%async_computation.26 | async-start | bytes 5013504
  888.4 230.4 %reduce-scatter.39.cloned.1.call-start = ((), (), s32[]{:S(2)}) async-start(), calls=%async_computation.27 | async-start | bytes 1253376
  892.4 287.0 %reduce-scatter.41.cloned.1.call-start = ((), (), s32[]{:S(2)}) async-start(), calls=%async_computation.28 | async-start | bytes 1253376
  904.4 335.6 %reduce-scatter.43.cloned.1.call-start = ((), (), s32[]{:S(2)}) async-start(), calls=%async_computation.29 | async-start | bytes 1253376
  1061.7 239.1 %reduce-scatter.25.cloned.1.call-start = ((), (), s32[]{:S(2)}) async-start(), calls=%async_computation.20 | async-start | bytes 1253376 | tf_op jit(solution)/shard_map/reduce_scatter | solution.py:311
  1064.3 314.9 %reduce-scatter.27.cloned.1.call-start = ((), (), s32[]{:S(2)}) async-start(), calls=%async_computation.21 | async-start | bytes 5013504 | tf_op jit(solution)/shard_map/reduce_scatter | solution.py:311
  1069.6 388.2 %reduce-scatter.29.cloned.1.call-start = ((), (), s32[]{:S(2)}) async-start(), calls=%async_computation.22 | async-start | bytes 5013504 | tf_op jit(solution)/shard_map/reduce_scatter | solution.py:311
  1076.2 468.0 %all-reduce.24.cloned.1.call-start = ((), (), s32[]{:S(2)}) async-start(), calls=%async_computation.30 | async-start | bytes 2506752 | tf_op jit(solution)/shard_map/psum | solution.py:314
  1076.2 10.0 copy-start.23
  1076.2 10.0 copy-start.77
  1086.3 34.2 %copy-start.35 = (bf16[192,768]{1,0:T(8,128)(2,1)S(1)}, bf16[192,768]{1,0:T(8,128)(2,1)}, u32[]{:S(2)}) copy-start(bf16[192,768]{1,0:T(8,128)(2,1)} %reduce-scatter.37.cloned.1.call-done) | copy-start | bytes 884740
  1086.3 34.4 %copy-start.34 = (bf16[192,768]{1,0:T(8,128)(2,1)S(1)}, bf16[192,768]{1,0:T(8,128)(2,1)}, u32[]{:S(2)}) copy-start(bf16[192,768]{1,0:T(8,128)(2,1)} %reduce-scatter.33.cloned.1.call-done) | copy-start | bytes 884740
  1086.3 34.9 %copy-start.11 = (bf16[768,768]{1,0:T(8,128)(2,1)S(1)}, bf16[768,768]{1,0:T(8,128)(2,1)}, u32[]{:S(2)}) copy-start(bf16[768,768]{1,0:T(8,128)(2,1)} %all-gather.11.cloned.1.call-done) | copy-start | bytes 3538948
  1087.7 33.5 %copy-start.41 = (f32[192,768]{1,0:T(8,128)S(1)}, f32[192,768]{1,0:T(8,128)}, u32[]{:S(2)}) copy-start(f32[192,768]{1,0:T(8,128)} %convolution_add_fusion.4) | copy-start | bytes 1769476
  1121.2 419.4 %copy-start.28 = (bf16[768,768]{1,0:T(8,128)(2,1)S(1)}, bf16[768,768]{1,0:T(8,128)(2,1)}, u32[]{:S(2)}) copy-start(bf16[768,768]{1,0:T(8,128)(2,1)} %all-gather.17.cloned.1.call-done) | copy-start | bytes 3538948
  1123.6 418.5 %copy-start.40 = (f32[192,768]{1,0:T(8,128)S(1)}, f32[192,768]{1,0:T(8,128)}, u32[]{:S(2)}) copy-start(f32[192,768]{1,0:T(8,128)} %convolution_add_fusion.7) | copy-start | bytes 1769476
  1530.0 12.2 copy-start.45
  (84 other events, 278.2 us)
Sparse Core Ops, SparseCore 0:
  11.0 56.6 all-gather.10
  70.6 52.8 all-gather.16
  126.5 52.9 all-gather.14
  182.2 52.0 all-gather.12
  237.0 51.6 all-gather.26
  291.4 51.6 all-gather.18
  345.9 51.6 all-gather.28
  400.6 52.5 all-gather.20
  456.0 62.5 all-gather.22
  521.3 61.8 all-gather.24
  727.2 73.8 reduce-scatter.30
  826.7 73.8 reduce-scatter.34
  904.5 74.8 reduce-scatter.32
  983.1 74.7 reduce-scatter.36
  1061.4 57.3 reduce-scatter.38
  1122.2 57.0 reduce-scatter.40
  1182.8 57.1 reduce-scatter.42
  1243.5 57.2 reduce-scatter.24
  1304.7 74.5 reduce-scatter.26
  1383.0 74.7 reduce-scatter.28
  1460.4 43.8 all-reduce.23
where the time goes:
time: 1580 us; the launch traced here: 1560 us
  waiting for transfers between devices  801 us (51%)
  local copies, waits for them, and re-layouts  329 us (21%)
  matrix products  197 us (12%)
  blocking collectives  103 us (7%)
  other arithmetic  87.6 us (6%)
  loops' own time  25.2 us (2%)
  between operations  17 us (1%)
    unnamed x28, waiting for transfers between devices  306 us
    reduce_scatter x3, waiting for transfers between devices, per_device(): lax.psum_scatter(shortened(totals), 'seq', scatter_dimension=0, tiled=True)  216 us
    unnamed x240, local copies, waits for them, and re-layouts  159 us
    unnamed x2, blocking collectives  97.6 us
    all_gather x2, waiting for transfers between devices, micro_step(): lax.all_gather(key_rows, 'seq', axis=0, tiled=True)  77.7 us
    all_gather x1, waiting for transfers between devices, per_device(): lax.all_gather(key_weight, ('grp', 'seq'), axis=0, tiled=True)  58.2 us
    all_gather x1, waiting for transfers between devices, per_device(): lax.all_gather(outer_weight, ('grp', 'seq'), axis=0, tiled=True)  55.6 us
    while x4, local copies, waits for them, and re-layouts, attend_forward(): context = lax.scan(value_step, empty, (key_blocks, value_blocks, starts))[0]  54.4 us
  transfers between devices with their start and end apart: 21, of which 17 were waited for; matrix products, arithmetic and copies ran while one was open for 29% of the time, Pallas kernels for 0%

commit v1 on v0

v1 whole, which is shorter than its diff:
```python
from functools import partial

import jax
import jax.numpy as jnp
from jax import lax
from jax.sharding import PartitionSpec as P

HEADS = 12
HEAD = 64
HEAD_GROUPS = 4
GROUP_WIDTH = HEADS * HEAD // HEAD_GROUPS

score_scale = 0.125
epsilon = 1e-12
masked_score = -1e30


def log2_of(size):
    return size.bit_length() - 1


def flip(value, axis, size, mask):
    return lax.ppermute(value, axis, [(i, i ^ mask) for i in range(size)])


def in_order(mine, theirs, bit):
    return jnp.where(bit == 0, jnp.stack([mine, theirs]), jnp.stack([theirs, mine]))


def pick(pair, bit):
    return jnp.where(bit == 0, pair[0], pair[1])


def layer_norm(hidden, norm_gain, norm_shift):
    centred = hidden - jnp.mean(hidden, axis=-1, keepdims=True)
    spread = jnp.mean(centred * centred, axis=-1, keepdims=True)
    return centred * lax.rsqrt(spread + epsilon) * norm_gain + norm_shift


def dot(left, right):
    return jnp.dot(left, right, preferred_element_type=jnp.float32)


def dot_t(left, right):
    return lax.dot_general(left, right, (((1,), (1,)), ((), ())), preferred_element_type=jnp.float32)


def t_dot(left, right):
    return lax.dot_general(left, right, (((0,), (0,)), ((), ())), preferred_element_type=jnp.float32)


def column_sums(matrix):
    return jnp.sum(matrix.astype(jnp.float32), axis=0)


def attend_forward(queries, keys, values, bias):
    context, peaks = [], []
    for h in range(GROUP_WIDTH // HEAD):
        cols = slice(h * HEAD, (h + 1) * HEAD)
        scores = dot_t(queries[:, cols], keys[:, cols]) * score_scale + bias
        log_total = jax.nn.logsumexp(scores, axis=-1, keepdims=True)
        probs = jnp.exp(scores - log_total).astype(jnp.bfloat16)
        context.append(dot(probs, values[:, cols]))
        peaks.append(log_total)
    return jnp.concatenate(context, axis=1), peaks


def attend_backward(queries, keys, values, bias, peaks, context, dcontext):
    dq, dk, dv = [], [], []
    for h in range(GROUP_WIDTH // HEAD):
        cols = slice(h * HEAD, (h + 1) * HEAD)
        scores = dot_t(queries[:, cols], keys[:, cols]) * score_scale + bias
        probs = jnp.exp(scores - peaks[h])
        dprobs = dot_t(dcontext[:, cols], values[:, cols])
        delta = jnp.sum(dcontext[:, cols].astype(jnp.float32) * context[:, cols], axis=1, keepdims=True)
        dscores = (probs * (dprobs - delta)).astype(jnp.bfloat16)
        dq.append(dot(dscores, keys[:, cols]) * score_scale)
        dk.append(t_dot(dscores, queries[:, cols]) * score_scale)
        dv.append(t_dot(probs.astype(jnp.bfloat16), dcontext[:, cols]))
    return tuple(jnp.concatenate(part, axis=1) for part in (dq, dk, dv))


def per_device(
    seq_size,
    grp_size,
    tokens,
    valid_len,
    query_weight,
    query_bias,
    key_weight,
    value_weight,
    value_bias,
    output_weight,
    output_bias,
    first_gain,
    first_shift,
    inner_weight,
    inner_bias,
    outer_weight,
    outer_bias,
    second_gain,
    second_shift,
    grad_out,
):
    bf16 = jnp.bfloat16
    rows, width = tokens.shape[1:]
    feed = inner_weight.shape[1]
    shard = query_weight.shape[0]
    HI, ZO, YO = seq_size // 2, seq_size // 4, 2
    extra_bits = [1 << b for b in range(2, log2_of(ZO))]
    part_bits = [1] + extra_bits
    me = lax.axis_index("seq")
    grp = lax.axis_index("grp")
    z1 = me // HI
    z0 = (me // ZO) % 2
    y0 = (me // YO) % 2
    head_group = 2 * z0 + y0
    my_part = me % 2 + 2 * ((me // 4) % max(ZO // 4, 1))
    n_parts = seq_size // 8

    def sflip(value, mask):
        return flip(value, "seq", seq_size, mask)

    packed = jnp.concatenate(
        [
            jnp.concatenate([inner_weight[:, i * width : (i + 1) * width] for i in range(feed // width)], axis=0),
            outer_weight,
            output_weight,
        ],
        axis=0,
    )
    gathered = lax.all_gather(packed, ("grp", "seq"), axis=0, tiled=False)

    x_mine = pick(tokens, z1)
    x_sent = pick(tokens, 1 - z1)
    half_width = width // 2
    x_pair = in_order(x_mine, sflip(x_sent, HI), z1)
    xa, xb = x_pair[:, :, :half_width], x_pair[:, :, half_width:]
    ra, rb = sflip(xa, YO), sflip(xb, ZO)
    xa, xb = in_order(xa, ra, y0), in_order(xb, rb, z0)
    ra, rb = sflip(xa, ZO), sflip(xb, YO)
    xa, xb = in_order(xa, ra, z0), in_order(xb, rb, y0)
    x_all = jnp.concatenate([xa.transpose(2, 0, 1, 3, 4), xb.transpose(2, 1, 0, 3, 4)], axis=-1)
    x_all = x_all.reshape(8 * rows, width)

    smalls = jnp.concatenate(
        [query_bias, value_bias, output_bias, first_gain, first_shift, outer_bias, second_gain, second_shift, inner_bias]
    )
    small_rows = 32 - shard if shard == 24 else 8
    grouped = jnp.stack([query_weight, key_weight, value_weight]).reshape(3, shard, HEAD_GROUPS, GROUP_WIDTH)
    grouped = grouped.transpose(2, 1, 0, 3).reshape(HEAD_GROUPS, shard, 3 * GROUP_WIDTH)
    small_block = jnp.zeros((small_rows * 3 * GROUP_WIDTH,), bf16).at[: smalls.shape[0]].set(smalls)
    small_block = jnp.broadcast_to(small_block.reshape(1, small_rows, -1), (HEAD_GROUPS, small_rows, 3 * GROUP_WIDTH))
    grouped = jnp.concatenate([grouped, small_block], axis=1)

    def group_block(k):
        return lax.dynamic_index_in_dim(grouped, head_group ^ k, 0, keepdims=False)

    w0 = group_block(0)
    w1 = sflip(group_block(1), YO)
    w2 = sflip(group_block(2), ZO)
    w3 = sflip(group_block(3), ZO | YO)
    w_all = in_order(in_order(w0, w1, y0), in_order(w2, w3, y0), z0)
    w_all = in_order(w_all, sflip(w_all, HI), z1)
    names = ["z1", "z0", "y0"]
    for b in extra_bits:
        w_all = in_order(w_all, sflip(w_all, b), (me // b) % 2)
        names = ["e%d" % b] + names
    for b in range(log2_of(grp_size)):
        w_all = in_order(w_all, flip(w_all, "grp", grp_size, 1 << b), (grp >> b) % 2)
        names = ["g%d" % b] + names
    w_all = in_order(w_all, sflip(w_all, 1), me % 2)
    names = ["c"] + names
    wanted = ["g%d" % b for b in reversed(range(log2_of(grp_size)))] + ["z1", "z0"]
    wanted += ["e%d" % b for b in reversed(extra_bits)] + ["y0", "c"]
    n = len(names)
    w_all = w_all.transpose(*[names.index(w) for w in wanted], n, n + 1)
    w_all = w_all.reshape(grp_size * seq_size, shard + small_rows, 3 * GROUP_WIDTH)
    small_all = w_all[:, shard:].reshape(grp_size * seq_size, -1)[:, : smalls.shape[0]]
    vectors = [small_all[:, i * shard : (i + 1) * shard].reshape(-1).astype(jnp.float32) for i in range(8)]
    q_bias, v_bias, o_bias, gain1, shift1, out_bias, gain2, shift2 = vectors
    in_bias = small_all[:, 8 * shard :].reshape(-1).astype(jnp.float32)
    w_all = w_all[:, :shard].reshape(width, 3 * GROUP_WIDTH)

    def own_columns(vector):
        return lax.dynamic_slice_in_dim(vector, head_group * GROUP_WIDTH, GROUP_WIDTH)

    qkv_bias = jnp.concatenate([own_columns(q_bias), jnp.zeros((GROUP_WIDTH,), jnp.float32), own_columns(v_bias)])
    qkv = (dot(x_all, w_all) + qkv_bias).astype(bf16)
    queries = qkv[:, :GROUP_WIDTH]
    kv = qkv[:, GROUP_WIDTH:][None]
    for b in part_bits:
        bit = (me // b) % 2
        theirs = sflip(kv, b)
        kv = jnp.where(bit == 0, jnp.concatenate([kv, theirs]), jnp.concatenate([theirs, kv]))
    kv = kv.reshape(-1, 2 * GROUP_WIDTH)
    keys, values = kv[:, :GROUP_WIDTH], kv[:, GROUP_WIDTH:]

    part = jnp.arange(n_parts, dtype=jnp.int32)
    part_device = part % 2 + 4 * (part // 2)
    member = jnp.arange(8, dtype=jnp.int32)
    member_device = (member // 4) * HI + ((member // 2) % 2) * ZO + (member % 2) * YO
    device = part_device[:, None] + member_device[None, :]
    position = (device[:, :, None] * rows + jnp.arange(rows, dtype=jnp.int32)).reshape(-1)
    bias = jnp.where(position < pick(valid_len, z1), 0.0, masked_score)[None, :]

    context_full, peaks = attend_forward(queries, keys, values, bias)

    teams = [
        [a * HI + b * ZO + c * YO + q for a in range(2) for b in range(2) for c in range(2)]
        for q in [i % 2 + 4 * (i // 2) for i in range(n_parts)]
    ]

    def exchange(blocks):
        return lax.all_to_all(blocks, "seq", 0, 0, axis_index_groups=teams, tiled=True)

    context = exchange(context_full.astype(bf16).reshape(8, rows, GROUP_WIDTH))
    context = context.reshape(2, HEAD_GROUPS, rows, GROUP_WIDTH).transpose(0, 2, 1, 3).reshape(2 * rows, width)

    n_dev = grp_size * seq_size
    inner_rows = shard * (feed // width)
    inner_all = gathered[:, :inner_rows].reshape(n_dev, feed // width, shard, width)
    inner_all = inner_all.transpose(0, 2, 1, 3).reshape(width, feed)
    outer_all = gathered[:, inner_rows : inner_rows + outer_weight.shape[0]].reshape(feed, width)
    output_all = gathered[:, inner_rows + outer_weight.shape[0] :].reshape(width, width)

    home = tokens.reshape(2 * rows, width)
    cotangent = grad_out.reshape(2 * rows, width)
    hidden_one = home.astype(jnp.float32) + dot(context, output_all) + o_bias
    norm_one, norm_back_one = jax.vjp(layer_norm, hidden_one, gain1, shift1)
    first_out = norm_one.astype(bf16)
    inner_pre = dot(first_out, inner_all) + in_bias
    active_full, gelu_back = jax.vjp(partial(jax.nn.gelu, approximate=False), inner_pre)
    active = active_full.astype(bf16)
    hidden_two = first_out.astype(jnp.float32) + dot(active, outer_all) + out_bias
    layer_out, norm_back_two = jax.vjp(layer_norm, hidden_two, gain2, shift2)
    dhidden_two, dsecond_gain, dsecond_shift = norm_back_two(cotangent.astype(jnp.float32))
    douter = dhidden_two.astype(bf16)
    douter_weight = t_dot(active, douter)
    dinner = gelu_back(dot_t(douter, outer_all))[0].astype(bf16)
    dinner_weight = t_dot(first_out, dinner)
    dfirst = dhidden_two + dot_t(dinner, inner_all)
    dhidden_one, dfirst_gain, dfirst_shift = norm_back_one(dfirst)
    dattend = dhidden_one.astype(bf16)
    doutput_weight = t_dot(context, dattend)
    dcontext = dot_t(dattend, output_all).astype(bf16)
    dcontext = dcontext.reshape(2, rows, HEAD_GROUPS, GROUP_WIDTH).transpose(0, 2, 1, 3)
    dcontext = exchange(dcontext.reshape(8, rows, GROUP_WIDTH)).reshape(8 * rows, GROUP_WIDTH)

    out_rows = width // seq_size
    small_grads = [
        column_sums(dattend),
        dfirst_gain,
        dfirst_shift,
        column_sums(douter),
        dsecond_gain,
        dsecond_shift,
    ]
    small_grads = jnp.concatenate(
        [g.reshape(seq_size, out_rows) for g in small_grads] + [column_sums(dinner).reshape(seq_size, -1)], axis=1
    )
    n_small = small_grads.shape[1]
    small_grads = jnp.pad(small_grads, ((0, 0), (0, 8 * width - n_small))).reshape(seq_size, 8, width)
    dinner_blocks = dinner_weight.reshape(seq_size, out_rows, feed // width, width).transpose(0, 2, 1, 3)
    grads = jnp.concatenate(
        [
            dinner_blocks.reshape(seq_size, -1, width).astype(bf16),
            douter_weight.reshape(seq_size, -1, width).astype(bf16),
            doutput_weight.reshape(seq_size, -1, width).astype(bf16),
            small_grads.astype(bf16),
        ],
        axis=1,
    )
    grads = lax.psum_scatter(grads, "seq", scatter_dimension=0, tiled=False)
    for b in range(log2_of(grp_size)):
        grads = (grads.astype(jnp.float32) + flip(grads, "grp", grp_size, 1 << b).astype(jnp.float32)).astype(bf16)
    grads = grads.astype(jnp.float32)
    r1 = out_rows * (feed // width)
    r2 = r1 + feed // seq_size
    r3 = r2 + out_rows
    dinner_weight = grads[:r1].reshape(feed // width, out_rows, width).transpose(1, 0, 2).reshape(out_rows, feed)
    douter_weight = grads[r1:r2]
    doutput_weight = grads[r2:r3]
    small = grads[r3:].reshape(-1)[:n_small]
    doutput_bias, dfirst_gain, dfirst_shift, douter_bias, dsecond_gain, dsecond_shift = (
        small[i * out_rows : (i + 1) * out_rows] for i in range(6)
    )
    dinner_bias = small[6 * out_rows :]

    dqueries, dkeys, dvalues = attend_backward(queries, keys, values, bias, peaks, context_full, dcontext)
    dkv = jnp.concatenate([dkeys, dvalues], axis=1).reshape(n_parts, 8 * rows, 2 * GROUP_WIDTH)
    for b in reversed(part_bits):
        bit = (me // b) % 2
        n_now = dkv.shape[0] // 2
        low, high = dkv[:n_now], dkv[n_now:]
        sent = jnp.where(bit == 0, high, low).astype(bf16)
        dkv = jnp.where(bit == 0, low, high) + sflip(sent, b).astype(jnp.float32)
    dqkv = jnp.concatenate([dqueries.astype(bf16), dkv[0].astype(bf16)], axis=1)

    dx = dot_t(dqkv, w_all).reshape(2, 2, 2, rows, width)
    da, db = dx[..., :half_width], dx[..., half_width:]

    def halve(low, high, bit, mask):
        sent = jnp.where(bit == 0, high, low).astype(bf16)
        return jnp.where(bit == 0, low, high) + sflip(sent, mask).astype(jnp.float32)

    da = halve(da[:, :, 0], da[:, :, 1], y0, YO)
    db = halve(db[:, 0], db[:, 1], z0, ZO)
    da = halve(da[:, 0], da[:, 1], z0, ZO)
    db = halve(db[:, 0], db[:, 1], y0, YO)
    dx = jnp.concatenate([da, db], axis=-1)
    mine = pick(dx, z1)
    theirs = sflip(pick(dx, 1 - z1).astype(bf16), HI).astype(jnp.float32)
    dtokens = dhidden_one.reshape(2, rows, width) + in_order(mine, theirs, z1)

    dw = t_dot(x_all, dqkv)
    dbias = column_sums(dqkv)
    dw = dw.reshape(seq_size, out_rows, 3 * GROUP_WIDTH)
    dw = jnp.concatenate([dw, jnp.broadcast_to(dbias, (seq_size, 8, 3 * GROUP_WIDTH))], axis=1)
    block = dw.shape[1]
    n_extra = 1 << len(extra_bits)
    dw = dw.reshape(2, 2, 2, n_extra, 2, 1, block, 3 * GROUP_WIDTH)[:, :, :, :, :, 0]
    dw = dw.reshape(2, 2, n_extra, 2, 2, block, 3 * GROUP_WIDTH)
    dw = halve(dw[:, :, :, :, 0], dw[:, :, :, :, 1], me % 2, 1)
    for b in reversed(extra_bits):
        m = dw.shape[2] // 2
        dw = halve(dw[:, :, :m], dw[:, :, m:], (me // b) % 2, b)
    dw = dw[:, :, 0]
    dw = halve(dw[0], dw[1], z1, HI)
    for b in range(log2_of(grp_size)):
        dw = dw + flip(dw.astype(bf16), "grp", grp_size, 1 << b).astype(jnp.float32)
    dw = dw.astype(bf16).reshape(HEAD_GROUPS, block, 3 * GROUP_WIDTH)

    def row_block(k):
        return lax.dynamic_index_in_dim(dw, head_group ^ k, 0, keepdims=False)

    w0 = row_block(0)
    w1 = sflip(row_block(1), YO)
    w2 = sflip(row_block(2), ZO)
    w3 = sflip(row_block(3), ZO | YO)
    dw = in_order(in_order(w0, w1, y0), in_order(w2, w3, y0), z0).reshape(HEAD_GROUPS, block, 3, GROUP_WIDTH)
    dw = dw.astype(jnp.float32).transpose(2, 1, 0, 3).reshape(3, block, width)
    dquery_weight, dkey_weight, dvalue_weight = dw[0, :out_rows], dw[1, :out_rows], dw[2, :out_rows]
    dquery_bias = lax.dynamic_slice_in_dim(dw[0, out_rows], me * out_rows, out_rows)
    dvalue_bias = lax.dynamic_slice_in_dim(dw[2, out_rows], me * out_rows, out_rows)

    return (
        layer_out.astype(bf16).reshape(2, rows, width),
        dtokens.astype(bf16),
        dquery_weight,
        dquery_bias,
        dkey_weight,
        dvalue_weight,
        dvalue_bias,
        doutput_weight,
        doutput_bias,
        dfirst_gain,
        dfirst_shift,
        dinner_weight,
        dinner_bias,
        douter_weight,
        douter_bias,
        dsecond_gain,
        dsecond_shift,
    )


def solution(mesh):
    in_specs = (
        P("grp", "seq", None),
        P("grp"),
        P(("grp", "seq"), None),
        P(("grp", "seq")),
        P(("grp", "seq"), None),
        P(("grp", "seq"), None),
        P(("grp", "seq")),
        P(("grp", "seq"), None),
        P(("grp", "seq")),
        P(("grp", "seq")),
        P(("grp", "seq")),
        P(("grp", "seq"), None),
        P(("grp", "seq")),
        P(("grp", "seq"), None),
        P(("grp", "seq")),
        P(("grp", "seq")),
        P(("grp", "seq")),
        P("grp", "seq", None),
    )
    out_specs = (
        P("grp", "seq", None),
        P("grp", "seq", None),
        P("seq", None),
        P("seq"),
        P("seq", None),
        P("seq", None),
        P("seq"),
        P("seq", None),
        P("seq"),
        P("seq"),
        P("seq"),
        P("seq", None),
        P("seq"),
        P("seq", None),
        P("seq"),
        P("seq"),
        P("seq"),
    )
    body = partial(per_device, mesh.shape["seq"], mesh.shape["grp"])
    return jax.shard_map(
        body, mesh=mesh, in_specs=in_specs, out_specs=out_specs, check_vma=False
    )
```

time: 1580 us -> 534 us (0.34)
  waiting for transfers between devices: 801 us -> 118 us
  local copies, waits for them, and re-layouts: 329 us -> 99 us
  blocking collectives: 103 us -> 0 us
  matrix products: 197 us -> 156 us
  starting transfers between devices: 1.64 us -> 41.7 us
  loops' own time: 25.2 us -> 0 us
    unnamed x28 -> x2, waiting for transfers between devices: 306 us -> 0.03 us
    all_gather x10 -> x1, waiting for transfers between devices: 279 us -> 0.02 us  [per_device(): gathered = lax.all_gather(packed, ('grp', 'seq'), axis=0, tiled=False)]
    reduce_scatter x3 -> x1, waiting for transfers between devices: 216 us -> 0.01 us  [per_device(): grads = lax.psum_scatter(grads, 'seq', scatter_dimension=0, tiled=False)]
    unnamed x240 -> x99, local copies, waits for them, and re-layouts: 159 us -> 9.58 us
    ppermute x0 -> x25, waiting for transfers between devices: none -> 108 us  [flip(): return lax.ppermute(value, axis, [(i, i ^ mask) for i in range(size)])]
    unnamed x2 -> x0, blocking collectives: 97.6 us -> none
    while x4 -> x0, local copies, waits for them, and re-layouts: 54.4 us -> none  [attend_forward(): context = lax.scan(value_step, empty, (key_blocks, value_blocks, starts))[0]]
    reshape x4 -> x17, local copies, waits for them, and re-layouts: 60.7 us -> 19.1 us  [the longest x6 7.44 us: per_device(): g.reshape(seq_size, out_rows)]
  transfers between devices with their start and end apart: 21 -> 29, of which waited for: 17 -> 14; matrix products, arithmetic and copies ran while one was open for 29% -> 52% of each run, Pallas kernels for 0% -> 0%
where the time goes in v1:
time: 534 us; the launch traced here: 526 us
  matrix products  156 us (29%)
  waiting for transfers between devices  118 us (22%)
  local copies, waits for them, and re-layouts  99 us (19%)
  other arithmetic  94.1 us (18%)
  starting transfers between devices  41.7 us (8%)
  between operations  16.9 us (3%)
    ppermute x25, waiting for transfers between devices, flip(): return lax.ppermute(value, axis, [(i, i ^ mask) for i in range(size)])  108 us
    dot_general x10, matrix products, dot_t(): lax.dot_general(left, right, (((1,), (1,)), ((), ())), preferred_element_...  72.6 us
    dot_general x10, matrix products, dot(): return jnp.dot(left, right, preferred_element_type=jnp.float32)  48.8 us
    dot_general x10, matrix products, t_dot(): lax.dot_general(left, right, (((0,), (0,)), ((), ())), preferred_element_...  34.9 us
    ppermute x25, starting transfers between devices, flip(): return lax.ppermute(value, axis, [(i, i ^ mask) for i in range(size)])  29 us
    reduce_sum x3, other arithmetic, attend_forward(): log_total = jax.nn.logsumexp(scores, axis=-1, keepdims=True)  27.1 us
    convert_element_type x3, other arithmetic, attend_forward(): probs = jnp.exp(scores - log_total).astype(jnp.bfloat16)  25.7 us
    convert_element_type x2, local copies, waits for them, and re-layouts, per_device(): dinner_blocks.reshape(seq_size, -1, width).astype(bf16)  13.1 us
  transfers between devices with their start and end apart: 29, of which 14 were waited for; matrix products, arithmetic and copies ran while one was open for 52% of the time, Pallas kernels for 0%

profile of v1, /device:TPU:0, one launch (start us, length us, event | category | flops | bytes accessed | tf_op | source)
XLA Modules:
  0.0 526.2 jit_solution(3562586312467293936)
XLA Ops:
  7.3 6.2 %concatenate.268 = bf16[288]{0:T(512)(128)(2,1)S(1)} concatenate(bf16[24]{0:T(256)(128)(2,1)} %param.23, bf16[24]{0:T(256)(128)(2,1)} %param.26, bf16[24]{0:T(256)(128)(2,1)} %param.28, bf16[24]{0:T(256)(128)(2,1)} %param.29, bf16[24]{0:T(256)(128)(2,1)} %param.30, bf16[24]{0:T(256)(128)(2,1)} %param.34, bf16[24]{0:T(256)(128)(2,1)} %param.35, bf16[24]{0:T(256)(128)(2,1)} %param.36, ...), dimensions={0} | concatenate | bytes 1152 | tf_op jit(solution)/shard_map/concatenate | solution.py:146
  17.2 4.1 collective-permute-start.7
  25.9 3.0 collective-permute-start
  29.2 26.3 %collective-permute-done.8 = bf16[2,2,32,576]{3,2,1,0:T(8,128)(2,1)S(1)} collective-permute-done((bf16[2,2,32,576]{3,2,1,0:T(8,128)(2,1)S(1)}, bf16[2,2,32,576]{3,2,1,0:T(8,128)(2,1)S(1)}, u32[]{:S(2)}, u32[]{:S(2)}) %collective-permute-start.8) | collective-permute-done | bytes 147488 | tf_op jit(solution)/shard_map/ppermute | solution.py:23
  59.9 11.3 %collective-permute-done.9 = bf16[2,2,2,32,576]{4,3,2,1,0:T(8,128)(2,1)S(1)} collective-permute-done((bf16[2,2,2,32,576]{4,3,2,1,0:T(8,128)(2,1)S(1)}, bf16[2,2,2,32,576]{4,3,2,1,0:T(8,128)(2,1)S(1)}, u32[]{:S(2)}, u32[]{:S(2)}) %collective-permute-start.9) | collective-permute-done | bytes 294944 | tf_op jit(solution)/shard_map/ppermute | solution.py:23
  79.2 11.2 %collective-permute-done.4 = bf16[2,2,192,384]{3,2,1,0:T(8,128)(2,1)S(1)} collective-permute-done((bf16[2,2,192,384]{3,2,1,0:T(8,128)(2,1)}, bf16[2,2,192,384]{3,2,1,0:T(8,128)(2,1)S(1)}, u32[]{:S(2)}, u32[]{:S(2)}) %collective-permute-start.4) | collective-permute-done | bytes 589856 | tf_op jit(solution)/shard_map/ppermute | solution.py:23
  102.7 3.5 copy.149
  106.2 9.2 %fusion.121 = (f32[1536]{0:T(1024)S(1)}, f32[1536,3072]{1,0:T(8,128)}) fusion(f32[3072]{0:T(1024)S(1)} %select_n.615, bf16[3072,384]{1,0:T(8,128)(2,1)S(1)} %bitcast.293, bf16[1536,576]{0,1:T(8,128)(2,1)} %copy-done.9), kind=kOutput, calls=%fused_computation.301 | convolution fusion | flops 618134016 | bytes 19875840 | tf_op jit(solution)/shard_map/dot_general | solution.py:45
  115.4 9.1 %exponential_reduce_fusion = f32[1536]{0:T(1024)S(1)} fusion(f32[1536,3072]{1,0:T(8,128)} %get-tuple-element.94, f32[1536]{0:T(1024)S(1)} %is-finite_select_fusion), kind=kLoop, calls=%fused_computation.4 | loop fusion | flops 9435648 | bytes 18886656 | tf_op jit(solution)/shard_map/reduce_sum | solution.py:61
  125.2 8.6 %fusion.2 = bf16[1536,3072]{1,0:T(8,128)(2,1)S(1)} fusion(f32[1536,3072]{1,0:T(8,128)} %get-tuple-element.94, f32[1536]{0:T(1024)S(1)} %log_add_fusion), kind=kLoop, calls=%fused_computation.14 | loop fusion | flops 9437184 | bytes 28317696 | tf_op jit(solution)/shard_map/convert_element_type | solution.py:62
  133.8 3.8 fusion.122
  138.6 9.0 %fusion.123 = (f32[1536]{0:T(1024)S(1)}, f32[1536,3072]{1,0:T(8,128)}) fusion(f32[3072]{0:T(1024)S(1)} %select_n.615, bf16[3072,384]{1,0:T(8,128)(2,1)S(1)} %bitcast.295, bf16[1536,576]{0,1:T(8,128)(2,1)} %copy-done.9), kind=kOutput, calls=%fused_computation.303 | convolution fusion | flops 618134016 | bytes 19875840 | tf_op jit(solution)/shard_map/dot_general | solution.py:45
  147.7 9.0 %exponential_reduce_fusion.1 = f32[1536]{0:T(1024)S(1)} fusion(f32[1536,3072]{1,0:T(8,128)} %get-tuple-element.98, f32[1536]{0:T(1024)S(1)} %is-finite_select_fusion.1), kind=kLoop, calls=%fused_computation.7 | loop fusion | flops 9435648 | bytes 18886656 | tf_op jit(solution)/shard_map/reduce_sum | solution.py:61
  156.7 8.6 %fusion.1 = bf16[1536,3072]{1,0:T(8,128)(2,1)S(1)} fusion(f32[1536,3072]{1,0:T(8,128)} %get-tuple-element.98, f32[1536]{0:T(1024)S(1)} %log_add_fusion.1), kind=kLoop, calls=%fused_computation.13 | loop fusion | flops 9437184 | bytes 28317696 | tf_op jit(solution)/shard_map/convert_element_type | solution.py:62
  165.3 3.9 fusion.124
  170.2 8.8 %fusion.125 = (f32[1536]{0:T(1024)S(1)}, f32[1536,3072]{1,0:T(8,128)}) fusion(f32[3072]{0:T(1024)S(1)} %select_n.615, bf16[3072,384]{1,0:T(8,128)(2,1)S(1)} %bitcast.297, bf16[1536,576]{0,1:T(8,128)(2,1)} %copy-done.9), kind=kOutput, calls=%fused_computation.305 | convolution fusion | flops 618134016 | bytes 19875840 | tf_op jit(solution)/shard_map/dot_general | solution.py:45
  179.0 9.0 %exponential_reduce_fusion.2 = f32[1536]{0:T(1024)S(1)} fusion(f32[1536,3072]{1,0:T(8,128)} %get-tuple-element.102, f32[1536]{0:T(1024)S(1)} %is-finite_select_fusion.2), kind=kLoop, calls=%fused_computation.10 | loop fusion | flops 9435648 | bytes 18886656 | tf_op jit(solution)/shard_map/reduce_sum | solution.py:61
  188.0 8.5 %fusion = bf16[1536,3072]{1,0:T(8,128)(2,1)S(1)} fusion(f32[1536,3072]{1,0:T(8,128)} %get-tuple-element.102, f32[1536]{0:T(1024)S(1)} %log_add_fusion.2), kind=kLoop, calls=%fused_computation.12 | loop fusion | flops 9437184 | bytes 28317696 | tf_op jit(solution)/shard_map/convert_element_type | solution.py:62
  196.5 3.8 fusion.126
  202.6 8.5 %all-to-all-start = ((bf16[8,192,192]{1,2,0:T(8,128)(2,1)}), bf16[8,192,192]{1,2,0:T(8,128)(2,1)}, u32[]{:S(2)}, u32[]{:S(2)}) async-start(bf16[8,192,192]{1,2,0:T(8,128)(2,1)} %pad_maximum_fusion.4), calls=%async_computation | async-start | bytes 1572864 | tf_op jit(solution)/shard_map/all_to_all | solution.py:215
  217.4 4.3 copy.172
  221.8 10.0 %all-to-all-done = bf16[8,192,192]{1,2,0:T(8,128)(2,1)} async-done(((bf16[8,192,192]{1,2,0:T(8,128)(2,1)}), bf16[8,192,192]{1,2,0:T(8,128)(2,1)}, u32[]{:S(2)}, u32[]{:S(2)}) %all-to-all-start) | async-done | bytes 589856 | tf_op jit(solution)/shard_map/all_to_all | solution.py:215
  237.0 6.7 %fusion.115 = (bf16[32,96,768]{2,1,0:T(8,128)(2,1)}, bf16[32,96,768]{2,1,0:T(8,128)(2,1)S(1)}) fusion(bf16[32,216,768]{2,1,0:T(8,128)(2,1)} %bitcast.317), kind=kLoop, calls=%fused_computation.295 | loop fusion | bytes 18874368 | tf_op jit(solution)/shard_map/slice | solution.py:224
  249.7 14.1 %multiply_convert_fusion.3 = (bf16[384,3072]{1,0:T(8,128)(2,1)S(1)}, f32[384,3072]{1,0:T(8,128)S(1)}, f32[384,3072]{1,0:T(8,128)}) fusion(f32[3072]{0:T(1024)S(1)} %copy-done.31, bf16[768,3072]{1,0:T(8,128)(2,1)S(1)} %bitcast.323, f32[384,768]{1,0:T(8,128)S(1)} %get-tuple-element.106, f32[768]{0:T(1024)S(1)} %copy-done.32, f32[768]{0:T(1024)S(1)} %copy-done.30, ...), kind=kOutput, calls=%fused_computation.21 | convolution fusion | flops 1891270656 | bytes 17716224 | tf_op jit(solution)/shard_map/dot_general | solution.py:41
  269.5 4.3 convolution_convert_fusion
  273.8 5.7 %fusion.110 = (bf16[3072]{0:T(1024)(128)(2,1)}, bf16[384,3072]{1,0:T(8,128)(2,1)S(1)}) fusion(f32[384,3072]{1,0:T(8,128)S(1)} %get-tuple-element.48, f32[384,3072]{1,0:T(8,128)} %get-tuple-element.107, bf16[384,768]{1,0:T(8,128)(2,1)S(1)} %get-tuple-element.40, bf16[3072,768]{1,0:T(8,128)(2,1)S(1)} %bitcast.333), kind=kOutput, calls=%fused_computation.291 | convolution fusion | flops 1829630976 | bytes 17111040 | tf_op jit(solution)/shard_map/dot_general | solution.py:45
  282.4 4.7 convolution_convert_fusion.1
  289.8 2.9 reshape.1365
  295.1 4.2 all-to-all-start.1
  313.2 9.7 %convert_element_type.386 = bf16[16,48,4,768]{3,2,1,0:T(4,128)(2,1)} reshape(bf16[768,3072]{1,0:T(8,128)(2,1)} %convolution_convert_fusion.1) | data formatting | bytes 9437184 | tf_op jit(solution)/shard_map/convert_element_type | solution.py:267
  323.0 3.4 copy.182
  327.1 11.1 %pad_maximum_fusion = bf16[16,440,768]{2,1,0:T(8,128)(2,1)} fusion(bf16[16,8,768]{2,1,0:T(8,128)(2,1)S(1)} %bitcast.353, bf16[16,48,768]{2,1,0:T(8,128)(2,1)S(1)} %copy-done.8, bf16[16,192,768]{2,1,0:T(8,128)(2,1)S(1)} %bitcast.329, bf16[16,192,768]{2,1,0:T(8,128)(2,1)S(1)} %bitcast.309), kind=kLoop, calls=%fused_computation.15 | loop fusion | flops 43253760 | bytes 21626880 | tf_op jit(solution)/shard_map/concatenate | solution.py:265
  345.3 12.1 %multiply_convert_fusion.2 = bf16[1536,3072]{1,0:T(8,128)(2,1)S(1)} fusion(f32[1536,3072]{1,0:T(8,128)} %get-tuple-element.102, f32[1536]{0:T(1024)S(1)} %get-tuple-element.35, f32[1536]{0:T(1024)S(1)} %log_add_fusion.2, bf16[3072,384]{1,0:T(8,128)(2,1)S(1)} %bitcast.299, bf16[1536,192]{0,1:T(8,128)(2,1)} %reshape.1367), kind=kOutput, calls=%fused_computation.2 | convolution fusion | flops 622854144 | bytes 29310976 | tf_op jit(solution)/shard_map/dot_general | solution.py:45
  357.4 3.2 fusion.11
  361.5 9.4 %multiply_convert_fusion.1 = bf16[1536,3072]{1,0:T(8,128)(2,1)S(1)} fusion(f32[1536,3072]{1,0:T(8,128)} %get-tuple-element.98, f32[1536]{0:T(1024)S(1)} %get-tuple-element.36, f32[1536]{0:T(1024)S(1)} %log_add_fusion.1, bf16[3072,384]{1,0:T(8,128)(2,1)S(1)} %bitcast.300, bf16[1536,192]{0,1:T(8,128)(2,1)S(1)} %copy-done.5), kind=kOutput, calls=%fused_computation.1 | convolution fusion | flops 622854144 | bytes 29310976 | tf_op jit(solution)/shard_map/dot_general | solution.py:45
  371.0 3.4 fusion.10
  374.8 9.3 %multiply_convert_fusion = bf16[1536,3072]{1,0:T(8,128)(2,1)S(1)} fusion(f32[1536,3072]{1,0:T(8,128)} %get-tuple-element.94, f32[1536]{0:T(1024)S(1)} %get-tuple-element.34, f32[1536]{0:T(1024)S(1)} %copy-done.25, bf16[3072,384]{1,0:T(8,128)(2,1)S(1)} %bitcast.301, bf16[1536,192]{0,1:T(8,128)(2,1)S(1)} %copy-done.5), kind=kOutput, calls=%fused_computation | convolution fusion | flops 622854144 | bytes 29310976 | tf_op jit(solution)/shard_map/dot_general | solution.py:45
  386.8 6.6 %convolution_dynamic-update-slice_fusion.2 = f32[3072,384]{0,1:T(8,128)} fusion(f32[3072,384]{0,1:T(8,128)} %fusion.9, bf16[1536,3072]{1,0:T(8,128)(2,1)} %copy-done.4, bf16[1536,192]{0,1:T(8,128)(2,1)S(1)} %copy-done.5), kind=kOutput, calls=%fused_computation.38 | convolution fusion | flops 603979776 | bytes 10420224 | tf_op jit(solution)/shard_map/dot_general | solution.py:49
  398.8 3.7 fusion.33
  402.5 3.7 fusion.15
  408.0 7.6 %fusion.14 = bf16[1536,64]{0,1:T(8,128)(2,1)} fusion(bf16[1536,3072]{1,0:T(8,128)(2,1)} %copy-done.1, bf16[3072,384]{1,0:T(8,128)(2,1)S(1)} %bitcast.303), kind=kOutput, calls=%fused_computation.56 | convolution fusion | flops 604176384 | bytes 10420224 | tf_op jit(solution)/shard_map/dot_general | solution.py:41
  417.4 7.5 %fusion.13 = bf16[1536,64]{0,1:T(8,128)(2,1)} fusion(bf16[1536,3072]{1,0:T(8,128)(2,1)} %copy-done, bf16[3072,384]{1,0:T(8,128)(2,1)S(1)} %bitcast.304), kind=kOutput, calls=%fused_computation.55 | convolution fusion | flops 604176384 | bytes 10420224 | tf_op jit(solution)/shard_map/dot_general | solution.py:41
  426.7 3.5 fusion.12
  431.7 4.5 fusion.16
  445.7 29.7 %collective-permute-done.15 = bf16[2,2,192,384]{3,2,1,0:T(8,128)(2,1)S(1)} collective-permute-done((bf16[2,2,192,384]{3,2,1,0:T(8,128)(2,1)S(1)}, bf16[2,2,192,384]{3,2,1,0:T(8,128)(2,1)S(1)}, u32[]{:S(2)}, u32[]{:S(2)}) %collective-permute-start.15) | collective-permute-done | bytes 589856 | tf_op jit(solution)/shard_map/ppermute | solution.py:23
  479.2 5.5 %collective-permute-done.16 = bf16[2,192,384]{2,1,0:T(8,128)(2,1)S(1)} collective-permute-done((bf16[2,192,384]{2,1,0:T(8,128)(2,1)S(1)}, bf16[2,192,384]{2,1,0:T(8,128)(2,1)S(1)}, u32[]{:S(2)}, u32[]{:S(2)}) %collective-permute-start.16) | collective-permute-done | bytes 294944 | tf_op jit(solution)/shard_map/ppermute | solution.py:23
  492.2 4.4 collective-permute-done.23
  504.3 11.1 %collective-permute-done.24 = bf16[440,768]{1,0:T(8,128)(2,1)S(1)} collective-permute-done((bf16[440,768]{1,0:T(8,128)(2,1)}, bf16[440,768]{1,0:T(8,128)(2,1)S(1)}, u32[]{:S(2)}, u32[]{:S(2)}) %collective-permute-start.24) | collective-permute-done | bytes 675872 | tf_op jit(solution)/shard_map/ppermute | solution.py:23
  (314 shorter events, 137.9 us)
Async XLA Ops:
  7.2 17.8 %copy-start.26 = (bf16[96,768]{1,0:T(8,128)(2,1)S(1)}, bf16[96,768]{1,0:T(8,128)(2,1)}, u32[]{:S(2)}) copy-start(bf16[96,768]{1,0:T(8,128)(2,1)} %param.33) | copy-start | bytes 442372
  7.2 17.8 %copy-start.28 = (bf16[24,768]{1,0:T(8,128)(2,1)S(1)}, bf16[24,768]{1,0:T(8,128)(2,1)}, u32[]{:S(2)}) copy-start(bf16[24,768]{1,0:T(8,128)(2,1)} %param.27) | copy-start | bytes 110596
  7.2 18.6 %copy-start.19 = (bf16[2,192,768]{2,1,0:T(8,128)(2,1)S(1)}, bf16[2,192,768]{2,1,0:T(8,128)(2,1)}, u32[]{:S(2)}) copy-start(bf16[2,192,768]{2,1,0:T(8,128)(2,1)} %param.20) | copy-start | bytes 1769476
  7.2 229.7 %all-gather.3.cloned.1.call-start = ((), (), s32[]{:S(2)}) async-start(), calls=%async_computation.4 | async-start | bytes 10948608 | tf_op jit(solution)/shard_map/all_gather | solution.py:132
  17.2 11.6 %collective-permute-start.7 = (bf16[32,576]{1,0:T(8,128)(2,1)S(1)}, bf16[32,576]{1,0:T(8,128)(2,1)S(1)}, u32[]{:S(2)}, u32[]{:S(2)}) collective-permute-start(bf16[32,576]{1,0:T(8,128)(2,1)S(1)} %get-tuple-element.84), channel_id=1, source_target_pairs={{0,6},{1,7},{2,4},{3,5},{4,2},{5,3},{6,0},{7,1},{8,14},{9,15},{10,... | collective-permute-start | bytes 110600 | tf_op jit(solution)/shard_map/ppermute | solution.py:23
  21.3 7.6 %collective-permute-start.6 = (bf16[32,576]{1,0:T(8,128)(2,1)S(1)}, bf16[32,576]{1,0:T(8,128)(2,1)S(1)}, u32[]{:S(2)}, u32[]{:S(2)}) collective-permute-start(bf16[32,576]{1,0:T(8,128)(2,1)S(1)} %get-tuple-element.83), channel_id=1, source_target_pairs={{0,4},{1,5},{2,6},{3,7},{4,0},{5,1},{6,2},{7,3},{8,12},{9,13},{10,... | collective-permute-start | bytes 110600 | tf_op jit(solution)/shard_map/ppermute | solution.py:23
  21.7 7.2 %collective-permute-start.5 = (bf16[32,576]{1,0:T(8,128)(2,1)S(1)}, bf16[32,576]{1,0:T(8,128)(2,1)S(1)}, u32[]{:S(2)}, u32[]{:S(2)}) collective-permute-start(bf16[32,576]{1,0:T(8,128)(2,1)S(1)} %get-tuple-element.82), channel_id=1, source_target_pairs={{0,2},{1,3},{2,0},{3,1},{4,6},{5,7},{6,4},{7,5},{8,10},{9,11},{10,... | collective-permute-start | bytes 110600 | tf_op jit(solution)/shard_map/ppermute | solution.py:23
  25.9 31.4 %collective-permute-start = (bf16[192,768]{1,0:T(8,128)(2,1)S(1)}, bf16[192,768]{1,0:T(8,128)(2,1)S(1)}, u32[]{:S(2)}, u32[]{:S(2)}) collective-permute-start(bf16[192,768]{1,0:T(8,128)(2,1)S(1)} %get-tuple-element.63), channel_id=1, source_target_pairs={{0,8},{1,9},{2,10},{3,11},{4,12},{5,13},{6,14},{7,15},{8,0},{9,1},... | collective-permute-start | bytes 884744 | tf_op jit(solution)/shard_map/ppermute | solution.py:23
  29.0 26.5 %collective-permute-start.8 = (bf16[2,2,32,576]{3,2,1,0:T(8,128)(2,1)S(1)}, bf16[2,2,32,576]{3,2,1,0:T(8,128)(2,1)S(1)}, u32[]{:S(2)}, u32[]{:S(2)}) collective-permute-start(bf16[2,2,32,576]{3,2,1,0:T(8,128)(2,1)S(1)} %maximum_select_fusion.15), channel_id=1, source_target_pairs={{0,8},{1,9},{2,10},{3,11},{4,12},{5,13},{6,14},{7,15},{8,0},{9,1},... | collective-permute-start | bytes 442376 | tf_op jit(solution)/shard_map/ppermute | solution.py:23
  55.6 15.7 %collective-permute-start.9 = (bf16[2,2,2,32,576]{4,3,2,1,0:T(8,128)(2,1)S(1)}, bf16[2,2,2,32,576]{4,3,2,1,0:T(8,128)(2,1)S(1)}, u32[]{:S(2)}, u32[]{:S(2)}) collective-permute-start(bf16[2,2,2,32,576]{4,3,2,1,0:T(8,128)(2,1)S(1)} %maximum_select_fusion.12), channel_id=1, source_target_pairs={{0,16},{16,0},{1,17},{17,1},{2,18},{18,2},{3,19},{19,3},{4,20},{20... | collective-permute-start | bytes 884744 | tf_op jit(solution)/shard_map/ppermute | solution.py:23
  57.6 16.6 %collective-permute-start.3 = (bf16[2,192,384]{2,1,0:T(8,128)(2,1)S(1)}, bf16[2,192,384]{2,1,0:T(8,128)(2,1)S(1)}, u32[]{:S(2)}, u32[]{:S(2)}) collective-permute-start(bf16[2,192,384]{2,1,0:T(8,128)(2,1)S(1)} %get-tuple-element.60), channel_id=1, source_target_pairs={{0,4},{1,5},{2,6},{3,7},{4,0},{5,1},{6,2},{7,3},{8,12},{9,13},{10,... | collective-permute-start | bytes 884744 | tf_op jit(solution)/shard_map/ppermute | solution.py:23
  58.4 18.2 %collective-permute-start.1 = (bf16[2,192,384]{2,1,0:T(8,128)(2,1)S(1)}, bf16[2,192,384]{2,1,0:T(8,128)(2,1)S(1)}, u32[]{:S(2)}, u32[]{:S(2)}) collective-permute-start(bf16[2,192,384]{2,1,0:T(8,128)(2,1)S(1)} %get-tuple-element.61), channel_id=1, source_target_pairs={{0,2},{1,3},{2,0},{3,1},{4,6},{5,7},{6,4},{7,5},{8,10},{9,11},{10,... | collective-permute-start | bytes 884744 | tf_op jit(solution)/shard_map/ppermute | solution.py:23
  71.5 6.3 %collective-permute-start.10 = (bf16[2,2,2,2,32,576]{5,4,3,2,1,0:T(8,128)(2,1)S(1)}, bf16[2,2,2,2,32,576]{5,4,3,2,1,0:T(8,128)(2,1)S(1)}, u32[]{:S(2)}, u32[]{:S(2)}) collective-permute-start(bf16[2,2,2,2,32,576]{5,4,3,2,1,0:T(8,128)(2,1)S(1)} %maximum_select_fusion.6), channel_id=1, source_target_pairs={{0,1},{1,0},{2,3},{3,2},{4,5},{5,4},{6,7},{7,6},{8,9},{9,8},{10,11... | collective-permute-start | bytes 1769480 | tf_op jit(solution)/shard_map/ppermute | solution.py:23
  75.1 15.2 %collective-permute-start.4 = (bf16[2,2,192,384]{3,2,1,0:T(8,128)(2,1)}, bf16[2,2,192,384]{3,2,1,0:T(8,128)(2,1)S(1)}, u32[]{:S(2)}, u32[]{:S(2)}) collective-permute-start(bf16[2,2,192,384]{3,2,1,0:T(8,128)(2,1)} %maximum_select_fusion.10), channel_id=1, source_target_pairs={{0,2},{1,3},{2,0},{3,1},{4,6},{5,7},{6,4},{7,5},{8,10},{9,11},{10,... | collective-permute-start | bytes 1769480 | tf_op jit(solution)/shard_map/ppermute | solution.py:23
  77.5 15.7 %collective-permute-start.2 = (bf16[2,2,192,384]{3,2,1,0:T(8,128)(2,1)}, bf16[2,2,192,384]{3,2,1,0:T(8,128)(2,1)}, u32[]{:S(2)}, u32[]{:S(2)}) collective-permute-start(bf16[2,2,192,384]{3,2,1,0:T(8,128)(2,1)} %maximum_select_fusion.8), channel_id=1, source_target_pairs={{0,4},{1,5},{2,6},{3,7},{4,0},{5,1},{6,2},{7,3},{8,12},{9,13},{10,... | collective-permute-start | bytes 1769480 | tf_op jit(solution)/shard_map/ppermute | solution.py:23
  78.4 16.7 %copy-start.16 = (bf16[32,24,576]{2,1,0:T(8,128)(2,1)}, bf16[32,24,576]{2,1,0:T(8,128)(2,1)S(1)}, u32[]{:S(2)}) copy-start(bf16[32,24,576]{2,1,0:T(8,128)(2,1)S(1)} %slice.354) | copy-start | bytes 2654212
  78.6 16.0 %copy-start.21 = (bf16[32,4608]{1,0:T(8,128)(2,1)}, bf16[32,4608]{1,0:T(8,128)(2,1)S(1)}, u32[]{:S(2)}) copy-start(bf16[32,4608]{1,0:T(8,128)(2,1)S(1)} %reshape.1356) | copy-start | bytes 884740
  97.9 3.0 collective-permute-start.11
  200.3 10.8 %copy-start.7 = (bf16[2,192,768]{2,1,0:T(8,128)(2,1)S(1)}, bf16[2,192,768]{2,1,0:T(8,128)(2,1)}, u32[]{:S(2)}) copy-start(bf16[2,192,768]{2,1,0:T(8,128)(2,1)} %param.37) | copy-start | bytes 1769476
  202.6 29.1 %all-to-all-start = ((bf16[8,192,192]{1,2,0:T(8,128)(2,1)}), bf16[8,192,192]{1,2,0:T(8,128)(2,1)}, u32[]{:S(2)}, u32[]{:S(2)}) async-start(bf16[8,192,192]{1,2,0:T(8,128)(2,1)} %pad_maximum_fusion.4), calls=%async_computation | async-start | bytes 1572864 | tf_op jit(solution)/shard_map/all_to_all | solution.py:215
  236.9 11.5 %copy-start.15 = (bf16[384,768]{0,1:T(8,128)(2,1)}, bf16[384,768]{0,1:T(8,128)(2,1)S(1)}, u32[]{:S(2)}) copy-start(bf16[384,768]{0,1:T(8,128)(2,1)S(1)} %reshape.1358) | copy-start | bytes 1769476
  248.5 15.2 %slice-start.8 = ((s8[4718592]{0:T(1024)(128)(4,1)}), s8[4194304]{0:T(1024)(128)(4,1)S(1)}, s32[]{:S(2)}) async-start(s8[4718592]{0:T(1024)(128)(4,1)} %bitcast.330), calls=%async_computation.13 | async-start | bytes 8388608
  249.6 14.1 %slice-start.9 = ((s8[4718592]{0:T(1024)(128)(4,1)}), s8[524288]{0:T(1024)(128)(4,1)S(1)}, s32[]{:S(2)}) async-start(s8[4718592]{0:T(1024)(128)(4,1)} %bitcast.330), calls=%async_computation.14 | async-start | bytes 1048576
  249.7 14.1 %copy-start.33 = (f32[768]{0:T(1024)S(1)}, f32[768]{0:T(1024)}, u32[]{:S(2)}) copy-start(f32[768]{0:T(1024)} %reshape.1388) | copy-start | bytes 9220
  295.1 43.1 %all-to-all-start.1 = ((bf16[8,192,192]{1,2,0:T(8,128)(2,1)}), bf16[8,192,192]{1,2,0:T(8,128)(2,1)}, u32[]{:S(2)}, u32[]{:S(2)}) async-start(bf16[8,192,192]{1,2,0:T(8,128)(2,1)} %bitcast.335), calls=%async_computation.1 | async-start | bytes 1572864 | tf_op jit(solution)/shard_map/all_to_all | solution.py:215
  299.3 200.3 %reduce-scatter.2.cloned.1.call-start = ((), (), s32[]{:S(2)}) async-start(), calls=%async_computation.3 | async-start | bytes 11489280 | tf_op jit(solution)/shard_map/reduce_scatter | solution.py:274
  345.3 12.1 %copy-start.10 = (bf16[1536,576]{0,1:T(8,128)(2,1)S(1)}, bf16[1536,576]{0,1:T(8,128)(2,1)}, u32[]{:S(2)}) copy-start(bf16[1536,576]{0,1:T(8,128)(2,1)} %copy-done.9) | copy-start | bytes 5308420
  384.1 9.3 %slice-start.3 = ((s8[9437184]{0:T(1024)(128)(4,1)}), s8[4194304]{0:T(1024)(128)(4,1)S(1)}, s32[]{:S(2)}) async-start(s8[9437184]{0:T(1024)(128)(4,1)} %bitcast.291), calls=%async_computation.8 | async-start | bytes 8388608
  384.1 9.3 %slice-start.4 = ((s8[9437184]{0:T(1024)(128)(4,1)}), s8[4194304]{0:T(1024)(128)(4,1)S(1)}, s32[]{:S(2)}) async-start(s8[9437184]{0:T(1024)(128)(4,1)} %bitcast.291), calls=%async_computation.9 | async-start | bytes 8388608
  386.8 6.6 %slice-start.5 = ((s8[9437184]{0:T(1024)(128)(4,1)}), s8[1048576]{0:T(1024)(128)(4,1)S(1)}, s32[]{:S(2)}) async-start(s8[9437184]{0:T(1024)(128)(4,1)} %bitcast.291), calls=%async_computation.10 | async-start | bytes 2097152
  386.8 9.3 %slice-start = ((s8[9437184]{0:T(1024)(128)(4,1)}), s8[4194304]{0:T(1024)(128)(4,1)S(1)}, s32[]{:S(2)}) async-start(s8[9437184]{0:T(1024)(128)(4,1)} %bitcast.289), calls=%async_computation.5 | async-start | bytes 8388608
  386.8 9.3 %slice-start.1 = ((s8[9437184]{0:T(1024)(128)(4,1)}), s8[4194304]{0:T(1024)(128)(4,1)S(1)}, s32[]{:S(2)}) async-start(s8[9437184]{0:T(1024)(128)(4,1)} %bitcast.289), calls=%async_computation.6 | async-start | bytes 8388608
  402.5 24.2 %collective-permute-start.12 = (bf16[1,1536,384]{1,2,0:T(8,128)(2,1)}, bf16[1,1536,384]{1,2,0:T(8,128)(2,1)}, u32[]{:S(2)}, u32[]{:S(2)}) collective-permute-start(bf16[1,1536,384]{1,2,0:T(8,128)(2,1)} %fusion.33), channel_id=1, source_target_pairs={{0,1},{1,0},{2,3},{3,2},{4,5},{5,4},{6,7},{7,6},{8,9},{9,8},{10,11... | collective-permute-start | bytes 3538952 | tf_op jit(solution)/shard_map/ppermute | solution.py:23
  431.7 6.5 %copy-start.12 = (bf16[1536,64]{0,1:T(8,128)(2,1)S(1)}, bf16[1536,64]{0,1:T(8,128)(2,1)}, u32[]{:S(2)}) copy-start(bf16[1536,64]{0,1:T(8,128)(2,1)} %fusion.14) | copy-start | bytes 589828
  431.7 6.6 %copy-start.13 = (bf16[1536,64]{0,1:T(8,128)(2,1)S(1)}, bf16[1536,64]{0,1:T(8,128)(2,1)}, u32[]{:S(2)}) copy-start(bf16[1536,64]{0,1:T(8,128)(2,1)} %fusion.13) | copy-start | bytes 589828
  436.3 39.1 %collective-permute-start.15 = (bf16[2,2,192,384]{3,2,1,0:T(8,128)(2,1)S(1)}, bf16[2,2,192,384]{3,2,1,0:T(8,128)(2,1)S(1)}, u32[]{:S(2)}, u32[]{:S(2)}) collective-permute-start(bf16[2,2,192,384]{3,2,1,0:T(8,128)(2,1)S(1)} %fusion.59), channel_id=1, source_target_pairs={{0,4},{1,5},{2,6},{3,7},{4,0},{5,1},{6,2},{7,3},{8,12},{9,13},{10,... | collective-permute-start | bytes 1769480 | tf_op jit(solution)/shard_map/ppermute | solution.py:23
  440.9 2.1 collective-permute-start.18
  441.5 35.8 %collective-permute-start.13 = (bf16[2,2,192,384]{3,2,0,1:T(8,128)(2,1)S(1)}, bf16[2,2,192,384]{3,2,0,1:T(8,128)(2,1)S(1)}, u32[]{:S(2)}, u32[]{:S(2)}) collective-permute-start(bf16[2,2,192,384]{3,2,0,1:T(8,128)(2,1)S(1)} %fusion.58), channel_id=1, source_target_pairs={{0,2},{1,3},{2,0},{3,1},{4,6},{5,7},{6,4},{7,5},{8,10},{9,11},{10,... | collective-permute-start | bytes 1769480 | tf_op jit(solution)/shard_map/ppermute | solution.py:23
  443.3 34.3 %collective-permute-start.19 = (bf16[2,2,56,576]{3,2,1,0:T(8,128)(2,1)S(1)}, bf16[2,2,56,576]{3,2,1,0:T(8,128)(2,1)S(1)}, u32[]{:S(2)}, u32[]{:S(2)}) collective-permute-start(bf16[2,2,56,576]{3,2,1,0:T(8,128)(2,1)S(1)} %fusion.70), channel_id=1, source_target_pairs={{0,8},{1,9},{2,10},{3,11},{4,12},{5,13},{6,14},{7,15},{8,0},{9,1},... | collective-permute-start | bytes 774152 | tf_op jit(solution)/shard_map/ppermute | solution.py:23
  475.7 9.0 %collective-permute-start.16 = (bf16[2,192,384]{2,1,0:T(8,128)(2,1)S(1)}, bf16[2,192,384]{2,1,0:T(8,128)(2,1)S(1)}, u32[]{:S(2)}, u32[]{:S(2)}) collective-permute-start(bf16[2,192,384]{2,1,0:T(8,128)(2,1)S(1)} %fusion.68), channel_id=1, source_target_pairs={{0,2},{1,3},{2,0},{3,1},{4,6},{5,7},{6,4},{7,5},{8,10},{9,11},{10,... | collective-permute-start | bytes 884744 | tf_op jit(solution)/shard_map/ppermute | solution.py:23
  477.5 8.7 %collective-permute-start.14 = (bf16[2,192,384]{2,1,0:T(8,128)(2,1)S(1)}, bf16[2,192,384]{2,1,0:T(8,128)(2,1)S(1)}, u32[]{:S(2)}, u32[]{:S(2)}) collective-permute-start(bf16[2,192,384]{2,1,0:T(8,128)(2,1)S(1)} %fusion.67), channel_id=1, source_target_pairs={{0,4},{1,5},{2,6},{3,7},{4,0},{5,1},{6,2},{7,3},{8,12},{9,13},{10,... | collective-permute-start | bytes 884744 | tf_op jit(solution)/shard_map/ppermute | solution.py:23
  477.7 10.7 %collective-permute-start.20 = (bf16[2,2,56,576]{3,2,1,0:T(8,128)(2,1)S(1)}, bf16[2,2,56,576]{3,2,1,0:T(8,128)(2,1)S(1)}, u32[]{:S(2)}, u32[]{:S(2)}) collective-permute-start(bf16[2,2,56,576]{3,2,1,0:T(8,128)(2,1)S(1)} %fusion.93), channel_id=1, source_target_pairs={{0,16},{16,0},{1,17},{17,1},{2,18},{18,2},{3,19},{19,3},{4,20},{20... | collective-permute-start | bytes 774152 | tf_op jit(solution)/shard_map/ppermute | solution.py:23
  487.0 15.3 %collective-permute-start.17 = (bf16[192,768]{1,0:T(8,128)(2,1)}, bf16[192,768]{1,0:T(8,128)(2,1)}, u32[]{:S(2)}, u32[]{:S(2)}) collective-permute-start(bf16[192,768]{1,0:T(8,128)(2,1)} %fusion.69), channel_id=1, source_target_pairs={{0,8},{1,9},{2,10},{3,11},{4,12},{5,13},{6,14},{7,15},{8,0},{9,1},... | collective-permute-start | bytes 884744 | tf_op jit(solution)/shard_map/ppermute | solution.py:23
  488.5 8.1 %collective-permute-start.23 = (bf16[56,576]{1,0:T(8,128)(2,1)S(1)}, bf16[56,576]{1,0:T(8,128)(2,1)S(1)}, u32[]{:S(2)}, u32[]{:S(2)}) collective-permute-start(bf16[56,576]{1,0:T(8,128)(2,1)S(1)} %get-tuple-element.78), channel_id=1, source_target_pairs={{0,6},{1,7},{2,4},{3,5},{4,2},{5,3},{6,0},{7,1},{8,14},{9,15},{10,... | collective-permute-start | bytes 193544 | tf_op jit(solution)/shard_map/ppermute | solution.py:23
  490.3 7.0 %collective-permute-start.22 = (bf16[56,576]{1,0:T(8,128)(2,1)S(1)}, bf16[56,576]{1,0:T(8,128)(2,1)S(1)}, u32[]{:S(2)}, u32[]{:S(2)}) collective-permute-start(bf16[56,576]{1,0:T(8,128)(2,1)S(1)} %get-tuple-element.79), channel_id=1, source_target_pairs={{0,4},{1,5},{2,6},{3,7},{4,0},{5,1},{6,2},{7,3},{8,12},{9,13},{10,... | collective-permute-start | bytes 193544 | tf_op jit(solution)/shard_map/ppermute | solution.py:23
  490.7 6.7 %collective-permute-start.21 = (bf16[56,576]{1,0:T(8,128)(2,1)S(1)}, bf16[56,576]{1,0:T(8,128)(2,1)S(1)}, u32[]{:S(2)}, u32[]{:S(2)}) collective-permute-start(bf16[56,576]{1,0:T(8,128)(2,1)S(1)} %get-tuple-element.80), channel_id=1, source_target_pairs={{0,2},{1,3},{2,0},{3,1},{4,6},{5,7},{6,4},{7,5},{8,10},{9,11},{10,... | collective-permute-start | bytes 193544 | tf_op jit(solution)/shard_map/ppermute | solution.py:23
  499.6 15.7 %copy-start.18 = (bf16[1,440,768]{2,1,0:T(8,128)(2,1)S(1)}, bf16[1,440,768]{2,1,0:T(8,128)(2,1)}, u32[]{:S(2)}) copy-start(bf16[1,440,768]{2,1,0:T(8,128)(2,1)} %reduce-scatter.2.cloned.1.call-done) | copy-start | bytes 2027524
  499.6 15.7 %collective-permute-start.24 = (bf16[440,768]{1,0:T(8,128)(2,1)}, bf16[440,768]{1,0:T(8,128)(2,1)S(1)}, u32[]{:S(2)}, u32[]{:S(2)}) collective-permute-start(bf16[440,768]{1,0:T(8,128)(2,1)} %bitcast.355), channel_id=1, source_target_pairs={{0,16},{16,0},{1,17},{17,1},{2,18},{18,2},{3,19},{19,3},{4,20},{20... | collective-permute-start | bytes 2027528 | tf_op jit(solution)/shard_map/ppermute | solution.py:23
  (27 other events, 70.7 us)
Sparse Core Ops, SparseCore 0:
  25.9 101.2 all-gather.2
  338.4 134.1 reduce-scatter.1

commit v2 on v1

--- a/solution.py
+++ b/solution.py
@@ -3,12 +3,17 @@
 import jax
 import jax.numpy as jnp
 from jax import lax
+from jax.experimental import pallas as pl
+from jax.experimental.pallas import tpu as pltpu
 from jax.sharding import PartitionSpec as P
 
 HEADS = 12
 HEAD = 64
 HEAD_GROUPS = 4
 GROUP_WIDTH = HEADS * HEAD // HEAD_GROUPS
+NH = HEADS // HEAD_GROUPS
+BF16 = jnp.bfloat16
+F32 = jnp.float32
 
 score_scale = 0.125
 epsilon = 1e-12
@@ -53,31 +58,113 @@
     return jnp.sum(matrix.astype(jnp.float32), axis=0)
 
 
-def attend_forward(queries, keys, values, bias):
-    context, peaks = [], []
-    for h in range(GROUP_WIDTH // HEAD):
-        cols = slice(h * HEAD, (h + 1) * HEAD)
-        scores = dot_t(queries[:, cols], keys[:, cols]) * score_scale + bias
-        log_total = jax.nn.logsumexp(scores, axis=-1, keepdims=True)
-        probs = jnp.exp(scores - log_total).astype(jnp.bfloat16)
-        context.append(dot(probs, values[:, cols]))
-        peaks.append(log_total)
-    return jnp.concatenate(context, axis=1), peaks
-
-
-def attend_backward(queries, keys, values, bias, peaks, context, dcontext):
-    dq, dk, dv = [], [], []
-    for h in range(GROUP_WIDTH // HEAD):
-        cols = slice(h * HEAD, (h + 1) * HEAD)
-        scores = dot_t(queries[:, cols], keys[:, cols]) * score_scale + bias
-        probs = jnp.exp(scores - peaks[h])
-        dprobs = dot_t(dcontext[:, cols], values[:, cols])
-        delta = jnp.sum(dcontext[:, cols].astype(jnp.float32) * context[:, cols], axis=1, keepdims=True)
-        dscores = (probs * (dprobs - delta)).astype(jnp.bfloat16)
-        dq.append(dot(dscores, keys[:, cols]) * score_scale)
-        dk.append(t_dot(dscores, queries[:, cols]) * score_scale)
-        dv.append(t_dot(probs.astype(jnp.bfloat16), dcontext[:, cols]))
-    return tuple(jnp.concatenate(part, axis=1) for part in (dq, dk, dv))
+def thirds(x):
+    hi=x.astype(BF16)
+    r=x-hi.astype(F32)
+    mid=r.astype(BF16)
+    lo=(r-mid.astype(F32)).astype(BF16)
+    return hi,mid,lo
+
+def fwd_body(q_ref, kv_ref, kb_ref, c_ref, cf_ref, st_ref, kt, va, oacc, lacc, *, bq):
+    i=pl.program_id(0); h=pl.program_id(1)
+    W=NH*HEAD
+    @pl.when((i==0)&(h==0))
+    def _():
+        tail=kb_ref[:,HEAD:]
+        for g in range(NH):
+            ka=jnp.concatenate([kv_ref[:,g*HEAD:(g+1)*HEAD],tail],axis=1)
+            kt[g]=ka.T
+            va[g]=jnp.concatenate([kv_ref[:,W+g*HEAD:W+(g+1)*HEAD],tail],axis=1)
+    one=jnp.where(lax.broadcasted_iota(jnp.int32,(bq,HEAD),1)==0,1.0,0.0).astype(BF16)
+    def head(g):
+        qa=jnp.concatenate([q_ref[:,g*HEAD:(g+1)*HEAD],one],axis=1)
+        s=dot(qa,kt[g])
+        m=jnp.max(s,axis=1,keepdims=True)
+        p=jnp.exp(s-m).astype(BF16)
+        o=dot(p,va[g])
+        l=o[:,HEAD+1:HEAD+2]
+        oacc[g]=o/l
+        lacc[g]=jnp.broadcast_to(m+jnp.log(l),(bq,128))
+    for g in range(NH):
+        @pl.when(h==g)
+        def _(): head(g)
+    @pl.when(h==NH-1)
+    def _():
+        c=jnp.concatenate([oacc[g][:,:HEAD] for g in range(NH)],axis=1)
+        c_ref[...]=c.astype(BF16)
+        cf_ref[...]=c
+        lane=lax.broadcasted_iota(jnp.int32,(bq,128),1)
+        st=lacc[0]
+        for g in range(1,NH): st=jnp.where(lane==g,lacc[g],st)
+        st_ref[...]=st
+
+def attend_forward(q,kv,kb,bq=256):
+    n,W=q.shape; L=kv.shape[0]
+    return pl.pallas_call(partial(fwd_body,bq=bq),
+        grid=(n//bq,NH),
+        in_specs=[pl.BlockSpec((bq,W),lambda i,h:(i,0)),pl.BlockSpec((L,2*W),lambda i,h:(0,0)),pl.BlockSpec((L,128),lambda i,h:(0,0))],
+        out_specs=[pl.BlockSpec((bq,W),lambda i,h:(i,0)),pl.BlockSpec((bq,W),lambda i,h:(i,0)),pl.BlockSpec((bq,128),lambda i,h:(i,0))],
+        out_shape=[jax.ShapeDtypeStruct((n,W),BF16),jax.ShapeDtypeStruct((n,W),F32),jax.ShapeDtypeStruct((n,128),F32)],
+        scratch_shapes=[pltpu.VMEM((NH,128,L),BF16),pltpu.VMEM((NH,L,128),BF16),pltpu.VMEM((NH,bq,128),F32),pltpu.VMEM((NH,bq,128),F32)],
+        name="attend_forward",
+    )(q,kv,kb)
+
+def bwd_body(q_ref, kv_ref, kb_ref, cf_ref, st_ref, dc_ref, dq_ref, dkv_ref, qt, qn, dct, dcn, dqt, dk, dv, *, bk, nk):
+    j=pl.program_id(0); h=pl.program_id(1)
+    W=NH*HEAD
+    n=q_ref.shape[0]
+    @pl.when((j==0)&(h==0))
+    def _():
+        lane=lax.broadcasted_iota(jnp.int32,(n,HEAD),1)
+        def tail(x,first):
+            hi,mid,lo=thirds(-x)
+            z=jnp.where(lane==1,hi.astype(F32),jnp.where(lane==2,mid.astype(F32),jnp.where(lane==3,lo.astype(F32),0.0)))
+            return jnp.where(lane==0,first,z).astype(BF16)
+        for g in range(NH):
+            cols=slice(g*HEAD,(g+1)*HEAD)
+            qa=jnp.concatenate([q_ref[:,cols],tail(st_ref[:,g:g+1],1.0)],axis=1)
+            qn[g]=qa
+            qt[g]=qa.T
+            d=dc_ref[:,cols]
+            delta=jnp.sum(d.astype(F32)*cf_ref[:,cols],axis=1,keepdims=True)
+            da=jnp.concatenate([d,tail(delta,0.0)],axis=1)
+            dcn[g]=da
+            dct[g]=da.T
+        dqt[...]=jnp.zeros_like(dqt)
+    tail=kb_ref[:,HEAD:]
+    def head(g):
+        k=kv_ref[:,g*HEAD:(g+1)*HEAD]
+        ka=jnp.concatenate([k,tail],axis=1)
+        va=jnp.concatenate([kv_ref[:,W+g*HEAD:W+(g+1)*HEAD],tail],axis=1)
+        p=jnp.exp(dot(ka,qt[g]))
+        dp=dot(va,dct[g])
+        ds=(p*dp).astype(BF16)
+        dv[g]=dot(p.astype(BF16),dcn[g])
+        dk[g]=dot(ds,qn[g])
+        dqt[g]=dqt[g]+t_dot(ka,ds)[:HEAD]
+    for g in range(NH):
+        @pl.when(h==g)
+        def _(): head(g)
+    @pl.when(h==NH-1)
+    def _():
+        dkv_ref[...]=jnp.concatenate([dk[g][:,:HEAD] for g in range(NH)]+[dv[g][:,:HEAD] for g in range(NH)],axis=1)
+    @pl.when((h==NH-1)&(j==nk-1))
+    def _():
+        for g in range(NH):
+            dq_ref[:,g*HEAD:(g+1)*HEAD]=(dqt[g].T*0.125).astype(BF16)
+
+def attend_backward(q,kv,kb,cf,st,dc,bk=512):
+    n,W=q.shape; L=kv.shape[0]; nk=L//bk
+    full=lambda a: pl.BlockSpec(a.shape,lambda j,h:(0,0))
+    return pl.pallas_call(partial(bwd_body,bk=bk,nk=nk),
+        grid=(nk,NH),
+        in_specs=[full(q),pl.BlockSpec((bk,2*W),lambda j,h:(j,0)),pl.BlockSpec((bk,128),lambda j,h:(j,0)),full(cf),full(st),full(dc)],
+        out_specs=[pl.BlockSpec((n,W),lambda j,h:(0,0)),pl.BlockSpec((bk,2*W),lambda j,h:(j,0))],
+        out_shape=[jax.ShapeDtypeStruct((n,W),BF16),jax.ShapeDtypeStruct((L,2*W),F32)],
+        scratch_shapes=[pltpu.VMEM((NH,128,n),BF16),pltpu.VMEM((NH,n,128),BF16),pltpu.VMEM((NH,128,n),BF16),pltpu.VMEM((NH,n,128),BF16),
+            pltpu.VMEM((NH,HEAD,n),F32),pltpu.VMEM((NH,bk,128),F32),pltpu.VMEM((NH,bk,128),F32)],
+        name="attend_backward",
+    )(q,kv,kb,cf,st,dc)
 
 
 def per_device(
@@ -186,15 +273,14 @@
         return lax.dynamic_slice_in_dim(vector, head_group * GROUP_WIDTH, GROUP_WIDTH)
 
     qkv_bias = jnp.concatenate([own_columns(q_bias), jnp.zeros((GROUP_WIDTH,), jnp.float32), own_columns(v_bias)])
-    qkv = (dot(x_all, w_all) + qkv_bias).astype(bf16)
-    queries = qkv[:, :GROUP_WIDTH]
-    kv = qkv[:, GROUP_WIDTH:][None]
+    qkv = dot(x_all, w_all) + qkv_bias
+    queries = (qkv[:, :GROUP_WIDTH] * score_scale).astype(bf16)
+    kv = qkv[:, GROUP_WIDTH:].astype(bf16)[None]
     for b in part_bits:
         bit = (me // b) % 2
         theirs = sflip(kv, b)
         kv = jnp.where(bit == 0, jnp.concatenate([kv, theirs]), jnp.concatenate([theirs, kv]))
     kv = kv.reshape(-1, 2 * GROUP_WIDTH)
-    keys, values = kv[:, :GROUP_WIDTH], kv[:, GROUP_WIDTH:]
 
     part = jnp.arange(n_parts, dtype=jnp.int32)
     part_device = part % 2 + 4 * (part // 2)
@@ -202,9 +288,11 @@
     member_device = (member // 4) * HI + ((member // 2) % 2) * ZO + (member % 2) * YO
     device = part_device[:, None] + member_device[None, :]
     position = (device[:, :, None] * rows + jnp.arange(rows, dtype=jnp.int32)).reshape(-1)
-    bias = jnp.where(position < pick(valid_len, z1), 0.0, masked_score)[None, :]
-
-    context_full, peaks = attend_forward(queries, keys, values, bias)
+    bias = jnp.where(position < pick(valid_len, z1), 0.0, masked_score)[:, None]
+    lane = jnp.arange(128, dtype=jnp.int32)[None, :]
+    key_tail = jnp.where(lane == HEAD, bias, jnp.where((lane > HEAD) & (lane < HEAD + 4), 1.0, 0.0)).astype(bf16)
+
+    context, context_full, stats = attend_forward(queries, kv, key_tail)
 
     teams = [
         [a * HI + b * ZO + c * YO + q for a in range(2) for b in range(2) for c in range(2)]
@@ -214,7 +302,7 @@
     def exchange(blocks):
         return lax.all_to_all(blocks, "seq", 0, 0, axis_index_groups=teams, tiled=True)
 
-    context = exchange(context_full.astype(bf16).reshape(8, rows, GROUP_WIDTH))
+    context = exchange(context.reshape(8, rows, GROUP_WIDTH))
     context = context.reshape(2, HEAD_GROUPS, rows, GROUP_WIDTH).transpose(0, 2, 1, 3).reshape(2 * rows, width)
 
     n_dev = grp_size * seq_size
@@ -287,15 +375,15 @@
     )
     dinner_bias = small[6 * out_rows :]
 
-    dqueries, dkeys, dvalues = attend_backward(queries, keys, values, bias, peaks, context_full, dcontext)
-    dkv = jnp.concatenate([dkeys, dvalues], axis=1).reshape(n_parts, 8 * rows, 2 * GROUP_WIDTH)
+    dqueries, dkv = attend_backward(queries, kv, key_tail, context_full, stats, dcontext)
+    dkv = dkv.reshape(n_parts, 8 * rows, 2 * GROUP_WIDTH)
     for b in reversed(part_bits):
         bit = (me // b) % 2
         n_now = dkv.shape[0] // 2
         low, high = dkv[:n_now], dkv[n_now:]
         sent = jnp.where(bit == 0, high, low).astype(bf16)
         dkv = jnp.where(bit == 0, low, high) + sflip(sent, b).astype(jnp.float32)
-    dqkv = jnp.concatenate([dqueries.astype(bf16), dkv[0].astype(bf16)], axis=1)
+    dqkv = jnp.concatenate([dqueries, dkv[0].astype(bf16)], axis=1)
 
     dx = dot_t(dqkv, w_all).reshape(2, 2, 2, rows, width)
     da, db = dx[..., :half_width], dx[..., half_width:]

time: 534 us -> 445 us (0.83)
  matrix products: 156 us -> 43.9 us
  Pallas kernels: 0 us -> 75 us
  other arithmetic: 94.1 us -> 40 us
  local copies, waits for them, and re-layouts: 99 us -> 73.7 us
  blocking collectives: 0 us -> 23.6 us
  waiting for transfers between devices: 118 us -> 135 us
  starting transfers between devices: 41.7 us -> 29 us
    pallas_call x0 -> x2, Pallas kernels: none -> 75 us  [the longest x1 46.4 us: attend_backward(): pl.pallas_call(partial(bwd_body, bk=bk, nk=nk), grid=(nk, NH), in_specs=[...]
    dot_general x10 -> x4, matrix products: 72.6 us -> 13.4 us  [dot_t(): lax.dot_general(left, right, (((1,), (1,)), ((), ())), preferred_element_...]
    dot_general x10 -> x4, matrix products: 48.8 us -> 18.7 us  [dot(): return jnp.dot(left, right, preferred_element_type=jnp.float32)]
    reduce_sum x4 -> x0, other arithmetic: 29.1 us -> none  [the longest x3 27.1 us: attend_forward(): log_total = jax.nn.logsumexp(scores, axis=-1, keepdims=True)]
    all_to_all x0 -> x1, blocking collectives: none -> 23.6 us  [exchange(): lax.all_to_all(blocks, 'seq', 0, 0, axis_index_groups=teams, tiled=True)]
    convert_element_type x4 -> x3, other arithmetic: 29.3 us -> 5.65 us  [the longest x1 3.26 us: per_device(): dqkv = jnp.concatenate([dqueries, dkv[0].astype(bf16)], axis=1)]
    dot_general x10 -> x4, matrix products: 34.9 us -> 11.8 us  [t_dot(): lax.dot_general(left, right, (((0,), (0,)), ((), ())), preferred_element_...]
    ppermute x25, waiting for transfers between devices: 108 us -> 118 us  [flip(): return lax.ppermute(value, axis, [(i, i ^ mask) for i in range(size)])]
  transfers between devices with their start and end apart: 29 -> 28, of which waited for: 14 -> 16; matrix products, arithmetic and copies ran while one was open for 52% -> 15% of each run, Pallas kernels for 0% -> 17%
where the time goes in v2:
time: 445 us; the launch traced here: 437 us
  waiting for transfers between devices  135 us (30%)
  Pallas kernels  75 us (17%)
  local copies, waits for them, and re-layouts  73.7 us (17%)
  matrix products  43.9 us (10%)
  other arithmetic  40 us (9%)
  starting transfers between devices  29 us (7%)
  blocking collectives  23.6 us (5%)
  between operations  16.6 us (4%)
    ppermute x25, waiting for transfers between devices, flip(): return lax.ppermute(value, axis, [(i, i ^ mask) for i in range(size)])  118 us
    pallas_call x1, Pallas kernels, attend_backward(): pl.pallas_call(partial(bwd_body, bk=bk, nk=nk), grid=(nk, NH), in_specs=[...  46.4 us
    pallas_call x1, Pallas kernels, attend_forward(): pl.pallas_call(partial(fwd_body, bq=bq), grid=(n // bq, NH), in_specs=[pl...  28.6 us
    all_to_all x1, blocking collectives, exchange(): lax.all_to_all(blocks, 'seq', 0, 0, axis_index_groups=teams, tiled=True)  23.6 us
    ppermute x25, starting transfers between devices, flip(): return lax.ppermute(value, axis, [(i, i ^ mask) for i in range(size)])  22.1 us
    dot_general x4, matrix products, dot(): return jnp.dot(left, right, preferred_element_type=jnp.float32)  18.7 us
    all_to_all x1, waiting for transfers between devices, exchange(): lax.all_to_all(blocks, 'seq', 0, 0, axis_index_groups=teams, tiled=True)  16.7 us
    convert_element_type x2, local copies, waits for them, and re-layouts, per_device(): dinner_blocks.reshape(seq_size, -1, width).astype(bf16)  13.6 us
  transfers between devices with their start and end apart: 28, of which 16 were waited for; matrix products, arithmetic and copies ran while one was open for 15% of the time, Pallas kernels for 17%

profile of v2, /device:TPU:0, one launch (start us, length us, event | category | flops | bytes accessed | tf_op | source)
XLA Modules:
  0.0 436.9 jit_solution(11488050365238293231)
XLA Ops:
  12.9 6.1 %concatenate.239 = bf16[288]{0:T(512)(128)(2,1)S(1)} concatenate(bf16[24]{0:T(256)(128)(2,1)} %param.23, bf16[24]{0:T(256)(128)(2,1)} %param.26, bf16[24]{0:T(256)(128)(2,1)} %param.28, bf16[24]{0:T(256)(128)(2,1)} %param.29, bf16[24]{0:T(256)(128)(2,1)} %param.30, bf16[24]{0:T(256)(128)(2,1)} %param.34, bf16[24]{0:T(256)(128)(2,1)} %param.35, bf16[24]{0:T(256)(128)(2,1)} %param.36, ...), dimensions={0} | concatenate | bytes 1152 | tf_op jit(solution)/shard_map/concatenate | solution.py:233
  22.7 4.1 collective-permute-start.7
  27.4 3.0 collective-permute-start
  32.6 2.5 collective-permute-done.6
  35.4 19.9 %collective-permute-done.8 = bf16[2,2,32,576]{3,2,1,0:T(8,128)(2,1)S(1)} collective-permute-done((bf16[2,2,32,576]{3,2,1,0:T(8,128)(2,1)S(1)}, bf16[2,2,32,576]{3,2,1,0:T(8,128)(2,1)S(1)}, u32[]{:S(2)}, u32[]{:S(2)}) %collective-permute-start.8) | collective-permute-done | bytes 147488 | tf_op jit(solution)/shard_map/ppermute | solution.py:28
  55.4 1.5 collective-permute-start.9
  57.6 1.6 collective-permute-start.1
  59.2 13.0 %collective-permute-done.9 = bf16[2,2,2,32,576]{4,3,2,1,0:T(8,128)(2,1)S(1)} collective-permute-done((bf16[2,2,2,32,576]{4,3,2,1,0:T(8,128)(2,1)S(1)}, bf16[2,2,2,32,576]{4,3,2,1,0:T(8,128)(2,1)S(1)}, u32[]{:S(2)}, u32[]{:S(2)}) %collective-permute-start.9) | collective-permute-done | bytes 294944 | tf_op jit(solution)/shard_map/ppermute | solution.py:28
  73.6 1.5 collective-permute-start.4
  79.5 11.1 %collective-permute-done.4 = bf16[2,2,192,384]{3,2,1,0:T(8,128)(2,1)S(1)} collective-permute-done((bf16[2,2,192,384]{3,2,1,0:T(8,128)(2,1)}, bf16[2,2,192,384]{3,2,1,0:T(8,128)(2,1)S(1)}, u32[]{:S(2)}, u32[]{:S(2)}) %collective-permute-start.4) | collective-permute-done | bytes 589856 | tf_op jit(solution)/shard_map/ppermute | solution.py:28
  90.9 11.0 %collective-permute-done.2 = bf16[2,2,192,384]{3,2,1,0:T(8,128)(2,1)} collective-permute-done((bf16[2,2,192,384]{3,2,1,0:T(8,128)(2,1)}, bf16[2,2,192,384]{3,2,1,0:T(8,128)(2,1)}, u32[]{:S(2)}, u32[]{:S(2)}) %collective-permute-start.2) | collective-permute-done | bytes 589856 | tf_op jit(solution)/shard_map/ppermute | solution.py:28
  101.9 1.5 fusion.20
  103.7 2.0 convolution_add_fusion.1
  109.1 1.8 maximum_select_fusion
  110.9 28.6 %attend_forward.1 = (bf16[1536,192]{1,0:T(8,128)(2,1)}, f32[1536,192]{1,0:T(8,128)}, f32[1536,128]{1,0:T(8,128)}) custom-call(bf16[1536,192]{1,0:T(8,128)(2,1)} %fusion.9.q_ref, bf16[3072,384]{1,0:T(8,128)(2,1)} %bitcast.272, bf16[3072,128]{1,0:T(8,128)(2,1)} %select_convert_fusion.1.kb_ref), custom_call_target="tpu_custom_call" | custom-call | tf_op jit(solution)/shard_map/attend_forward/pallas_call | solution.py:103
  139.5 6.8 %all-to-all-start = ((bf16[8,192,192]{2,1,0:T(8,128)(2,1)}), bf16[8,192,192]{2,1,0:T(8,128)(2,1)}, u32[]{:S(2)}, u32[]{:S(2)}) async-start(bf16[8,192,192]{2,1,0:T(8,128)(2,1)} %bitcast.322), calls=%async_computation | async-start | bytes 1572864 | tf_op jit(solution)/shard_map/all_to_all | solution.py:303
  150.4 16.7 %all-to-all-done = bf16[8,192,192]{2,1,0:T(8,128)(2,1)} async-done(((bf16[8,192,192]{2,1,0:T(8,128)(2,1)}), bf16[8,192,192]{2,1,0:T(8,128)(2,1)}, u32[]{:S(2)}, u32[]{:S(2)}) %all-to-all-start) | async-done | bytes 589856 | tf_op jit(solution)/shard_map/all_to_all | solution.py:303
  167.0 3.5 copy.107
  170.6 2.4 reshape.1312
  173.0 6.7 %fusion.72 = (bf16[32,96,768]{2,1,0:T(8,128)(2,1)}, bf16[32,96,768]{2,1,0:T(8,128)(2,1)S(1)}) fusion(bf16[32,216,768]{2,1,0:T(8,128)(2,1)} %bitcast.284), kind=kLoop, calls=%fused_computation.225 | loop fusion | bytes 18874368 | tf_op jit(solution)/shard_map/slice | solution.py:312
  181.0 2.3 copy.108
  185.6 13.8 %multiply_convert_fusion = (bf16[384,3072]{1,0:T(8,128)(2,1)S(1)}, f32[384,3072]{1,0:T(8,128)S(1)}, f32[384,3072]{1,0:T(8,128)}) fusion(f32[3072]{0:T(1024)S(1)} %copy-done.13, bf16[768,3072]{1,0:T(8,128)(2,1)S(1)} %bitcast.290, f32[384,768]{1,0:T(8,128)S(1)} %get-tuple-element.101, f32[768]{0:T(1024)S(1)} %reshape.1340, f32[768]{0:T(1024)S(1)} %reshape.1339, ...), kind=kOutput, calls=%fused_computation.6 | convolution fusion | flops 1891270656 | bytes 17716224 | tf_op jit(solution)/shard_map/dot_general | solution.py:46
  199.5 2.1 fusion.79
  204.0 4.3 convolution_convert_fusion
  208.3 5.7 %fusion.67 = (bf16[3072]{0:T(1024)(128)(2,1)}, bf16[384,3072]{1,0:T(8,128)(2,1)S(1)}) fusion(f32[384,3072]{1,0:T(8,128)S(1)} %get-tuple-element.55, f32[384,3072]{1,0:T(8,128)} %get-tuple-element.102, bf16[384,768]{1,0:T(8,128)(2,1)S(1)} %get-tuple-element.47, bf16[3072,768]{1,0:T(8,128)(2,1)S(1)} %bitcast.300), kind=kOutput, calls=%fused_computation.221 | convolution fusion | flops 1829630976 | bytes 17111040 | tf_op jit(solution)/shard_map/dot_general | solution.py:50
  214.0 2.9 multiply_reduce_fusion
  216.9 4.7 %convolution_convert_fusion.1 = bf16[768,3072]{1,0:T(8,128)(2,1)} fusion(bf16[384,3072]{1,0:T(8,128)(2,1)S(1)} %get-tuple-element.45, f32[384,768]{1,0:T(8,128)S(1)} %get-tuple-element.101, f32[768]{0:T(1024)S(1)} %copy-done.15, f32[768]{0:T(1024)S(1)} %reshape.1339, f32[384]{0:T(512)S(1)} %fusion.53, f32[384]{0:T(512)S(1)} %broadcast_multiply_fusion.1), kind=kOutput, calls=%fused_computation.3 | convolution fusion | flops 1815773184 | bytes 8266752 | tf_op jit(solution)/shard_map/dot_general | solution.py:54
  230.0 10.2 %convert_element_type.343 = bf16[16,48,4,768]{3,2,1,0:T(4,128)(2,1)} reshape(bf16[768,3072]{1,0:T(8,128)(2,1)} %convolution_convert_fusion.1) | data formatting | bytes 9437184 | tf_op jit(solution)/shard_map/convert_element_type | solution.py:355
  240.2 3.4 copy.132
  244.6 11.1 %pad_maximum_fusion = bf16[16,440,768]{2,1,0:T(8,128)(2,1)} fusion(bf16[16,8,768]{2,1,0:T(8,128)(2,1)S(1)} %bitcast.321, bf16[16,48,768]{2,1,0:T(8,128)(2,1)S(1)} %convolution_convert_fusion.2, bf16[16,192,768]{2,1,0:T(8,128)(2,1)S(1)} %bitcast.296, bf16[16,192,768]{2,1,0:T(8,128)(2,1)S(1)} %bitcast.277), kind=kLoop, calls=%fused_computation | loop fusion | flops 43253760 | bytes 21626880 | tf_op jit(solution)/shard_map/concatenate | solution.py:353
  255.7 2.8 convolution_convert_fusion.3
  258.5 3.0 reshape.1319
  261.6 1.4 copy.109
  263.0 23.6 %all_to_all.10 = bf16[8,192,192]{2,1,0:T(8,128)(2,1)} all-to-all(bf16[8,192,192]{2,1,0:T(8,128)(2,1)S(1)} %bitcast.303), channel_id=1, replica_groups={{0,2,4,6,8,10,12,14},{1,3,5,7,9,11,13,15},{16,18,20,22,24,26,28,30},{17..., dimensions={0} | all-to-all | bytes 1179648 | tf_op jit(solution)/shard_map/all_to_all | solution.py:303
  286.6 46.4 %attend_backward.1 = (bf16[1536,192]{1,0:T(8,128)(2,1)}, f32[3072,384]{1,0:T(8,128)}) custom-call(bf16[1536,192]{1,0:T(8,128)(2,1)} %fusion.9.q_ref, bf16[3072,384]{1,0:T(8,128)(2,1)} %bitcast.273, bf16[3072,128]{1,0:T(8,128)(2,1)} %select_convert_fusion.1.kb_ref, f32[1536,192]{1,0:T(8,128)} %get-tuple-element.35.cf_ref, ...), custom_call_target="tpu_custom_call" | custom-call | tf_op jit(solution)/shard_map/attend_backward/pallas_call | solution.py:159
  333.0 3.7 fusion.17
  336.7 2.6 copy.121
  339.9 3.3 fusion.18
  344.3 2.0 fusion.80
  348.6 2.1 fusion.7
  353.2 1.5 collective-permute-start.19
  354.7 35.1 %collective-permute-done.15 = bf16[2,2,192,384]{3,2,1,0:T(8,128)(2,1)S(1)} collective-permute-done((bf16[2,2,192,384]{3,2,1,0:T(8,128)(2,1)S(1)}, bf16[2,2,192,384]{3,2,1,0:T(8,128)(2,1)S(1)}, u32[]{:S(2)}, u32[]{:S(2)}) %collective-permute-start.15) | collective-permute-done | bytes 589856 | tf_op jit(solution)/shard_map/ppermute | solution.py:28
  390.1 1.4 collective-permute-start.16
  392.0 6.5 %collective-permute-done.16 = bf16[2,192,384]{2,1,0:T(8,128)(2,1)S(1)} collective-permute-done((bf16[2,192,384]{2,1,0:T(8,128)(2,1)S(1)}, bf16[2,192,384]{2,1,0:T(8,128)(2,1)S(1)}, u32[]{:S(2)}, u32[]{:S(2)}) %collective-permute-start.16) | collective-permute-done | bytes 294944 | tf_op jit(solution)/shard_map/ppermute | solution.py:28
  401.3 2.1 collective-permute-start.23
  405.0 3.3 collective-permute-done.23
  411.9 3.4 collective-permute-done.17
  417.3 8.6 %collective-permute-done.24 = bf16[440,768]{1,0:T(8,128)(2,1)S(1)} collective-permute-done((bf16[440,768]{1,0:T(8,128)(2,1)}, bf16[440,768]{1,0:T(8,128)(2,1)S(1)}, u32[]{:S(2)}, u32[]{:S(2)}) %collective-permute-start.24) | collective-permute-done | bytes 675872 | tf_op jit(solution)/shard_map/ppermute | solution.py:28
  (227 shorter events, 61.5 us)
Async XLA Ops:
  7.2 20.2 %copy-start.10 = (bf16[2,192,768]{2,1,0:T(8,128)(2,1)S(1)}, bf16[2,192,768]{2,1,0:T(8,128)(2,1)}, u32[]{:S(2)}) copy-start(bf16[2,192,768]{2,1,0:T(8,128)(2,1)} %param.20) | copy-start | bytes 1769476
  7.2 165.8 %all-gather.3.cloned.1.call-start = ((), (), s32[]{:S(2)}) async-start(), calls=%async_computation.4 | async-start | bytes 10948608 | tf_op jit(solution)/shard_map/all_gather | solution.py:219
  10.4 20.0 %copy-start.18 = (s32[2]{0:T(128)S(1)}, s32[2]{0:T(128)}, u32[]{:S(2)}) copy-start(s32[2]{0:T(128)} %param.21) | copy-start | bytes 28
  22.7 9.9 %collective-permute-start.7 = (bf16[32,576]{1,0:T(8,128)(2,1)S(1)}, bf16[32,576]{1,0:T(8,128)(2,1)S(1)}, u32[]{:S(2)}, u32[]{:S(2)}) collective-permute-start(bf16[32,576]{1,0:T(8,128)(2,1)S(1)} %get-tuple-element.91), channel_id=1, source_target_pairs={{0,6},{1,7},{2,4},{3,5},{4,2},{5,3},{6,0},{7,1},{8,14},{9,15},{10,... | collective-permute-start | bytes 110600 | tf_op jit(solution)/shard_map/ppermute | solution.py:28
  26.7 8.3 %collective-permute-start.6 = (bf16[32,576]{1,0:T(8,128)(2,1)S(1)}, bf16[32,576]{1,0:T(8,128)(2,1)S(1)}, u32[]{:S(2)}, u32[]{:S(2)}) collective-permute-start(bf16[32,576]{1,0:T(8,128)(2,1)S(1)} %get-tuple-element.90), channel_id=1, source_target_pairs={{0,4},{1,5},{2,6},{3,7},{4,0},{5,1},{6,2},{7,3},{8,12},{9,13},{10,... | collective-permute-start | bytes 110600 | tf_op jit(solution)/shard_map/ppermute | solution.py:28
  27.2 7.9 %collective-permute-start.5 = (bf16[32,576]{1,0:T(8,128)(2,1)S(1)}, bf16[32,576]{1,0:T(8,128)(2,1)S(1)}, u32[]{:S(2)}, u32[]{:S(2)}) collective-permute-start(bf16[32,576]{1,0:T(8,128)(2,1)S(1)} %get-tuple-element.89), channel_id=1, source_target_pairs={{0,2},{1,3},{2,0},{3,1},{4,6},{5,7},{6,4},{7,5},{8,10},{9,11},{10,... | collective-permute-start | bytes 110600 | tf_op jit(solution)/shard_map/ppermute | solution.py:28
  27.4 29.7 %collective-permute-start = (bf16[192,768]{1,0:T(8,128)(2,1)S(1)}, bf16[192,768]{1,0:T(8,128)(2,1)S(1)}, u32[]{:S(2)}, u32[]{:S(2)}) collective-permute-start(bf16[192,768]{1,0:T(8,128)(2,1)S(1)} %get-tuple-element.70), channel_id=1, source_target_pairs={{0,8},{1,9},{2,10},{3,11},{4,12},{5,13},{6,14},{7,15},{8,0},{9,1},... | collective-permute-start | bytes 884744 | tf_op jit(solution)/shard_map/ppermute | solution.py:28
  35.2 20.2 %collective-permute-start.8 = (bf16[2,2,32,576]{3,2,1,0:T(8,128)(2,1)S(1)}, bf16[2,2,32,576]{3,2,1,0:T(8,128)(2,1)S(1)}, u32[]{:S(2)}, u32[]{:S(2)}) collective-permute-start(bf16[2,2,32,576]{3,2,1,0:T(8,128)(2,1)S(1)} %maximum_select_fusion.15), channel_id=1, source_target_pairs={{0,8},{1,9},{2,10},{3,11},{4,12},{5,13},{6,14},{7,15},{8,0},{9,1},... | collective-permute-start | bytes 442376 | tf_op jit(solution)/shard_map/ppermute | solution.py:28
  55.4 16.8 %collective-permute-start.9 = (bf16[2,2,2,32,576]{4,3,2,1,0:T(8,128)(2,1)S(1)}, bf16[2,2,2,32,576]{4,3,2,1,0:T(8,128)(2,1)S(1)}, u32[]{:S(2)}, u32[]{:S(2)}) collective-permute-start(bf16[2,2,2,32,576]{4,3,2,1,0:T(8,128)(2,1)S(1)} %maximum_select_fusion.12), channel_id=1, source_target_pairs={{0,16},{16,0},{1,17},{17,1},{2,18},{18,2},{3,19},{19,3},{4,20},{20... | collective-permute-start | bytes 884744 | tf_op jit(solution)/shard_map/ppermute | solution.py:28
  57.4 15.2 %collective-permute-start.3 = (bf16[2,192,384]{2,1,0:T(8,128)(2,1)S(1)}, bf16[2,192,384]{2,1,0:T(8,128)(2,1)S(1)}, u32[]{:S(2)}, u32[]{:S(2)}) collective-permute-start(bf16[2,192,384]{2,1,0:T(8,128)(2,1)S(1)} %get-tuple-element.67), channel_id=1, source_target_pairs={{0,4},{1,5},{2,6},{3,7},{4,0},{5,1},{6,2},{7,3},{8,12},{9,13},{10,... | collective-permute-start | bytes 884744 | tf_op jit(solution)/shard_map/ppermute | solution.py:28
  57.6 17.6 %collective-permute-start.1 = (bf16[2,192,384]{2,1,0:T(8,128)(2,1)S(1)}, bf16[2,192,384]{2,1,0:T(8,128)(2,1)S(1)}, u32[]{:S(2)}, u32[]{:S(2)}) collective-permute-start(bf16[2,192,384]{2,1,0:T(8,128)(2,1)S(1)} %get-tuple-element.68), channel_id=1, source_target_pairs={{0,2},{1,3},{2,0},{3,1},{4,6},{5,7},{6,4},{7,5},{8,10},{9,11},{10,... | collective-permute-start | bytes 884744 | tf_op jit(solution)/shard_map/ppermute | solution.py:28
  72.4 4.0 collective-permute-start.10
  73.6 17.1 %collective-permute-start.4 = (bf16[2,2,192,384]{3,2,1,0:T(8,128)(2,1)}, bf16[2,2,192,384]{3,2,1,0:T(8,128)(2,1)S(1)}, u32[]{:S(2)}, u32[]{:S(2)}) collective-permute-start(bf16[2,2,192,384]{3,2,1,0:T(8,128)(2,1)} %maximum_select_fusion.10), channel_id=1, source_target_pairs={{0,2},{1,3},{2,0},{3,1},{4,6},{5,7},{6,4},{7,5},{8,10},{9,11},{10,... | collective-permute-start | bytes 1769480 | tf_op jit(solution)/shard_map/ppermute | solution.py:28
  76.0 25.9 %collective-permute-start.2 = (bf16[2,2,192,384]{3,2,1,0:T(8,128)(2,1)}, bf16[2,2,192,384]{3,2,1,0:T(8,128)(2,1)}, u32[]{:S(2)}, u32[]{:S(2)}) collective-permute-start(bf16[2,2,192,384]{3,2,1,0:T(8,128)(2,1)} %maximum_select_fusion.8), channel_id=1, source_target_pairs={{0,4},{1,5},{2,6},{3,7},{4,0},{5,1},{6,2},{7,3},{8,12},{9,13},{10,... | collective-permute-start | bytes 1769480 | tf_op jit(solution)/shard_map/ppermute | solution.py:28
  77.1 26.6 %copy-start.6 = (bf16[32,24,576]{2,1,0:T(8,128)(2,1)}, bf16[32,24,576]{2,1,0:T(8,128)(2,1)S(1)}, u32[]{:S(2)}) copy-start(bf16[32,24,576]{2,1,0:T(8,128)(2,1)S(1)} %slice.278) | copy-start | bytes 2654212
  106.2 2.9 collective-permute-start.11
  110.9 35.5 %copy-start = (bf16[2,192,768]{2,1,0:T(8,128)(2,1)S(1)}, bf16[2,192,768]{2,1,0:T(8,128)(2,1)}, u32[]{:S(2)}) copy-start(bf16[2,192,768]{2,1,0:T(8,128)(2,1)} %param.37) | copy-start | bytes 1769476
  139.5 27.5 %all-to-all-start = ((bf16[8,192,192]{2,1,0:T(8,128)(2,1)}), bf16[8,192,192]{2,1,0:T(8,128)(2,1)}, u32[]{:S(2)}, u32[]{:S(2)}) async-start(bf16[8,192,192]{2,1,0:T(8,128)(2,1)} %bitcast.322), calls=%async_computation | async-start | bytes 1572864 | tf_op jit(solution)/shard_map/all_to_all | solution.py:303
  146.3 265.0 %reduce-scatter.2.cloned.1.call-start = ((), (), s32[]{:S(2)}) async-start(), calls=%async_computation.3 | async-start | bytes 11489280 | tf_op jit(solution)/shard_map/reduce_scatter | solution.py:362
  150.1 49.3 %copy-start.14 = (f32[768]{0:T(1024)}, f32[768]{0:T(1024)S(1)}, u32[]{:S(2)}) copy-start(f32[768]{0:T(1024)S(1)} %reshape.1340) | copy-start | bytes 9220
  172.9 11.5 %copy-start.4 = (bf16[384,768]{0,1:T(8,128)(2,1)}, bf16[384,768]{0,1:T(8,128)(2,1)S(1)}, u32[]{:S(2)}) copy-start(bf16[384,768]{0,1:T(8,128)(2,1)S(1)} %reshape.1312) | copy-start | bytes 1769476
  181.0 3.5 copy-start.1
  183.4 1.1 copy-start.11
  183.4 1.1 copy-start.17
  184.5 14.9 %slice-start.2 = ((s8[4718592]{0:T(1024)(128)(4,1)}), s8[4194304]{0:T(1024)(128)(4,1)S(1)}, s32[]{:S(2)}) async-start(s8[4718592]{0:T(1024)(128)(4,1)} %bitcast.297), calls=%async_computation.7 | async-start | bytes 8388608
  185.6 13.8 %slice-start.3 = ((s8[4718592]{0:T(1024)(128)(4,1)}), s8[524288]{0:T(1024)(128)(4,1)S(1)}, s32[]{:S(2)}) async-start(s8[4718592]{0:T(1024)(128)(4,1)} %bitcast.297), calls=%async_computation.8 | async-start | bytes 1048576
  185.6 13.8 %copy-start.16 = (f32[768]{0:T(1024)S(1)}, f32[768]{0:T(1024)}, u32[]{:S(2)}) copy-start(f32[768]{0:T(1024)} %reshape.1342) | copy-start | bytes 9220
  214.0 2.9 copy-start.15
  240.1 4.2 slice-start
  240.1 3.4 copy-start.5
  240.2 4.2 slice-start.1
  336.7 3.2 collective-permute-start.12
  339.3 3.9 copy-start.2
  343.1 1.2 copy-start.7
  346.4 2.2 copy-start.3
  346.5 43.3 %collective-permute-start.15 = (bf16[2,2,192,384]{3,2,1,0:T(8,128)(2,1)S(1)}, bf16[2,2,192,384]{3,2,1,0:T(8,128)(2,1)S(1)}, u32[]{:S(2)}, u32[]{:S(2)}) collective-permute-start(bf16[2,2,192,384]{3,2,1,0:T(8,128)(2,1)S(1)} %fusion.30), channel_id=1, source_target_pairs={{0,4},{1,5},{2,6},{3,7},{4,0},{5,1},{6,2},{7,3},{8,12},{9,13},{10,... | collective-permute-start | bytes 1769480 | tf_op jit(solution)/shard_map/ppermute | solution.py:28
  351.0 2.0 collective-permute-start.18
  351.3 40.2 %collective-permute-start.13 = (bf16[2,2,192,384]{3,2,0,1:T(8,128)(2,1)S(1)}, bf16[2,2,192,384]{3,2,0,1:T(8,128)(2,1)S(1)}, u32[]{:S(2)}, u32[]{:S(2)}) collective-permute-start(bf16[2,2,192,384]{3,2,0,1:T(8,128)(2,1)S(1)} %fusion.29), channel_id=1, source_target_pairs={{0,2},{1,3},{2,0},{3,1},{4,6},{5,7},{6,4},{7,5},{8,10},{9,11},{10,... | collective-permute-start | bytes 1769480 | tf_op jit(solution)/shard_map/ppermute | solution.py:28
  353.2 38.6 %collective-permute-start.19 = (bf16[2,2,56,576]{3,2,1,0:T(8,128)(2,1)S(1)}, bf16[2,2,56,576]{3,2,1,0:T(8,128)(2,1)S(1)}, u32[]{:S(2)}, u32[]{:S(2)}) collective-permute-start(bf16[2,2,56,576]{3,2,1,0:T(8,128)(2,1)S(1)} %fusion.41), channel_id=1, source_target_pairs={{0,8},{1,9},{2,10},{3,11},{4,12},{5,13},{6,14},{7,15},{8,0},{9,1},... | collective-permute-start | bytes 774152 | tf_op jit(solution)/shard_map/ppermute | solution.py:28
  390.1 8.4 %collective-permute-start.16 = (bf16[2,192,384]{2,1,0:T(8,128)(2,1)S(1)}, bf16[2,192,384]{2,1,0:T(8,128)(2,1)S(1)}, u32[]{:S(2)}, u32[]{:S(2)}) collective-permute-start(bf16[2,192,384]{2,1,0:T(8,128)(2,1)S(1)} %fusion.39), channel_id=1, source_target_pairs={{0,2},{1,3},{2,0},{3,1},{4,6},{5,7},{6,4},{7,5},{8,10},{9,11},{10,... | collective-permute-start | bytes 884744 | tf_op jit(solution)/shard_map/ppermute | solution.py:28
  391.8 8.1 %collective-permute-start.14 = (bf16[2,192,384]{2,1,0:T(8,128)(2,1)S(1)}, bf16[2,192,384]{2,1,0:T(8,128)(2,1)S(1)}, u32[]{:S(2)}, u32[]{:S(2)}) collective-permute-start(bf16[2,192,384]{2,1,0:T(8,128)(2,1)S(1)} %fusion.38), channel_id=1, source_target_pairs={{0,4},{1,5},{2,6},{3,7},{4,0},{5,1},{6,2},{7,3},{8,12},{9,13},{10,... | collective-permute-start | bytes 884744 | tf_op jit(solution)/shard_map/ppermute | solution.py:28
  392.0 9.2 %collective-permute-start.20 = (bf16[2,2,56,576]{3,2,1,0:T(8,128)(2,1)S(1)}, bf16[2,2,56,576]{3,2,1,0:T(8,128)(2,1)S(1)}, u32[]{:S(2)}, u32[]{:S(2)}) collective-permute-start(bf16[2,2,56,576]{3,2,1,0:T(8,128)(2,1)S(1)} %fusion.52), channel_id=1, source_target_pairs={{0,16},{16,0},{1,17},{17,1},{2,18},{18,2},{3,19},{19,3},{4,20},{20... | collective-permute-start | bytes 774152 | tf_op jit(solution)/shard_map/ppermute | solution.py:28
  400.7 14.7 %collective-permute-start.17 = (bf16[192,768]{1,0:T(8,128)(2,1)}, bf16[192,768]{1,0:T(8,128)(2,1)}, u32[]{:S(2)}, u32[]{:S(2)}) collective-permute-start(bf16[192,768]{1,0:T(8,128)(2,1)} %fusion.40), channel_id=1, source_target_pairs={{0,8},{1,9},{2,10},{3,11},{4,12},{5,13},{6,14},{7,15},{8,0},{9,1},... | collective-permute-start | bytes 884744 | tf_op jit(solution)/shard_map/ppermute | solution.py:28
  401.3 7.0 %collective-permute-start.23 = (bf16[56,576]{1,0:T(8,128)(2,1)S(1)}, bf16[56,576]{1,0:T(8,128)(2,1)S(1)}, u32[]{:S(2)}, u32[]{:S(2)}) collective-permute-start(bf16[56,576]{1,0:T(8,128)(2,1)S(1)} %get-tuple-element.85), channel_id=1, source_target_pairs={{0,6},{1,7},{2,4},{3,5},{4,2},{5,3},{6,0},{7,1},{8,14},{9,15},{10,... | collective-permute-start | bytes 193544 | tf_op jit(solution)/shard_map/ppermute | solution.py:28
  403.4 5.7 %collective-permute-start.22 = (bf16[56,576]{1,0:T(8,128)(2,1)S(1)}, bf16[56,576]{1,0:T(8,128)(2,1)S(1)}, u32[]{:S(2)}, u32[]{:S(2)}) collective-permute-start(bf16[56,576]{1,0:T(8,128)(2,1)S(1)} %get-tuple-element.86), channel_id=1, source_target_pairs={{0,4},{1,5},{2,6},{3,7},{4,0},{5,1},{6,2},{7,3},{8,12},{9,13},{10,... | collective-permute-start | bytes 193544 | tf_op jit(solution)/shard_map/ppermute | solution.py:28
  403.8 5.4 %collective-permute-start.21 = (bf16[56,576]{1,0:T(8,128)(2,1)S(1)}, bf16[56,576]{1,0:T(8,128)(2,1)S(1)}, u32[]{:S(2)}, u32[]{:S(2)}) collective-permute-start(bf16[56,576]{1,0:T(8,128)(2,1)S(1)} %get-tuple-element.87), channel_id=1, source_target_pairs={{0,2},{1,3},{2,0},{3,1},{4,6},{5,7},{6,4},{7,5},{8,10},{9,11},{10,... | collective-permute-start | bytes 193544 | tf_op jit(solution)/shard_map/ppermute | solution.py:28
  411.3 14.7 %copy-start.9 = (bf16[1,440,768]{2,1,0:T(8,128)(2,1)S(1)}, bf16[1,440,768]{2,1,0:T(8,128)(2,1)}, u32[]{:S(2)}) copy-start(bf16[1,440,768]{2,1,0:T(8,128)(2,1)} %reduce-scatter.2.cloned.1.call-done) | copy-start | bytes 2027524
  411.3 14.7 %collective-permute-start.24 = (bf16[440,768]{1,0:T(8,128)(2,1)}, bf16[440,768]{1,0:T(8,128)(2,1)S(1)}, u32[]{:S(2)}, u32[]{:S(2)}) collective-permute-start(bf16[440,768]{1,0:T(8,128)(2,1)} %bitcast.324), channel_id=1, source_target_pairs={{0,16},{16,0},{1,17},{17,1},{2,18},{18,2},{3,19},{19,3},{4,20},{20... | collective-permute-start | bytes 2027528 | tf_op jit(solution)/shard_map/ppermute | solution.py:28
  (3 other events, 2.9 us)
Sparse Core Ops, SparseCore 0:
  13.0 109.7 all-gather.2
  255.9 134.2 reduce-scatter.1

commit v3 on v2

--- a/solution.py
+++ b/solution.py
@@ -167,6 +167,42 @@
     )(q,kv,kb,cf,st,dc)
 
 
+def weight_grads_body(y_ref, dz_ref, a_ref, do_ref, ctx_ref, da_ref, vec_ref, out_ref, *, chips):
+    width = y_ref.shape[1]
+    r_in, r_ctx = width // chips, ctx_ref.shape[1] // chips
+    r_out = a_ref.shape[1] // chips
+    for j in range(2):
+        grad = t_dot(y_ref[...], dz_ref[:, j * width : (j + 1) * width]).astype(BF16)
+        for q in range(chips):
+            out_ref[q, j * r_in : (j + 1) * r_in] = grad[q * r_in : (q + 1) * r_in]
+        grad = t_dot(a_ref[:, j * width : (j + 1) * width], do_ref[...]).astype(BF16)
+        half = chips // 2
+        for q in range(half):
+            out_ref[j * half + q, 2 * r_in : 2 * r_in + r_out] = grad[q * r_out : (q + 1) * r_out]
+    first = 2 * r_in + r_out
+    grad = t_dot(ctx_ref[...], da_ref[...]).astype(BF16)
+    for q in range(chips):
+        out_ref[q, first : first + r_ctx] = grad[q * r_ctx : (q + 1) * r_ctx]
+    own = vec_ref.shape[0]
+    n = da_ref.shape[0] // 2
+    ones = jnp.ones((16, y_ref.shape[0]), BF16)
+    sums = [dot(ones[:, :n], da_ref[:n])[:1], dot(ones[:, :n], do_ref[:n])[:1]]
+    sums += [dot(ones, dz_ref[:, j * width : (j + 1) * width])[:1] for j in range(2)]
+    small = jnp.concatenate([vec_ref[...]] + sums, axis=0).astype(BF16)
+    for q in range(chips):
+        out_ref[q, first + r_ctx : first + r_ctx + own + 4] = small
+
+
+def weight_grads(y, dz, a, do, ctx, da, vec, chips):
+    width = y.shape[1]
+    total = 2 * width // chips + a.shape[1] // chips + ctx.shape[1] // chips + vec.shape[0] + 4
+    return pl.pallas_call(
+        partial(weight_grads_body, chips=chips),
+        out_shape=jax.ShapeDtypeStruct((chips, total, width), BF16),
+        name="weight_grads",
+    )(y, dz, a, do, ctx, da, vec)
+
+
 def per_device(
     seq_size,
     grp_size,
@@ -208,15 +244,31 @@
     def sflip(value, mask):
         return flip(value, "seq", seq_size, mask)
 
+    core = me % 2
+    chips = seq_size // 2
+    piece = feed // seq_size
+    n_dev = grp_size * seq_size
+    half_feed = feed // 2
+    split = inner_weight.reshape(shard, chips, 2, piece)
+    split = [split[:, :, i].reshape(shard, 2, width).transpose(1, 0, 2).reshape(2 * shard, width) for i in range(2)]
+    near = jnp.concatenate([pick(split, 1 - core), output_weight], axis=0)
+    far = sflip(near, 1)
+    outer_far = lax.ppermute(
+        outer_weight,
+        ("grp", "seq"),
+        [(d, d ^ (1 | grp_size) if d % 2 != (d // grp_size) % 2 else d) for d in range(n_dev)],
+    )
+    inner_pair = in_order(pick(split, core).reshape(2, shard, width), far[: 2 * shard].reshape(2, shard, width), core)
     packed = jnp.concatenate(
         [
-            jnp.concatenate([inner_weight[:, i * width : (i + 1) * width] for i in range(feed // width)], axis=0),
-            outer_weight,
-            output_weight,
+            inner_pair.transpose(1, 0, 2, 3).reshape(4 * shard, width),
+            outer_far,
+            in_order(output_weight, far[2 * shard :], core).reshape(2 * shard, width),
         ],
         axis=0,
     )
-    gathered = lax.all_gather(packed, ("grp", "seq"), axis=0, tiled=False)
+    same_core = [[2 * d + i for d in range(n_dev // 2)] for i in range(2)]
+    gathered = lax.all_gather(packed, ("grp", "seq"), axis=0, tiled=False, axis_index_groups=same_core)
 
     x_mine = pick(tokens, z1)
     x_sent = pick(tokens, 1 - z1)
@@ -305,75 +357,71 @@
     context = exchange(context.reshape(8, rows, GROUP_WIDTH))
     context = context.reshape(2, HEAD_GROUPS, rows, GROUP_WIDTH).transpose(0, 2, 1, 3).reshape(2 * rows, width)
 
-    n_dev = grp_size * seq_size
-    inner_rows = shard * (feed // width)
-    inner_all = gathered[:, :inner_rows].reshape(n_dev, feed // width, shard, width)
-    inner_all = inner_all.transpose(0, 2, 1, 3).reshape(width, feed)
-    outer_all = gathered[:, inner_rows : inner_rows + outer_weight.shape[0]].reshape(feed, width)
-    output_all = gathered[:, inner_rows + outer_weight.shape[0] :].reshape(width, width)
+    inner_lo = gathered[:, : 2 * shard].reshape(width, width)
+    inner_hi = gathered[:, 2 * shard : 4 * shard].reshape(width, width)
+    outer_end = 4 * shard + outer_weight.shape[0]
+    outer_all = gathered[:, 4 * shard : outer_end].reshape(-1, 2, grp_size // 2, outer_weight.shape[0], width)
+    outer_all = outer_all.transpose(0, 2, 1, 3, 4).reshape(half_feed, width)
+    output_all = gathered[:, outer_end:].reshape(width, width)
+    outer_lo, outer_hi = outer_all[:width], outer_all[width:]
+    in_bias = pick(in_bias.reshape(chips, 2, piece).transpose(1, 0, 2).reshape(2, half_feed), core)
 
     home = tokens.reshape(2 * rows, width)
     cotangent = grad_out.reshape(2 * rows, width)
     hidden_one = home.astype(jnp.float32) + dot(context, output_all) + o_bias
     norm_one, norm_back_one = jax.vjp(layer_norm, hidden_one, gain1, shift1)
     first_out = norm_one.astype(bf16)
-    inner_pre = dot(first_out, inner_all) + in_bias
-    active_full, gelu_back = jax.vjp(partial(jax.nn.gelu, approximate=False), inner_pre)
-    active = active_full.astype(bf16)
-    hidden_two = first_out.astype(jnp.float32) + dot(active, outer_all) + out_bias
+    n_own = 2 * rows
+    both_first = jnp.concatenate([first_out, sflip(first_out, 1)], axis=0)
+
+    def gelu_pair(pre):
+        full, back = jax.vjp(partial(jax.nn.gelu, approximate=False), pre)
+        return full.astype(bf16), back(jnp.ones_like(pre))[0]
+
+    inner_all = jnp.concatenate([inner_lo, inner_hi], axis=1)
+    active, slope = gelu_pair(dot(both_first, inner_all) + in_bias)
+    outer_part = dot(active, outer_all)
+    outer_sum = outer_part[:n_own] + sflip(outer_part[n_own:].astype(bf16), 1).astype(jnp.float32)
+    hidden_two = first_out.astype(jnp.float32) + outer_sum + out_bias
     layer_out, norm_back_two = jax.vjp(layer_norm, hidden_two, gain2, shift2)
     dhidden_two, dsecond_gain, dsecond_shift = norm_back_two(cotangent.astype(jnp.float32))
     douter = dhidden_two.astype(bf16)
-    douter_weight = t_dot(active, douter)
-    dinner = gelu_back(dot_t(douter, outer_all))[0].astype(bf16)
-    dinner_weight = t_dot(first_out, dinner)
-    dfirst = dhidden_two + dot_t(dinner, inner_all)
+    both_douter = jnp.concatenate([douter, sflip(douter, 1)], axis=0)
+    dinner = (dot_t(both_douter, outer_all) * slope).astype(bf16)
+    dfirst_part = dot_t(dinner, inner_all)
+    dfirst = dhidden_two + dfirst_part[:n_own] + sflip(dfirst_part[n_own:].astype(bf16), 1).astype(jnp.float32)
     dhidden_one, dfirst_gain, dfirst_shift = norm_back_one(dfirst)
     dattend = dhidden_one.astype(bf16)
-    doutput_weight = t_dot(context, dattend)
     dcontext = dot_t(dattend, output_all).astype(bf16)
     dcontext = dcontext.reshape(2, rows, HEAD_GROUPS, GROUP_WIDTH).transpose(0, 2, 1, 3)
     dcontext = exchange(dcontext.reshape(8, rows, GROUP_WIDTH)).reshape(8 * rows, GROUP_WIDTH)
 
     out_rows = width // seq_size
-    small_grads = [
-        column_sums(dattend),
-        dfirst_gain,
-        dfirst_shift,
-        column_sums(douter),
-        dsecond_gain,
-        dsecond_shift,
-    ]
-    small_grads = jnp.concatenate(
-        [g.reshape(seq_size, out_rows) for g in small_grads] + [column_sums(dinner).reshape(seq_size, -1)], axis=1
-    )
-    n_small = small_grads.shape[1]
-    small_grads = jnp.pad(small_grads, ((0, 0), (0, 8 * width - n_small))).reshape(seq_size, 8, width)
-    dinner_blocks = dinner_weight.reshape(seq_size, out_rows, feed // width, width).transpose(0, 2, 1, 3)
-    grads = jnp.concatenate(
-        [
-            dinner_blocks.reshape(seq_size, -1, width).astype(bf16),
-            douter_weight.reshape(seq_size, -1, width).astype(bf16),
-            doutput_weight.reshape(seq_size, -1, width).astype(bf16),
-            small_grads.astype(bf16),
-        ],
-        axis=1,
-    )
-    grads = lax.psum_scatter(grads, "seq", scatter_dimension=0, tiled=False)
+    ctx_split = context.reshape(n_own, chips, 2, out_rows)
+    ctx_split = [ctx_split[:, :, i].reshape(n_own, width // 2) for i in range(2)]
+    both_ctx = jnp.concatenate([pick(ctx_split, core), sflip(pick(ctx_split, 1 - core), 1)], axis=0)
+    both_dattend = jnp.concatenate([dattend, sflip(dattend, 1)], axis=0)
+    vectors = jnp.stack([dfirst_gain, dfirst_shift, dsecond_gain, dsecond_shift])
+    grads = weight_grads(both_first, dinner, active, both_douter, both_ctx, both_dattend, vectors, chips)
+    chip_groups = [[2 * q + i for q in range(chips)] for i in range(2)]
+    grads = lax.psum_scatter(grads, "seq", scatter_dimension=0, tiled=False, axis_index_groups=chip_groups)
     for b in range(log2_of(grp_size)):
         grads = (grads.astype(jnp.float32) + flip(grads, "grp", grp_size, 1 << b).astype(jnp.float32)).astype(bf16)
-    grads = grads.astype(jnp.float32)
-    r1 = out_rows * (feed // width)
-    r2 = r1 + feed // seq_size
+    r1 = 4 * out_rows
+    r2 = r1 + piece
     r3 = r2 + out_rows
-    dinner_weight = grads[:r1].reshape(feed // width, out_rows, width).transpose(1, 0, 2).reshape(out_rows, feed)
-    douter_weight = grads[r1:r2]
-    doutput_weight = grads[r2:r3]
-    small = grads[r3:].reshape(-1)[:n_small]
-    doutput_bias, dfirst_gain, dfirst_shift, douter_bias, dsecond_gain, dsecond_shift = (
-        small[i * out_rows : (i + 1) * out_rows] for i in range(6)
-    )
-    dinner_bias = small[6 * out_rows :]
+    inner_grad = grads[:r1].reshape(2, 2, out_rows, width)
+    inner_grad = [inner_grad[:, i] for i in range(2)]
+    far = sflip(jnp.concatenate([pick(inner_grad, 1 - core).reshape(2 * out_rows, width), grads[r3:]], axis=0), 1)
+    dinner_weight = in_order(pick(inner_grad, core), far[: 2 * out_rows].reshape(2, out_rows, width), core)
+    dinner_weight = dinner_weight.transpose(2, 0, 1, 3).reshape(out_rows, 2, chips, piece).transpose(0, 2, 1, 3)
+    dinner_weight = dinner_weight.reshape(out_rows, feed).astype(jnp.float32)
+    douter_weight = grads[r1:r2].astype(jnp.float32)
+    doutput_weight = grads[r2:r3].astype(jnp.float32)
+    small = grads[r3:].astype(jnp.float32)
+    both = lax.dynamic_slice_in_dim(small + far[2 * out_rows :].astype(jnp.float32), me * out_rows, out_rows, axis=1)
+    dfirst_gain, dfirst_shift, dsecond_gain, dsecond_shift, doutput_bias, douter_bias = (both[i] for i in range(6))
+    dinner_bias = lax.dynamic_slice_in_dim(small[6:8].reshape(half_feed), (me // 2) * piece, piece)
 
     dqueries, dkv = attend_backward(queries, kv, key_tail, context_full, stats, dcontext)
     dkv = dkv.reshape(n_parts, 8 * rows, 2 * GROUP_WIDTH)

time: 445 us -> 431 us (0.969)
  local copies, waits for them, and re-layouts: 73.7 us -> 35.8 us
  blocking collectives: 23.6 us -> 43.3 us
  starting transfers between devices: 29 us -> 46.1 us
  waiting for transfers between devices: 135 us -> 120 us
  matrix products: 43.9 us -> 29.9 us
  Pallas kernels: 75 us -> 85.5 us
    all_to_all x1, blocking collectives: 23.6 us -> 43.3 us  [exchange(): lax.all_to_all(blocks, 'seq', 0, 0, axis_index_groups=teams, tiled=True)]
    ppermute x25 -> x33, waiting for transfers between devices: 118 us -> 99.6 us  [flip(): return lax.ppermute(value, axis, [(i, i ^ mask) for i in range(size)])]
    ppermute x25 -> x33, starting transfers between devices: 22.1 us -> 38.6 us  [flip(): return lax.ppermute(value, axis, [(i, i ^ mask) for i in range(size)])]
    convert_element_type x3, local copies, waits for them, and re-layouts: 14.2 us -> 2.58 us  [per_device(): dinner_weight = dinner_weight.reshape(out_rows, feed).astype(jnp.float32)]
    pallas_call x0 -> x1, Pallas kernels: none -> 10.7 us  [weight_grads(): pl.pallas_call(partial(weight_grads_body, chips=chips), out_shape=jax.Sha...]
    dot_general x4 -> x1, matrix products: 11.8 us -> 2.07 us  [t_dot(): lax.dot_general(left, right, (((0,), (0,)), ((), ())), preferred_element_...]
    reshape x9 -> x6, local copies, waits for them, and re-layouts: 7.69 us -> 1.2 us  [the longest x1 1.17 us: per_device(): split = inner_weight.reshape(shard, chips, 2, piece)]
    concatenate x1, local copies, waits for them, and re-layouts: 6.11 us -> 0.1 us  [per_device(): jnp.concatenate([query_bias, value_bias, output_bias, first_gain, first_s...]
  transfers between devices with their start and end apart: 28 -> 37, of which waited for: 16 -> 20; matrix products, arithmetic and copies ran while one was open for 15% -> 15% of each run, Pallas kernels for 17% -> 18%
where the time goes in v3:
time: 431 us; the launch traced here: 422 us
  waiting for transfers between devices  120 us (28%)
  Pallas kernels  85.5 us (20%)
  starting transfers between devices  46.1 us (11%)
  other arithmetic  44.2 us (10%)
  blocking collectives  43.3 us (10%)
  local copies, waits for them, and re-layouts  35.8 us (8%)
  matrix products  29.9 us (7%)
  between operations  17.3 us (4%)
    ppermute x33, waiting for transfers between devices, flip(): return lax.ppermute(value, axis, [(i, i ^ mask) for i in range(size)])  99.6 us
    pallas_call x1, Pallas kernels, attend_backward(): pl.pallas_call(partial(bwd_body, bk=bk, nk=nk), grid=(nk, NH), in_specs=[...  46.5 us
    all_to_all x1, blocking collectives, exchange(): lax.all_to_all(blocks, 'seq', 0, 0, axis_index_groups=teams, tiled=True)  43.3 us
    ppermute x33, starting transfers between devices, flip(): return lax.ppermute(value, axis, [(i, i ^ mask) for i in range(size)])  38.6 us
    pallas_call x1, Pallas kernels, attend_forward(): pl.pallas_call(partial(fwd_body, bq=bq), grid=(n // bq, NH), in_specs=[pl...  28.3 us
    all_to_all x1, waiting for transfers between devices, exchange(): lax.all_to_all(blocks, 'seq', 0, 0, axis_index_groups=teams, tiled=True)  20.2 us
    dot_general x4, matrix products, dot(): return jnp.dot(left, right, preferred_element_type=jnp.float32)  19.4 us
    pallas_call x1, Pallas kernels, weight_grads(): pl.pallas_call(partial(weight_grads_body, chips=chips), out_shape=jax.Sha...  10.7 us
  transfers between devices with their start and end apart: 37, of which 20 were waited for; matrix products, arithmetic and copies ran while one was open for 15% of the time, Pallas kernels for 18%

profile of v3, /device:TPU:0, one launch (start us, length us, event | category | flops | bytes accessed | tf_op | source)
XLA Modules:
  0.0 421.9 jit_solution(7238915244844063930)
XLA Ops:
  13.4 7.7 %collective-permute-start.5 = (bf16[32,576]{1,0:T(8,128)(2,1)S(1)}, bf16[32,576]{1,0:T(8,128)(2,1)S(1)}, u32[]{:S(2)}, u32[]{:S(2)}) collective-permute-start(bf16[32,576]{1,0:T(8,128)(2,1)S(1)} %get-tuple-element.101), channel_id=1, source_target_pairs={{0,2},{1,3},{2,0},{3,1},{4,6},{5,7},{6,4},{7,5},{8,10},{9,11},{10,... | collective-permute-start | bytes 110600 | tf_op jit(solution)/shard_map/ppermute | solution.py:28
  21.1 1.6 collective-permute-start.6
  22.8 2.7 collective-permute-start
  28.1 2.7 collective-permute-start.8
  31.0 22.9 %collective-permute-done.8 = bf16[2,2,32,576]{3,2,1,0:T(8,128)(2,1)S(1)} collective-permute-done((bf16[2,2,32,576]{3,2,1,0:T(8,128)(2,1)S(1)}, bf16[2,2,32,576]{3,2,1,0:T(8,128)(2,1)S(1)}, u32[]{:S(2)}, u32[]{:S(2)}) %collective-permute-start.8) | collective-permute-done | bytes 147488 | tf_op jit(solution)/shard_map/ppermute | solution.py:28
  54.0 1.6 collective-permute-start.9
  57.3 8.4 %collective-permute-done.9 = bf16[2,2,2,32,576]{4,3,2,1,0:T(8,128)(2,1)S(1)} collective-permute-done((bf16[2,2,2,32,576]{4,3,2,1,0:T(8,128)(2,1)S(1)}, bf16[2,2,2,32,576]{4,3,2,1,0:T(8,128)(2,1)S(1)}, u32[]{:S(2)}, u32[]{:S(2)}) %collective-permute-start.9) | collective-permute-done | bytes 294944 | tf_op jit(solution)/shard_map/ppermute | solution.py:28
  69.5 2.7 collective-permute-done.3
  73.1 4.6 %collective-permute-start.4 = (bf16[2,2,192,384]{3,2,1,0:T(8,128)(2,1)}, bf16[2,2,192,384]{3,2,1,0:T(8,128)(2,1)}, u32[]{:S(2)}, u32[]{:S(2)}) collective-permute-start(bf16[2,2,192,384]{3,2,1,0:T(8,128)(2,1)} %maximum_select_fusion.10), channel_id=1, source_target_pairs={{0,2},{1,3},{2,0},{3,1},{4,6},{5,7},{6,4},{7,5},{8,10},{9,11},{10,... | collective-permute-start | bytes 1769480 | tf_op jit(solution)/shard_map/ppermute | solution.py:28
  79.4 13.0 %collective-permute-done.2 = bf16[2,2,192,384]{3,2,1,0:T(8,128)(2,1)S(1)} collective-permute-done((bf16[2,2,192,384]{3,2,1,0:T(8,128)(2,1)}, bf16[2,2,192,384]{3,2,1,0:T(8,128)(2,1)S(1)}, u32[]{:S(2)}, u32[]{:S(2)}) %collective-permute-start.2) | collective-permute-done | bytes 589856 | tf_op jit(solution)/shard_map/ppermute | solution.py:28
  94.5 2.0 convolution_add_fusion
  99.9 1.8 maximum_select_fusion
  101.7 28.3 %attend_forward.1 = (bf16[1536,192]{1,0:T(8,128)(2,1)}, f32[1536,192]{1,0:T(8,128)}, f32[1536,128]{1,0:T(8,128)}) custom-call(bf16[1536,192]{1,0:T(8,128)(2,1)} %fusion.9.q_ref, bf16[3072,384]{1,0:T(8,128)(2,1)} %bitcast.298, bf16[3072,128]{1,0:T(8,128)(2,1)} %select_convert_fusion.1.kb_ref), custom_call_target="tpu_custom_call" | custom-call | tf_op jit(solution)/shard_map/attend_forward/pallas_call | solution.py:103
  130.0 6.8 %all-to-all-start = ((bf16[8,192,192]{2,1,0:T(8,128)(2,1)}), bf16[8,192,192]{2,1,0:T(8,128)(2,1)S(1)}, u32[]{:S(2)}, u32[]{:S(2)}) async-start(bf16[8,192,192]{2,1,0:T(8,128)(2,1)} %bitcast.344), calls=%async_computation | async-start | bytes 1572864 | tf_op jit(solution)/shard_map/all_to_all | solution.py:355
  137.1 20.2 %all-to-all-done = bf16[8,192,192]{2,1,0:T(8,128)(2,1)S(1)} async-done(((bf16[8,192,192]{2,1,0:T(8,128)(2,1)}), bf16[8,192,192]{2,1,0:T(8,128)(2,1)S(1)}, u32[]{:S(2)}, u32[]{:S(2)}) %all-to-all-start) | async-done | bytes 589856 | tf_op jit(solution)/shard_map/all_to_all | solution.py:355
  158.6 3.7 fusion.79
  164.4 2.0 slice.346
  166.7 14.7 %multiply_convert_fusion.1 = (bf16[768,1536]{1,0:T(8,128)(2,1)S(1)}, f32[768,1536]{1,0:T(8,128)}, f32[768,1536]{1,0:T(8,128)}) fusion(f32[1536]{0:T(1024)S(1)} %select_n.746, bf16[768,768]{1,0:T(8,128)(2,1)S(1)} %bitcast.330, bf16[768,768]{1,0:T(8,128)(2,1)S(1)} %bitcast.332, bf16[384,768]{1,0:T(8,128)(2,1)S(1)} %collective-permute-done.14, ...), kind=kOutput, calls=%fused_computation.3 | convolution fusion | flops 1896873984 | bytes 15341568 | tf_op jit(solution)/shard_map/dot_general | solution.py:46
  181.5 2.0 fusion.87
  187.0 1.9 fusion.76
  192.5 1.6 collective-permute-done.16
  194.2 3.7 multiply_convert_fusion.dz_ref
  198.0 2.0 fusion.10
  202.0 1.9 copy.144
  203.9 2.4 reshape_reshape.3
  207.1 1.8 copy.145
  209.1 2.2 multiply_reduce_fusion
  213.2 1.9 pad_maximum_fusion.10.ctx_ref
  215.1 2.2 pad_maximum_fusion.6.y_ref
  219.0 2.2 pad_maximum_fusion.8.da_ref
  221.2 10.7 %weight_grads.1 = bf16[8,440,768]{2,1,0:T(8,128)(2,1)} custom-call(bf16[768,768]{1,0:T(8,128)(2,1)} %pad_maximum_fusion.6.y_ref, bf16[768,1536]{1,0:T(8,128)(2,1)} %copy-done.6, bf16[768,1536]{1,0:T(8,128)(2,1)} %copy-done.5, bf16[768,768]{1,0:T(8,128)(2,1)} %pad_maximum_fusion.7.do_ref, bf16[768,384]{1,0:T(8,128)(2,1)} %pad_maximum_fusion.10.ctx_ref, ...), custom_call_target="tpu_custom_call" | custom-call | tf_op jit(solution)/shard_map/weight_grads/pallas_call | solution.py:199
  234.5 43.3 %all_to_all.10 = bf16[8,192,192]{2,1,0:T(8,128)(2,1)} all-to-all(bf16[8,192,192]{2,1,0:T(8,128)(2,1)S(1)} %bitcast.316), channel_id=1, replica_groups={{0,2,4,6,8,10,12,14},{1,3,5,7,9,11,13,15},{16,18,20,22,24,26,28,30},{17..., dimensions={0} | all-to-all | bytes 1179648 | tf_op jit(solution)/shard_map/all_to_all | solution.py:355
  277.8 46.5 %attend_backward.1 = (bf16[1536,192]{1,0:T(8,128)(2,1)}, f32[3072,384]{1,0:T(8,128)}) custom-call(bf16[1536,192]{1,0:T(8,128)(2,1)} %fusion.9.q_ref, bf16[3072,384]{1,0:T(8,128)(2,1)} %bitcast.299, bf16[3072,128]{1,0:T(8,128)(2,1)} %select_convert_fusion.1.kb_ref, f32[1536,192]{1,0:T(8,128)} %get-tuple-element.35.cf_ref, ...), custom_call_target="tpu_custom_call" | custom-call | tf_op jit(solution)/shard_map/attend_backward/pallas_call | solution.py:159
  324.3 4.3 %fusion.14 = bf16[1,1536,384]{2,1,0:T(8,128)(2,1)} fusion(f32[3072,384]{1,0:T(8,128)} %get-tuple-element.38, pred[]{:T(512)S(6)} %eq.39), kind=kLoop, calls=%fused_computation.43 | loop fusion | flops 589824 | bytes 3538945 | tf_op jit(solution)/shard_map/convert_element_type | solution.py:432
  328.5 2.7 copy.133
  331.7 3.2 fusion.15
  335.9 2.1 fusion.7
  339.5 2.0 fusion.88
  342.1 1.7 collective-permute-start.19
  345.2 23.3 %collective-permute-done.21 = bf16[2,2,192,384]{3,2,1,0:T(8,128)(2,1)S(1)} collective-permute-done((bf16[2,2,192,384]{3,2,1,0:T(8,128)(2,1)S(1)}, bf16[2,2,192,384]{3,2,1,0:T(8,128)(2,1)S(1)}, u32[]{:S(2)}, u32[]{:S(2)}) %collective-permute-start.21) | collective-permute-done | bytes 589856 | tf_op jit(solution)/shard_map/ppermute | solution.py:28
  368.7 1.5 collective-permute-start.22
  370.7 1.5 collective-permute-start.26
  372.2 5.6 %collective-permute-done.22 = bf16[2,192,384]{2,1,0:T(8,128)(2,1)S(1)} collective-permute-done((bf16[2,192,384]{2,1,0:T(8,128)(2,1)S(1)}, bf16[2,192,384]{2,1,0:T(8,128)(2,1)S(1)}, u32[]{:S(2)}, u32[]{:S(2)}) %collective-permute-start.22) | collective-permute-done | bytes 294944 | tf_op jit(solution)/shard_map/ppermute | solution.py:28
  381.4 1.8 collective-permute-start.29
  385.1 4.2 %collective-permute-done.29 = bf16[56,576]{1,0:T(8,128)(2,1)S(1)} collective-permute-done((bf16[56,576]{1,0:T(8,128)(2,1)S(1)}, bf16[56,576]{1,0:T(8,128)(2,1)S(1)}, u32[]{:S(2)}, u32[]{:S(2)}) %collective-permute-start.29) | collective-permute-done | bytes 64544 | tf_op jit(solution)/shard_map/ppermute | solution.py:28
  392.3 1.7 collective-permute-start.32
  397.5 10.5 %collective-permute-done.32 = bf16[440,768]{1,0:T(8,128)(2,1)S(1)} collective-permute-done((bf16[440,768]{1,0:T(8,128)(2,1)}, bf16[440,768]{1,0:T(8,128)(2,1)S(1)}, u32[]{:S(2)}, u32[]{:S(2)}) %collective-permute-start.32) | collective-permute-done | bytes 675872 | tf_op jit(solution)/shard_map/ppermute | solution.py:28
  413.0 1.6 reshape.1374
  (315 shorter events, 63.0 us)
Async XLA Ops:
  7.2 151.4 %all-gather.3.cloned.1.call-start = ((), (), s32[]{:S(2)}) async-start(), calls=%async_computation.4 | async-start | bytes 6266880 | tf_op jit(solution)/shard_map/all_gather | solution.py:271
  9.1 1.5 collective-permute-start.12
  9.7 1.3 collective-permute-start.13
  11.0 11.7 %copy-start.25 = (bf16[2,192,768]{2,1,0:T(8,128)(2,1)S(1)}, bf16[2,192,768]{2,1,0:T(8,128)(2,1)}, u32[]{:S(2)}) copy-start(bf16[2,192,768]{2,1,0:T(8,128)(2,1)} %param.20) | copy-start | bytes 1769476
  12.1 13.4 %copy-start.34 = (s32[2]{0:T(128)S(1)}, s32[2]{0:T(128)}, u32[]{:S(2)}) copy-start(s32[2]{0:T(128)} %param.21) | copy-start | bytes 28
  13.4 14.6 %collective-permute-start.5 = (bf16[32,576]{1,0:T(8,128)(2,1)S(1)}, bf16[32,576]{1,0:T(8,128)(2,1)S(1)}, u32[]{:S(2)}, u32[]{:S(2)}) collective-permute-start(bf16[32,576]{1,0:T(8,128)(2,1)S(1)} %get-tuple-element.101), channel_id=1, source_target_pairs={{0,2},{1,3},{2,0},{3,1},{4,6},{5,7},{6,4},{7,5},{8,10},{9,11},{10,... | collective-permute-start | bytes 110600 | tf_op jit(solution)/shard_map/ppermute | solution.py:28
  21.1 6.5 %collective-permute-start.6 = (bf16[32,576]{1,0:T(8,128)(2,1)S(1)}, bf16[32,576]{1,0:T(8,128)(2,1)S(1)}, u32[]{:S(2)}, u32[]{:S(2)}) collective-permute-start(bf16[32,576]{1,0:T(8,128)(2,1)S(1)} %get-tuple-element.102), channel_id=1, source_target_pairs={{0,4},{1,5},{2,6},{3,7},{4,0},{5,1},{6,2},{7,3},{8,12},{9,13},{10,... | collective-permute-start | bytes 110600 | tf_op jit(solution)/shard_map/ppermute | solution.py:28
  22.7 5.3 %collective-permute-start.7 = (bf16[32,576]{1,0:T(8,128)(2,1)S(1)}, bf16[32,576]{1,0:T(8,128)(2,1)S(1)}, u32[]{:S(2)}, u32[]{:S(2)}) collective-permute-start(bf16[32,576]{1,0:T(8,128)(2,1)S(1)} %get-tuple-element.103), channel_id=1, source_target_pairs={{0,6},{1,7},{2,4},{3,5},{4,2},{5,3},{6,0},{7,1},{8,14},{9,15},{10,... | collective-permute-start | bytes 110600 | tf_op jit(solution)/shard_map/ppermute | solution.py:28
  22.8 32.9 %collective-permute-start = (bf16[192,768]{1,0:T(8,128)(2,1)S(1)}, bf16[192,768]{1,0:T(8,128)(2,1)S(1)}, u32[]{:S(2)}, u32[]{:S(2)}) collective-permute-start(bf16[192,768]{1,0:T(8,128)(2,1)S(1)} %get-tuple-element.74), channel_id=1, source_target_pairs={{0,8},{1,9},{2,10},{3,11},{4,12},{5,13},{6,14},{7,15},{8,0},{9,1},... | collective-permute-start | bytes 884744 | tf_op jit(solution)/shard_map/ppermute | solution.py:28
  28.1 25.8 %collective-permute-start.8 = (bf16[2,2,32,576]{3,2,1,0:T(8,128)(2,1)S(1)}, bf16[2,2,32,576]{3,2,1,0:T(8,128)(2,1)S(1)}, u32[]{:S(2)}, u32[]{:S(2)}) collective-permute-start(bf16[2,2,32,576]{3,2,1,0:T(8,128)(2,1)S(1)} %maximum_select_fusion.15), channel_id=1, source_target_pairs={{0,8},{1,9},{2,10},{3,11},{4,12},{5,13},{6,14},{7,15},{8,0},{9,1},... | collective-permute-start | bytes 442376 | tf_op jit(solution)/shard_map/ppermute | solution.py:28
  54.0 11.8 %collective-permute-start.9 = (bf16[2,2,2,32,576]{4,3,2,1,0:T(8,128)(2,1)S(1)}, bf16[2,2,2,32,576]{4,3,2,1,0:T(8,128)(2,1)S(1)}, u32[]{:S(2)}, u32[]{:S(2)}) collective-permute-start(bf16[2,2,2,32,576]{4,3,2,1,0:T(8,128)(2,1)S(1)} %maximum_select_fusion.12), channel_id=1, source_target_pairs={{0,16},{16,0},{1,17},{17,1},{2,18},{18,2},{3,19},{19,3},{4,20},{20... | collective-permute-start | bytes 884744 | tf_op jit(solution)/shard_map/ppermute | solution.py:28
  56.0 11.5 %collective-permute-start.1 = (bf16[2,192,384]{2,1,0:T(8,128)(2,1)S(1)}, bf16[2,192,384]{2,1,0:T(8,128)(2,1)S(1)}, u32[]{:S(2)}, u32[]{:S(2)}) collective-permute-start(bf16[2,192,384]{2,1,0:T(8,128)(2,1)S(1)} %get-tuple-element.72), channel_id=1, source_target_pairs={{0,2},{1,3},{2,0},{3,1},{4,6},{5,7},{6,4},{7,5},{8,10},{9,11},{10,... | collective-permute-start | bytes 884744 | tf_op jit(solution)/shard_map/ppermute | solution.py:28
  56.5 15.7 %collective-permute-start.3 = (bf16[2,192,384]{2,1,0:T(8,128)(2,1)S(1)}, bf16[2,192,384]{2,1,0:T(8,128)(2,1)S(1)}, u32[]{:S(2)}, u32[]{:S(2)}) collective-permute-start(bf16[2,192,384]{2,1,0:T(8,128)(2,1)S(1)} %get-tuple-element.71), channel_id=1, source_target_pairs={{0,4},{1,5},{2,6},{3,7},{4,0},{5,1},{6,2},{7,3},{8,12},{9,13},{10,... | collective-permute-start | bytes 884744 | tf_op jit(solution)/shard_map/ppermute | solution.py:28
  65.9 12.1 %collective-permute-start.10 = (bf16[2,2,2,2,32,576]{5,4,3,2,1,0:T(8,128)(2,1)S(1)}, bf16[2,2,2,2,32,576]{5,4,3,2,1,0:T(8,128)(2,1)S(1)}, u32[]{:S(2)}, u32[]{:S(2)}) collective-permute-start(bf16[2,2,2,2,32,576]{5,4,3,2,1,0:T(8,128)(2,1)S(1)} %maximum_select_fusion.6), channel_id=1, source_target_pairs={{0,1},{1,0},{2,3},{3,2},{4,5},{5,4},{6,7},{7,6},{8,9},{9,8},{10,11... | collective-permute-start | bytes 1769480 | tf_op jit(solution)/shard_map/ppermute | solution.py:28
  68.4 24.0 %collective-permute-start.2 = (bf16[2,2,192,384]{3,2,1,0:T(8,128)(2,1)}, bf16[2,2,192,384]{3,2,1,0:T(8,128)(2,1)S(1)}, u32[]{:S(2)}, u32[]{:S(2)}) collective-permute-start(bf16[2,2,192,384]{3,2,1,0:T(8,128)(2,1)} %maximum_select_fusion.8), channel_id=1, source_target_pairs={{0,4},{1,5},{2,6},{3,7},{4,0},{5,1},{6,2},{7,3},{8,12},{9,13},{10,... | collective-permute-start | bytes 1769480 | tf_op jit(solution)/shard_map/ppermute | solution.py:28
  73.1 19.5 %collective-permute-start.4 = (bf16[2,2,192,384]{3,2,1,0:T(8,128)(2,1)}, bf16[2,2,192,384]{3,2,1,0:T(8,128)(2,1)}, u32[]{:S(2)}, u32[]{:S(2)}) collective-permute-start(bf16[2,2,192,384]{3,2,1,0:T(8,128)(2,1)} %maximum_select_fusion.10), channel_id=1, source_target_pairs={{0,2},{1,3},{2,0},{3,1},{4,6},{5,7},{6,4},{7,5},{8,10},{9,11},{10,... | collective-permute-start | bytes 1769480 | tf_op jit(solution)/shard_map/ppermute | solution.py:28
  78.6 15.9 %copy-start.22 = (bf16[32,24,576]{2,1,0:T(8,128)(2,1)}, bf16[32,24,576]{2,1,0:T(8,128)(2,1)S(1)}, u32[]{:S(2)}) copy-start(bf16[32,24,576]{2,1,0:T(8,128)(2,1)S(1)} %slice.327) | copy-start | bytes 2654212
  97.0 2.9 collective-permute-start.11
  130.0 27.3 %all-to-all-start = ((bf16[8,192,192]{2,1,0:T(8,128)(2,1)}), bf16[8,192,192]{2,1,0:T(8,128)(2,1)S(1)}, u32[]{:S(2)}, u32[]{:S(2)}) async-start(bf16[8,192,192]{2,1,0:T(8,128)(2,1)} %bitcast.344), calls=%async_computation | async-start | bytes 1572864 | tf_op jit(solution)/shard_map/all_to_all | solution.py:355
  136.8 255.5 %reduce-scatter.2.cloned.1.call-start = ((), (), s32[]{:S(2)}) async-start(), calls=%async_computation.3 | async-start | bytes 6082560 | tf_op jit(solution)/shard_map/reduce_scatter | solution.py:407
  164.1 2.3 collective-permute-start.14
  166.4 15.1 %copy-start.7 = (bf16[16,96,768]{2,1,0:T(8,128)(2,1)}, bf16[16,96,768]{2,1,0:T(8,128)(2,1)S(1)}, u32[]{:S(2)}) copy-start(bf16[16,96,768]{2,1,0:T(8,128)(2,1)S(1)} %slice.346) | copy-start | bytes 7077892
  166.4 15.1 %copy-start.27 = (bf16[384,768]{1,0:T(8,128)(2,1)}, bf16[384,768]{1,0:T(8,128)(2,1)S(1)}, u32[]{:S(2)}) copy-start(bf16[384,768]{1,0:T(8,128)(2,1)S(1)} %collective-permute-done.14) | copy-start | bytes 1769476
  184.9 2.1 collective-permute-start.15
  187.0 7.2 %copy-start.46 = (f32[768,1536]{1,0:T(8,128)S(1)}, f32[768,1536]{1,0:T(8,128)}, u32[]{:S(2)}) copy-start(f32[768,1536]{1,0:T(8,128)} %get-tuple-element.114) | copy-start | bytes 14155780
  190.0 4.2 copy-start.45
  192.1 5.8 %copy-start.12 = (bf16[384,768]{1,0:T(8,128)(2,1)}, bf16[384,768]{1,0:T(8,128)(2,1)S(1)}, u32[]{:S(2)}) copy-start(bf16[384,768]{1,0:T(8,128)(2,1)S(1)} %add_convert_fusion.3) | copy-start | bytes 1769476
  192.1 2.1 collective-permute-start.16
  201.6 7.4 %collective-permute-start.17 = (bf16[384,768]{1,0:T(8,128)(2,1)}, bf16[384,768]{1,0:T(8,128)(2,1)}, u32[]{:S(2)}, u32[]{:S(2)}) collective-permute-start(bf16[384,768]{1,0:T(8,128)(2,1)} %slice.510), channel_id=1, source_target_pairs={{0,1},{1,0},{2,3},{3,2},{4,5},{5,4},{6,7},{7,6},{8,9},{9,8},{10,11... | collective-permute-start | bytes 1769480 | tf_op jit(solution)/shard_map/ppermute | solution.py:28
  208.9 4.2 %collective-permute-start.30 = (bf16[384,384]{1,0:T(8,128)(2,1)}, bf16[384,384]{1,0:T(8,128)(2,1)}, u32[]{:S(2)}, u32[]{:S(2)}) collective-permute-start(bf16[384,384]{1,0:T(8,128)(2,1)} %copy.145), channel_id=1, source_target_pairs={{0,1},{1,0},{2,3},{3,2},{4,5},{5,4},{6,7},{7,6},{8,9},{9,8},{10,11... | collective-permute-start | bytes 884744 | tf_op jit(solution)/shard_map/ppermute | solution.py:28
  212.0 7.0 %collective-permute-start.31 = (bf16[384,768]{1,0:T(8,128)(2,1)S(1)}, bf16[384,768]{1,0:T(8,128)(2,1)}, u32[]{:S(2)}, u32[]{:S(2)}) collective-permute-start(bf16[384,768]{1,0:T(8,128)(2,1)S(1)} %get-tuple-element.44), channel_id=1, source_target_pairs={{0,1},{1,0},{2,3},{3,2},{4,5},{5,4},{6,7},{7,6},{8,9},{9,8},{10,11... | collective-permute-start | bytes 1769480 | tf_op jit(solution)/shard_map/ppermute | solution.py:28
  324.3 4.3 %copy-start.1 = (bf16[2,2,2,192,768]{4,3,2,1,0:T(8,128)(2,1)S(1)}, bf16[2,2,2,192,768]{4,3,2,1,0:T(8,128)(2,1)}, u32[]{:S(2)}) copy-start(bf16[2,2,2,192,768]{4,3,2,1,0:T(8,128)(2,1)} %copy-done) | copy-start | bytes 7077892
  328.5 3.2 collective-permute-start.18
  331.7 4.2 %copy-start.9 = (bf16[768,1536]{1,0:T(8,128)(2,1)S(1)}, bf16[768,1536]{1,0:T(8,128)(2,1)}, u32[]{:S(2)}) copy-start(bf16[768,1536]{1,0:T(8,128)(2,1)} %copy.133) | copy-start | bytes 7077892
  338.4 5.5 %collective-permute-start.24 = (bf16[2,2,1,2,56,576]{5,4,3,1,0,2:T(8,128)(2,1)S(1)}, bf16[2,2,1,2,56,576]{5,4,3,1,0,2:T(8,128)(2,1)S(1)}, u32[]{:S(2)}, u32[]{:S(2)}) collective-permute-start(bf16[2,2,1,2,56,576]{5,4,3,1,0,2:T(8,128)(2,1)S(1)} %fusion.38), channel_id=1, source_target_pairs={{0,1},{1,0},{2,3},{3,2},{4,5},{5,4},{6,7},{7,6},{8,9},{9,8},{10,11... | collective-permute-start | bytes 1548296 | tf_op jit(solution)/shard_map/ppermute | solution.py:28
  341.7 26.7 %collective-permute-start.21 = (bf16[2,2,192,384]{3,2,1,0:T(8,128)(2,1)S(1)}, bf16[2,2,192,384]{3,2,1,0:T(8,128)(2,1)S(1)}, u32[]{:S(2)}, u32[]{:S(2)}) collective-permute-start(bf16[2,2,192,384]{3,2,1,0:T(8,128)(2,1)S(1)} %fusion.33), channel_id=1, source_target_pairs={{0,4},{1,5},{2,6},{3,7},{4,0},{5,1},{6,2},{7,3},{8,12},{9,13},{10,... | collective-permute-start | bytes 1769480 | tf_op jit(solution)/shard_map/ppermute | solution.py:28
  342.1 28.2 %collective-permute-start.19 = (bf16[2,2,192,384]{3,2,0,1:T(8,128)(2,1)S(1)}, bf16[2,2,192,384]{3,2,0,1:T(8,128)(2,1)S(1)}, u32[]{:S(2)}, u32[]{:S(2)}) collective-permute-start(bf16[2,2,192,384]{3,2,0,1:T(8,128)(2,1)S(1)} %fusion.32), channel_id=1, source_target_pairs={{0,2},{1,3},{2,0},{3,1},{4,6},{5,7},{6,4},{7,5},{8,10},{9,11},{10,... | collective-permute-start | bytes 1769480 | tf_op jit(solution)/shard_map/ppermute | solution.py:28
  344.0 26.5 %collective-permute-start.25 = (bf16[2,2,56,576]{3,2,1,0:T(8,128)(2,1)S(1)}, bf16[2,2,56,576]{3,2,1,0:T(8,128)(2,1)S(1)}, u32[]{:S(2)}, u32[]{:S(2)}) collective-permute-start(bf16[2,2,56,576]{3,2,1,0:T(8,128)(2,1)S(1)} %fusion.43), channel_id=1, source_target_pairs={{0,8},{1,9},{2,10},{3,11},{4,12},{5,13},{6,14},{7,15},{8,0},{9,1},... | collective-permute-start | bytes 774152 | tf_op jit(solution)/shard_map/ppermute | solution.py:28
  368.7 9.1 %collective-permute-start.22 = (bf16[2,192,384]{2,1,0:T(8,128)(2,1)S(1)}, bf16[2,192,384]{2,1,0:T(8,128)(2,1)S(1)}, u32[]{:S(2)}, u32[]{:S(2)}) collective-permute-start(bf16[2,192,384]{2,1,0:T(8,128)(2,1)S(1)} %fusion.41), channel_id=1, source_target_pairs={{0,2},{1,3},{2,0},{3,1},{4,6},{5,7},{6,4},{7,5},{8,10},{9,11},{10,... | collective-permute-start | bytes 884744 | tf_op jit(solution)/shard_map/ppermute | solution.py:28
  370.5 8.8 %collective-permute-start.20 = (bf16[2,192,384]{2,1,0:T(8,128)(2,1)S(1)}, bf16[2,192,384]{2,1,0:T(8,128)(2,1)S(1)}, u32[]{:S(2)}, u32[]{:S(2)}) collective-permute-start(bf16[2,192,384]{2,1,0:T(8,128)(2,1)S(1)} %fusion.40), channel_id=1, source_target_pairs={{0,4},{1,5},{2,6},{3,7},{4,0},{5,1},{6,2},{7,3},{8,12},{9,13},{10,... | collective-permute-start | bytes 884744 | tf_op jit(solution)/shard_map/ppermute | solution.py:28
  370.7 10.5 %collective-permute-start.26 = (bf16[2,2,56,576]{3,2,1,0:T(8,128)(2,1)S(1)}, bf16[2,2,56,576]{3,2,1,0:T(8,128)(2,1)S(1)}, u32[]{:S(2)}, u32[]{:S(2)}) collective-permute-start(bf16[2,2,56,576]{3,2,1,0:T(8,128)(2,1)S(1)} %fusion.57), channel_id=1, source_target_pairs={{0,16},{16,0},{1,17},{17,1},{2,18},{18,2},{3,19},{19,3},{4,20},{20... | collective-permute-start | bytes 774152 | tf_op jit(solution)/shard_map/ppermute | solution.py:28
  380.1 15.4 %collective-permute-start.23 = (bf16[192,768]{1,0:T(8,128)(2,1)}, bf16[192,768]{1,0:T(8,128)(2,1)}, u32[]{:S(2)}, u32[]{:S(2)}) collective-permute-start(bf16[192,768]{1,0:T(8,128)(2,1)} %fusion.42), channel_id=1, source_target_pairs={{0,8},{1,9},{2,10},{3,11},{4,12},{5,13},{6,14},{7,15},{8,0},{9,1},... | collective-permute-start | bytes 884744 | tf_op jit(solution)/shard_map/ppermute | solution.py:28
  381.4 7.9 %collective-permute-start.29 = (bf16[56,576]{1,0:T(8,128)(2,1)S(1)}, bf16[56,576]{1,0:T(8,128)(2,1)S(1)}, u32[]{:S(2)}, u32[]{:S(2)}) collective-permute-start(bf16[56,576]{1,0:T(8,128)(2,1)S(1)} %get-tuple-element.95), channel_id=1, source_target_pairs={{0,6},{1,7},{2,4},{3,5},{4,2},{5,3},{6,0},{7,1},{8,14},{9,15},{10,... | collective-permute-start | bytes 193544 | tf_op jit(solution)/shard_map/ppermute | solution.py:28
  383.2 6.8 %collective-permute-start.28 = (bf16[56,576]{1,0:T(8,128)(2,1)S(1)}, bf16[56,576]{1,0:T(8,128)(2,1)S(1)}, u32[]{:S(2)}, u32[]{:S(2)}) collective-permute-start(bf16[56,576]{1,0:T(8,128)(2,1)S(1)} %get-tuple-element.96), channel_id=1, source_target_pairs={{0,4},{1,5},{2,6},{3,7},{4,0},{5,1},{6,2},{7,3},{8,12},{9,13},{10,... | collective-permute-start | bytes 193544 | tf_op jit(solution)/shard_map/ppermute | solution.py:28
  383.6 6.5 %collective-permute-start.27 = (bf16[56,576]{1,0:T(8,128)(2,1)S(1)}, bf16[56,576]{1,0:T(8,128)(2,1)S(1)}, u32[]{:S(2)}, u32[]{:S(2)}) collective-permute-start(bf16[56,576]{1,0:T(8,128)(2,1)S(1)} %get-tuple-element.97), channel_id=1, source_target_pairs={{0,2},{1,3},{2,0},{3,1},{4,6},{5,7},{6,4},{7,5},{8,10},{9,11},{10,... | collective-permute-start | bytes 193544 | tf_op jit(solution)/shard_map/ppermute | solution.py:28
  392.3 15.7 %collective-permute-start.32 = (bf16[440,768]{1,0:T(8,128)(2,1)}, bf16[440,768]{1,0:T(8,128)(2,1)S(1)}, u32[]{:S(2)}, u32[]{:S(2)}) collective-permute-start(bf16[440,768]{1,0:T(8,128)(2,1)} %bitcast.345), channel_id=1, source_target_pairs={{0,16},{16,0},{1,17},{17,1},{2,18},{18,2},{3,19},{19,3},{4,20},{20... | collective-permute-start | bytes 2027528 | tf_op jit(solution)/shard_map/ppermute | solution.py:28
  396.6 11.4 %copy-start.24 = (bf16[1,440,768]{2,1,0:T(8,128)(2,1)S(1)}, bf16[1,440,768]{2,1,0:T(8,128)(2,1)}, u32[]{:S(2)}) copy-start(bf16[1,440,768]{2,1,0:T(8,128)(2,1)} %reduce-scatter.2.cloned.1.call-done) | copy-start | bytes 2027524
  409.5 1.5 collective-permute-start.33
  (36 other events, 97.6 us)
Sparse Core Ops, SparseCore 0:
  11.9 122.0 all-gather.2
  232.0 127.9 reduce-scatter.1

commit v4 on v3

--- a/solution.py
+++ b/solution.py
@@ -106,6 +106,7 @@
         out_specs=[pl.BlockSpec((bq,W),lambda i,h:(i,0)),pl.BlockSpec((bq,W),lambda i,h:(i,0)),pl.BlockSpec((bq,128),lambda i,h:(i,0))],
         out_shape=[jax.ShapeDtypeStruct((n,W),BF16),jax.ShapeDtypeStruct((n,W),F32),jax.ShapeDtypeStruct((n,128),F32)],
         scratch_shapes=[pltpu.VMEM((NH,128,L),BF16),pltpu.VMEM((NH,L,128),BF16),pltpu.VMEM((NH,bq,128),F32),pltpu.VMEM((NH,bq,128),F32)],
+        cost_estimate=pl.CostEstimate(flops=16*n*L*W, transcendentals=NH*n*L, bytes_accessed=4*n*L),
         name="attend_forward",
     )(q,kv,kb)
 
@@ -163,6 +164,7 @@
         out_shape=[jax.ShapeDtypeStruct((n,W),BF16),jax.ShapeDtypeStruct((L,2*W),F32)],
         scratch_shapes=[pltpu.VMEM((NH,128,n),BF16),pltpu.VMEM((NH,n,128),BF16),pltpu.VMEM((NH,128,n),BF16),pltpu.VMEM((NH,n,128),BF16),
             pltpu.VMEM((NH,HEAD,n),F32),pltpu.VMEM((NH,bk,128),F32),pltpu.VMEM((NH,bk,128),F32)],
+        cost_estimate=pl.CostEstimate(flops=32*n*L*W, transcendentals=NH*n*L, bytes_accessed=4*n*L),
         name="attend_backward",
     )(q,kv,kb,cf,st,dc)
 
@@ -191,14 +193,19 @@
     small = jnp.concatenate([vec_ref[...]] + sums, axis=0).astype(BF16)
     for q in range(chips):
         out_ref[q, first + r_ctx : first + r_ctx + own + 4] = small
-
-
-def weight_grads(y, dz, a, do, ctx, da, vec, chips):
+        out_ref[q, first + r_ctx + own + 4 :] = jnp.zeros((out_ref.shape[1] - first - r_ctx - own - 4, width), BF16)
+
+
+def weight_grads(y, dz, a, do, ctx, da, vec, chips, parts):
     width = y.shape[1]
     total = 2 * width // chips + a.shape[1] // chips + ctx.shape[1] // chips + vec.shape[0] + 4
+    total = -(-total // (16 * parts)) * 16 * parts
     return pl.pallas_call(
         partial(weight_grads_body, chips=chips),
         out_shape=jax.ShapeDtypeStruct((chips, total, width), BF16),
+        cost_estimate=pl.CostEstimate(
+            flops=2 * width * (y.shape[0] * (2 * dz.shape[1] + ctx.shape[1])), transcendentals=0, bytes_accessed=15 * width * width * 2
+        ),
         name="weight_grads",
     )(y, dz, a, do, ctx, da, vec)
 
@@ -267,8 +274,11 @@
         ],
         axis=0,
     )
-    same_core = [[2 * d + i for d in range(n_dev // 2)] for i in range(2)]
-    gathered = lax.all_gather(packed, ("grp", "seq"), axis=0, tiled=False, axis_index_groups=same_core)
+    chip_groups = [[2 * q + i for q in range(chips)] for i in range(2)]
+    gathered = lax.all_gather(packed, "seq", axis=0, tiled=False, axis_index_groups=chip_groups)
+    for b in range(log2_of(grp_size)):
+        theirs = flip(gathered, "grp", grp_size, 1 << b)
+        gathered = in_order(gathered, theirs, (grp >> b) % 2).reshape((-1,) + packed.shape)
 
     x_mine = pick(tokens, z1)
     x_sent = pick(tokens, 1 - z1)
@@ -402,23 +412,28 @@
     both_ctx = jnp.concatenate([pick(ctx_split, core), sflip(pick(ctx_split, 1 - core), 1)], axis=0)
     both_dattend = jnp.concatenate([dattend, sflip(dattend, 1)], axis=0)
     vectors = jnp.stack([dfirst_gain, dfirst_shift, dsecond_gain, dsecond_shift])
-    grads = weight_grads(both_first, dinner, active, both_douter, both_ctx, both_dattend, vectors, chips)
-    chip_groups = [[2 * q + i for q in range(chips)] for i in range(2)]
-    grads = lax.psum_scatter(grads, "seq", scatter_dimension=0, tiled=False, axis_index_groups=chip_groups)
+    grads = weight_grads(both_first, dinner, active, both_douter, both_ctx, both_dattend, vectors, chips, grp_size)
+    grads = grads.reshape(chips, grp_size, -1, width)
+    for b in reversed(range(log2_of(grp_size))):
+        bit = (grp >> b) % 2
+        n_half = grads.shape[1] // 2
+        kept, sent = (lax.dynamic_slice_in_dim(grads, n_half * i, n_half, axis=1) for i in (bit, 1 - bit))
+        grads = (kept.astype(jnp.float32) + flip(sent, "grp", grp_size, 1 << b).astype(jnp.float32)).astype(bf16)
+    grads = lax.psum_scatter(grads[:, 0], "seq", scatter_dimension=0, tiled=False, axis_index_groups=chip_groups)
     for b in range(log2_of(grp_size)):
-        grads = (grads.astype(jnp.float32) + flip(grads, "grp", grp_size, 1 << b).astype(jnp.float32)).astype(bf16)
+        grads = in_order(grads, flip(grads, "grp", grp_size, 1 << b), (grp >> b) % 2).reshape(-1, width)
     r1 = 4 * out_rows
     r2 = r1 + piece
     r3 = r2 + out_rows
     inner_grad = grads[:r1].reshape(2, 2, out_rows, width)
     inner_grad = [inner_grad[:, i] for i in range(2)]
-    far = sflip(jnp.concatenate([pick(inner_grad, 1 - core).reshape(2 * out_rows, width), grads[r3:]], axis=0), 1)
+    far = sflip(jnp.concatenate([pick(inner_grad, 1 - core).reshape(2 * out_rows, width), grads[r3 : r3 + 8]], axis=0), 1)
     dinner_weight = in_order(pick(inner_grad, core), far[: 2 * out_rows].reshape(2, out_rows, width), core)
     dinner_weight = dinner_weight.transpose(2, 0, 1, 3).reshape(out_rows, 2, chips, piece).transpose(0, 2, 1, 3)
     dinner_weight = dinner_weight.reshape(out_rows, feed).astype(jnp.float32)
     douter_weight = grads[r1:r2].astype(jnp.float32)
     doutput_weight = grads[r2:r3].astype(jnp.float32)
-    small = grads[r3:].astype(jnp.float32)
+    small = grads[r3 : r3 + 8].astype(jnp.float32)
     both = lax.dynamic_slice_in_dim(small + far[2 * out_rows :].astype(jnp.float32), me * out_rows, out_rows, axis=1)
     dfirst_gain, dfirst_shift, dsecond_gain, dsecond_shift, doutput_bias, douter_bias = (both[i] for i in range(6))
     dinner_bias = lax.dynamic_slice_in_dim(small[6:8].reshape(half_feed), (me // 2) * piece, piece)

time: 431 us -> 475 us (1.10)
  waiting for transfers between devices: 120 us -> 169 us
  blocking collectives: 43.3 us -> 0 us
  matrix products: 29.9 us -> 45.8 us
  other arithmetic: 44.2 us -> 57.3 us
  local copies, waits for them, and re-layouts: 35.8 us -> 48.5 us
    all_to_all x1 -> x0, blocking collectives: 43.3 us -> none  [exchange(): lax.all_to_all(blocks, 'seq', 0, 0, axis_index_groups=teams, tiled=True)]
    ppermute x33 -> x35, waiting for transfers between devices: 99.6 us -> 127 us  [flip(): return lax.ppermute(value, axis, [(i, i ^ mask) for i in range(size)])]
    reduce_scatter x1, waiting for transfers between devices: 0.01 us -> 21.6 us  [per_device(): lax.psum_scatter(grads[:, 0], 'seq', scatter_dimension=0, tiled=False, ax...]
    dot_general x4, matrix products: 19.4 us -> 30.4 us  [dot(): return jnp.dot(left, right, preferred_element_type=jnp.float32)]
    concatenate x1, local copies, waits for them, and re-layouts: 0.1 us -> 6.13 us  [per_device(): jnp.concatenate([query_bias, value_bias, output_bias, first_gain, first_s...]
    select_n x16 -> x18, other arithmetic: 2.87 us -> 8.36 us  [in_order(): jnp.where(bit == 0, jnp.stack([mine, theirs]), jnp.stack([theirs, mine]))]
    dot_general x4, matrix products: 8.41 us -> 13.3 us  [dot_t(): lax.dot_general(left, right, (((1,), (1,)), ((), ())), preferred_element_...]
    all_to_all x1 -> x2, starting transfers between devices: 6.81 us -> 9.88 us  [exchange(): lax.all_to_all(blocks, 'seq', 0, 0, axis_index_groups=teams, tiled=True)]
  transfers between devices with their start and end apart: 37 -> 40, of which waited for: 20 -> 18; matrix products, arithmetic and copies ran while one was open for 15% -> 16% of each run, Pallas kernels for 18% -> 18%
where the time goes in v4:
time: 475 us; the launch traced here: 470 us
  waiting for transfers between devices  169 us (36%)
  Pallas kernels  85.9 us (18%)
  other arithmetic  57.3 us (12%)
  local copies, waits for them, and re-layouts  48.5 us (10%)
  starting transfers between devices  47.2 us (10%)
  matrix products  45.8 us (10%)
  between operations  17 us (4%)
    ppermute x35, waiting for transfers between devices, flip(): return lax.ppermute(value, axis, [(i, i ^ mask) for i in range(size)])  127 us
    pallas_call x1, Pallas kernels, attend_backward(): pl.pallas_call(partial(bwd_body, bk=bk, nk=nk), grid=(nk, NH), in_specs=[...  46.9 us
    ppermute x35, starting transfers between devices, flip(): return lax.ppermute(value, axis, [(i, i ^ mask) for i in range(size)])  36.6 us
    dot_general x4, matrix products, dot(): return jnp.dot(left, right, preferred_element_type=jnp.float32)  30.4 us
    pallas_call x1, Pallas kernels, attend_forward(): pl.pallas_call(partial(fwd_body, bq=bq), grid=(n // bq, NH), in_specs=[pl...  28.4 us
    reduce_scatter x1, waiting for transfers between devices, per_device(): lax.psum_scatter(grads[:, 0], 'seq', scatter_dimension=0, tiled=False, ax...  21.6 us
    all_to_all x2, waiting for transfers between devices, exchange(): lax.all_to_all(blocks, 'seq', 0, 0, axis_index_groups=teams, tiled=True)  20.3 us
    dot_general x4, matrix products, dot_t(): lax.dot_general(left, right, (((1,), (1,)), ((), ())), preferred_element_...  13.3 us
  transfers between devices with their start and end apart: 40, of which 18 were waited for; matrix products, arithmetic and copies ran while one was open for 16% of the time, Pallas kernels for 18%

profile of v4, /device:TPU:0, one launch (start us, length us, event | category | flops | bytes accessed | tf_op | source)
XLA Modules:
  0.0 470.3 jit_solution(4845344026310379990)
XLA Ops:
  7.3 6.1 %concatenate.253 = bf16[288]{0:T(512)(128)(2,1)S(1)} concatenate(bf16[24]{0:T(256)(128)(2,1)} %param.23, bf16[24]{0:T(256)(128)(2,1)} %param.26, bf16[24]{0:T(256)(128)(2,1)} %param.28, bf16[24]{0:T(256)(128)(2,1)} %param.29, bf16[24]{0:T(256)(128)(2,1)} %param.30, bf16[24]{0:T(256)(128)(2,1)} %param.34, bf16[24]{0:T(256)(128)(2,1)} %param.35, bf16[24]{0:T(256)(128)(2,1)} %param.36, ...), dimensions={0} | concatenate | bytes 1152 | tf_op jit(solution)/shard_map/concatenate | solution.py:295
  17.2 3.1 collective-permute-start.5
  23.3 3.3 collective-permute-start.12
  28.9 2.7 collective-permute-start
  33.5 30.5 %collective-permute-done.8 = bf16[2,2,32,576]{3,2,1,0:T(8,128)(2,1)S(1)} collective-permute-done((bf16[2,2,32,576]{3,2,1,0:T(8,128)(2,1)S(1)}, bf16[2,2,32,576]{3,2,1,0:T(8,128)(2,1)S(1)}, u32[]{:S(2)}, u32[]{:S(2)}) %collective-permute-start.8) | collective-permute-done | bytes 147488 | tf_op jit(solution)/shard_map/ppermute | solution.py:28
  67.3 5.6 %collective-permute-done.9 = bf16[2,2,2,32,576]{4,3,2,1,0:T(8,128)(2,1)S(1)} collective-permute-done((bf16[2,2,2,32,576]{4,3,2,1,0:T(8,128)(2,1)S(1)}, bf16[2,2,2,32,576]{4,3,2,1,0:T(8,128)(2,1)S(1)}, u32[]{:S(2)}, u32[]{:S(2)}) %collective-permute-start.9) | collective-permute-done | bytes 294944 | tf_op jit(solution)/shard_map/ppermute | solution.py:28
  73.4 7.9 %collective-permute-done.1 = bf16[2,192,384]{2,1,0:T(8,128)(2,1)S(1)} collective-permute-done((bf16[2,192,384]{2,1,0:T(8,128)(2,1)S(1)}, bf16[2,192,384]{2,1,0:T(8,128)(2,1)S(1)}, u32[]{:S(2)}, u32[]{:S(2)}) %collective-permute-start.1) | collective-permute-done | bytes 294944 | tf_op jit(solution)/shard_map/ppermute | solution.py:28
  82.9 6.8 %collective-permute-done.3 = bf16[2,192,384]{2,1,0:T(8,128)(2,1)S(1)} collective-permute-done((bf16[2,192,384]{2,1,0:T(8,128)(2,1)S(1)}, bf16[2,192,384]{2,1,0:T(8,128)(2,1)S(1)}, u32[]{:S(2)}, u32[]{:S(2)}) %collective-permute-start.3) | collective-permute-done | bytes 294944 | tf_op jit(solution)/shard_map/ppermute | solution.py:28
  93.9 16.8 %collective-permute-done.2 = bf16[2,2,192,384]{3,2,1,0:T(8,128)(2,1)S(1)} collective-permute-done((bf16[2,2,192,384]{3,2,1,0:T(8,128)(2,1)}, bf16[2,2,192,384]{3,2,1,0:T(8,128)(2,1)S(1)}, u32[]{:S(2)}, u32[]{:S(2)}) %collective-permute-start.2) | collective-permute-done | bytes 589856 | tf_op jit(solution)/shard_map/ppermute | solution.py:28
  112.8 2.0 convolution_add_fusion
  118.9 2.5 fusion.10.q_ref
  123.2 28.4 %attend_forward.1 = (bf16[1536,192]{1,0:T(8,128)(2,1)}, f32[1536,192]{1,0:T(8,128)}, f32[1536,128]{1,0:T(8,128)}) custom-call(bf16[1536,192]{1,0:T(8,128)(2,1)} %fusion.10.q_ref, bf16[3072,384]{1,0:T(8,128)(2,1)} %bitcast.331, bf16[3072,128]{1,0:T(8,128)(2,1)} %select_convert_fusion.1.kb_ref), custom_call_target="tpu_custom_call" | custom-call | flops 14495514624 | bytes 18874368 | tf_op jit(solution)/shard_map/attend_forward/pallas_call | solution.py:103
  151.6 5.3 %all-to-all-start = ((bf16[8,192,192]{2,1,0:T(8,128)(2,1)}), bf16[8,192,192]{2,1,0:T(8,128)(2,1)S(1)}, u32[]{:S(2)}, u32[]{:S(2)}) async-start(bf16[8,192,192]{2,1,0:T(8,128)(2,1)} %bitcast.359), calls=%async_computation | async-start | bytes 1572864 | tf_op jit(solution)/shard_map/all_to_all | solution.py:365
  157.1 20.3 %all-to-all-done = bf16[8,192,192]{2,1,0:T(8,128)(2,1)S(1)} async-done(((bf16[8,192,192]{2,1,0:T(8,128)(2,1)}), bf16[8,192,192]{2,1,0:T(8,128)(2,1)S(1)}, u32[]{:S(2)}, u32[]{:S(2)}) %all-to-all-start) | async-done | bytes 589856 | tf_op jit(solution)/shard_map/all_to_all | solution.py:365
  178.7 6.1 %collective-permute-done.14 = bf16[8,240,768]{2,1,0:T(8,128)(2,1)} collective-permute-done((bf16[8,240,768]{2,1,0:T(8,128)(2,1)}, bf16[8,240,768]{2,1,0:T(8,128)(2,1)}, u32[]{:S(2)}, u32[]{:S(2)}) %collective-permute-start.14) | collective-permute-done | bytes 2949152 | tf_op jit(solution)/shard_map/ppermute | solution.py:28
  184.8 5.4 %maximum_select_fusion = bf16[2,8,240,768]{3,2,1,0:T(8,128)(2,1)S(1)} fusion(bf16[1,8,240,768]{3,2,1,0:T(8,128)(2,1)} %bitcast.58, bf16[1,8,240,768]{3,2,1,0:T(8,128)(2,1)} %bitcast.327, pred[]{:T(512)S(6)} %eq.43), kind=kLoop, calls=%fused_computation.1 | loop fusion | flops 8847360 | bytes 11796481 | tf_op jit(solution)/shard_map/jit(_where)/select_n | solution.py:32
  195.1 2.0 slice.346
  197.4 25.7 %multiply_convert_fusion.1 = (bf16[768,1536]{1,0:T(8,128)(2,1)S(1)}, f32[768,1536]{1,0:T(8,128)}, f32[768,1536]{1,0:T(8,128)}) fusion(f32[1536]{0:T(1024)S(1)} %select_n.785, bf16[768,768]{1,0:T(8,128)(2,1)S(1)} %bitcast.344, bf16[768,768]{1,0:T(8,128)(2,1)S(1)} %bitcast.346, bf16[384,768]{1,0:T(8,128)(2,1)S(1)} %collective-permute-done.15, ...), kind=kOutput, calls=%fused_computation.5 | convolution fusion | flops 1896873984 | bytes 15341568 | tf_op jit(solution)/shard_map/dot_general | solution.py:46
  223.1 2.0 fusion.89
  234.1 1.9 copy.144
  236.0 3.0 reshape_reshape.3
  239.1 7.8 %multiply_convert_fusion.dz_ref = bf16[768,1536]{1,0:T(8,128)(2,1)S(1)} fusion(f32[768,1536]{1,0:T(8,128)} %get-tuple-element.54, f32[768,1536]{1,0:T(8,128)} %get-tuple-element.114, bf16[1536,768]{1,0:T(8,128)(2,1)} %bitcast.334, f32[1536]{0:T(1024)S(1)} %select_n.785, bf16[384,768]{1,0:T(8,128)(2,1)} %collective-permute-done.17, ...), kind=kOutput, calls=%fused_computation.4 | convolution fusion | flops 1829634048 | bytes 15341568 | tf_op jit(solution)/shard_map/dot_general | solution.py:50
  246.9 2.0 fusion.11
  254.5 1.9 pad_maximum_fusion.10.ctx_ref
  256.4 2.2 multiply_reduce_fusion
  262.2 2.4 reshape.1362
  265.6 4.6 all-to-all-start.1
  271.4 2.4 pad_maximum_fusion.7.do_ref
  275.4 10.6 %weight_grads.1 = bf16[8,448,768]{2,1,0:T(8,128)(2,1)} custom-call(bf16[768,768]{1,0:T(8,128)(2,1)} %pad_maximum_fusion.6.y_ref, bf16[768,1536]{1,0:T(8,128)(2,1)} %copy-done.34, bf16[768,1536]{1,0:T(8,128)(2,1)} %copy-done.33, bf16[768,768]{1,0:T(8,128)(2,1)} %pad_maximum_fusion.7.do_ref, bf16[768,384]{1,0:T(8,128)(2,1)} %pad_maximum_fusion.10.ctx_ref, ...), custom_call_target="tpu_custom_call" | custom-call | flops 4076863488 | bytes 17694720 | tf_op jit(solution)/shard_map/weight_grads/pallas_call | solution.py:203
  286.0 3.5 constant_dynamic-slice_fusion.2
  291.9 46.9 %attend_backward.1 = (bf16[1536,192]{1,0:T(8,128)(2,1)}, f32[3072,384]{1,0:T(8,128)}) custom-call(bf16[1536,192]{1,0:T(8,128)(2,1)} %fusion.10.q_ref, bf16[3072,384]{1,0:T(8,128)(2,1)} %bitcast.332, bf16[3072,128]{1,0:T(8,128)(2,1)} %select_convert_fusion.1.kb_ref, f32[1536,192]{1,0:T(8,128)} %get-tuple-element.35.cf_ref, ...), custom_call_target="tpu_custom_call" | custom-call | flops 28991029248 | bytes 18874368 | tf_op jit(solution)/shard_map/attend_backward/pallas_call | solution.py:160
  338.9 2.8 fusion.15
  342.0 2.6 copy.133
  344.7 3.2 fusion.16
  348.9 2.1 fusion.8
  352.3 4.0 fusion.6
  356.4 2.1 pad_maximum_fusion.3
  358.5 2.0 fusion.90
  360.7 2.0 collective-permute-start.22
  365.8 2.4 collective-permute-start.26
  368.2 30.5 %collective-permute-done.22 = bf16[2,2,192,384]{3,2,1,0:T(8,128)(2,1)S(1)} collective-permute-done((bf16[2,2,192,384]{3,2,1,0:T(8,128)(2,1)S(1)}, bf16[2,2,192,384]{3,2,1,0:T(8,128)(2,1)S(1)}, u32[]{:S(2)}, u32[]{:S(2)}) %collective-permute-start.22) | collective-permute-done | bytes 589856 | tf_op jit(solution)/shard_map/ppermute | solution.py:28
  399.0 2.4 collective-permute-start.23
  401.9 8.2 %collective-permute-done.23 = bf16[2,192,384]{2,1,0:T(8,128)(2,1)S(1)} collective-permute-done((bf16[2,192,384]{2,1,0:T(8,128)(2,1)S(1)}, bf16[2,192,384]{2,1,0:T(8,128)(2,1)S(1)}, u32[]{:S(2)}, u32[]{:S(2)}) %collective-permute-start.23) | collective-permute-done | bytes 294944 | tf_op jit(solution)/shard_map/ppermute | solution.py:28
  410.1 2.2 collective-permute-done.21
  415.0 3.5 collective-permute-start.30
  419.3 2.8 collective-permute-done.30
  426.4 21.6 %reduce-scatter.2.cloned.1.call-done = bf16[1,224,768]{2,1,0:T(8,128)(2,1)} async-done(((bf16[8,224,768]{2,1,0:T(8,128)(2,1)}), bf16[1,224,768]{2,1,0:T(8,128)(2,1)}) %reduce-scatter.2.cloned.1.call-update) | async-done | bytes 344080 | tf_op jit(solution)/shard_map/reduce_scatter | solution.py:422
  451.4 5.3 %collective-permute-done.34 = bf16[224,768]{1,0:T(8,128)(2,1)S(1)} collective-permute-done((bf16[224,768]{1,0:T(8,128)(2,1)}, bf16[224,768]{1,0:T(8,128)(2,1)S(1)}, u32[]{:S(2)}, u32[]{:S(2)}) %collective-permute-start.34) | collective-permute-done | bytes 344096 | tf_op jit(solution)/shard_map/ppermute | solution.py:28
  (304 shorter events, 82.2 us)
Async XLA Ops:
  7.2 14.6 %copy-start.32 = (bf16[96,768]{1,0:T(8,128)(2,1)S(1)}, bf16[96,768]{1,0:T(8,128)(2,1)}, u32[]{:S(2)}) copy-start(bf16[96,768]{1,0:T(8,128)(2,1)} %param.33) | copy-start | bytes 442372
  7.2 15.3 %copy-start.30 = (bf16[24,3072]{1,0:T(8,128)(2,1)S(1)}, bf16[24,3072]{1,0:T(8,128)(2,1)}, u32[]{:S(2)}) copy-start(bf16[24,3072]{1,0:T(8,128)(2,1)} %param.31) | copy-start | bytes 442372
  7.2 111.0 %all-gather.3.cloned.1.call-start = ((), (), s32[]{:S(2)}) async-start(), calls=%async_computation.4 | async-start | bytes 3317760 | tf_op jit(solution)/shard_map/all_gather | solution.py:278
  15.4 11.2 %copy-start.31 = (s32[2]{0:T(128)S(1)}, s32[2]{0:T(128)}, u32[]{:S(2)}) copy-start(s32[2]{0:T(128)} %param.21) | copy-start | bytes 28
  15.4 13.1 %copy-start.24 = (bf16[2,192,768]{2,1,0:T(8,128)(2,1)S(1)}, bf16[2,192,768]{2,1,0:T(8,128)(2,1)}, u32[]{:S(2)}) copy-start(bf16[2,192,768]{2,1,0:T(8,128)(2,1)} %param.20) | copy-start | bytes 1769476
  17.2 15.7 %collective-permute-start.5 = (bf16[32,576]{1,0:T(8,128)(2,1)S(1)}, bf16[32,576]{1,0:T(8,128)(2,1)S(1)}, u32[]{:S(2)}, u32[]{:S(2)}) collective-permute-start(bf16[32,576]{1,0:T(8,128)(2,1)S(1)} %get-tuple-element.101), channel_id=1, source_target_pairs={{0,2},{1,3},{2,0},{3,1},{4,6},{5,7},{6,4},{7,5},{8,10},{9,11},{10,... | collective-permute-start | bytes 110600 | tf_op jit(solution)/shard_map/ppermute | solution.py:28
  20.2 12.6 %collective-permute-start.6 = (bf16[32,576]{1,0:T(8,128)(2,1)S(1)}, bf16[32,576]{1,0:T(8,128)(2,1)S(1)}, u32[]{:S(2)}, u32[]{:S(2)}) collective-permute-start(bf16[32,576]{1,0:T(8,128)(2,1)S(1)} %get-tuple-element.102), channel_id=1, source_target_pairs={{0,4},{1,5},{2,6},{3,7},{4,0},{5,1},{6,2},{7,3},{8,12},{9,13},{10,... | collective-permute-start | bytes 110600 | tf_op jit(solution)/shard_map/ppermute | solution.py:28
  21.8 11.0 %collective-permute-start.7 = (bf16[32,576]{1,0:T(8,128)(2,1)S(1)}, bf16[32,576]{1,0:T(8,128)(2,1)S(1)}, u32[]{:S(2)}, u32[]{:S(2)}) collective-permute-start(bf16[32,576]{1,0:T(8,128)(2,1)S(1)} %get-tuple-element.103), channel_id=1, source_target_pairs={{0,6},{1,7},{2,4},{3,5},{4,2},{5,3},{6,0},{7,1},{8,14},{9,15},{10,... | collective-permute-start | bytes 110600 | tf_op jit(solution)/shard_map/ppermute | solution.py:28
  21.8 10.1 %collective-permute-start.13 = (bf16[96,768]{1,0:T(8,128)(2,1)S(1)}, bf16[96,768]{1,0:T(8,128)(2,1)S(1)}, u32[]{:S(2)}, u32[]{:S(2)}) collective-permute-start(bf16[96,768]{1,0:T(8,128)(2,1)S(1)} %copy-done.32), channel_id=1, source_target_pairs={{0,0},{1,2},{2,1},{3,3},{4,4},{5,6},{6,5},{7,7},{8,8},{9,10},{10,9... | collective-permute-start | bytes 442376 | tf_op jit(solution)/shard_map/ppermute | solution.py:263
  23.3 5.6 %collective-permute-start.12 = (bf16[72,768]{1,0:T(8,128)(2,1)S(1)}, bf16[72,768]{1,0:T(8,128)(2,1)S(1)}, u32[]{:S(2)}, u32[]{:S(2)}) collective-permute-start(bf16[72,768]{1,0:T(8,128)(2,1)S(1)} %pad_maximum_fusion.13), channel_id=1, source_target_pairs={{0,1},{1,0},{2,3},{3,2},{4,5},{5,4},{6,7},{7,6},{8,9},{9,8},{10,11... | collective-permute-start | bytes 331784 | tf_op jit(solution)/shard_map/ppermute | solution.py:28
  28.9 36.8 %collective-permute-start = (bf16[192,768]{1,0:T(8,128)(2,1)S(1)}, bf16[192,768]{1,0:T(8,128)(2,1)S(1)}, u32[]{:S(2)}, u32[]{:S(2)}) collective-permute-start(bf16[192,768]{1,0:T(8,128)(2,1)S(1)} %get-tuple-element.74), channel_id=1, source_target_pairs={{0,8},{1,9},{2,10},{3,11},{4,12},{5,13},{6,14},{7,15},{8,0},{9,1},... | collective-permute-start | bytes 884744 | tf_op jit(solution)/shard_map/ppermute | solution.py:28
  33.0 31.0 %collective-permute-start.8 = (bf16[2,2,32,576]{3,2,1,0:T(8,128)(2,1)S(1)}, bf16[2,2,32,576]{3,2,1,0:T(8,128)(2,1)S(1)}, u32[]{:S(2)}, u32[]{:S(2)}) collective-permute-start(bf16[2,2,32,576]{3,2,1,0:T(8,128)(2,1)S(1)} %maximum_select_fusion.17), channel_id=1, source_target_pairs={{0,8},{1,9},{2,10},{3,11},{4,12},{5,13},{6,14},{7,15},{8,0},{9,1},... | collective-permute-start | bytes 442376 | tf_op jit(solution)/shard_map/ppermute | solution.py:28
  64.1 8.9 %collective-permute-start.9 = (bf16[2,2,2,32,576]{4,3,2,1,0:T(8,128)(2,1)S(1)}, bf16[2,2,2,32,576]{4,3,2,1,0:T(8,128)(2,1)S(1)}, u32[]{:S(2)}, u32[]{:S(2)}) collective-permute-start(bf16[2,2,2,32,576]{4,3,2,1,0:T(8,128)(2,1)S(1)} %maximum_select_fusion.14), channel_id=1, source_target_pairs={{0,16},{16,0},{1,17},{17,1},{2,18},{18,2},{3,19},{19,3},{4,20},{20... | collective-permute-start | bytes 884744 | tf_op jit(solution)/shard_map/ppermute | solution.py:28
  66.0 15.2 %collective-permute-start.1 = (bf16[2,192,384]{2,1,0:T(8,128)(2,1)S(1)}, bf16[2,192,384]{2,1,0:T(8,128)(2,1)S(1)}, u32[]{:S(2)}, u32[]{:S(2)}) collective-permute-start(bf16[2,192,384]{2,1,0:T(8,128)(2,1)S(1)} %get-tuple-element.72), channel_id=1, source_target_pairs={{0,2},{1,3},{2,0},{3,1},{4,6},{5,7},{6,4},{7,5},{8,10},{9,11},{10,... | collective-permute-start | bytes 884744 | tf_op jit(solution)/shard_map/ppermute | solution.py:28
  66.6 23.1 %collective-permute-start.3 = (bf16[2,192,384]{2,1,0:T(8,128)(2,1)S(1)}, bf16[2,192,384]{2,1,0:T(8,128)(2,1)S(1)}, u32[]{:S(2)}, u32[]{:S(2)}) collective-permute-start(bf16[2,192,384]{2,1,0:T(8,128)(2,1)S(1)} %get-tuple-element.71), channel_id=1, source_target_pairs={{0,4},{1,5},{2,6},{3,7},{4,0},{5,1},{6,2},{7,3},{8,12},{9,13},{10,... | collective-permute-start | bytes 884744 | tf_op jit(solution)/shard_map/ppermute | solution.py:28
  73.1 19.4 %collective-permute-start.10 = (bf16[2,2,2,2,32,576]{5,4,3,2,1,0:T(8,128)(2,1)S(1)}, bf16[2,2,2,2,32,576]{5,4,3,2,1,0:T(8,128)(2,1)S(1)}, u32[]{:S(2)}, u32[]{:S(2)}) collective-permute-start(bf16[2,2,2,2,32,576]{5,4,3,2,1,0:T(8,128)(2,1)S(1)} %maximum_select_fusion.8), channel_id=1, source_target_pairs={{0,1},{1,0},{2,3},{3,2},{4,5},{5,4},{6,7},{7,6},{8,9},{9,8},{10,11... | collective-permute-start | bytes 1769480 | tf_op jit(solution)/shard_map/ppermute | solution.py:28
  82.1 28.6 %collective-permute-start.2 = (bf16[2,2,192,384]{3,2,1,0:T(8,128)(2,1)}, bf16[2,2,192,384]{3,2,1,0:T(8,128)(2,1)S(1)}, u32[]{:S(2)}, u32[]{:S(2)}) collective-permute-start(bf16[2,2,192,384]{3,2,1,0:T(8,128)(2,1)} %maximum_select_fusion.10), channel_id=1, source_target_pairs={{0,4},{1,5},{2,6},{3,7},{4,0},{5,1},{6,2},{7,3},{8,12},{9,13},{10,... | collective-permute-start | bytes 1769480 | tf_op jit(solution)/shard_map/ppermute | solution.py:28
  90.7 20.3 %collective-permute-start.4 = (bf16[2,2,192,384]{3,2,1,0:T(8,128)(2,1)}, bf16[2,2,192,384]{3,2,1,0:T(8,128)(2,1)}, u32[]{:S(2)}, u32[]{:S(2)}) collective-permute-start(bf16[2,2,192,384]{3,2,1,0:T(8,128)(2,1)} %maximum_select_fusion.12), channel_id=1, source_target_pairs={{0,2},{1,3},{2,0},{3,1},{4,6},{5,7},{6,4},{7,5},{8,10},{9,11},{10,... | collective-permute-start | bytes 1769480 | tf_op jit(solution)/shard_map/ppermute | solution.py:28
  93.2 19.7 %copy-start.21 = (bf16[32,24,576]{2,1,0:T(8,128)(2,1)}, bf16[32,24,576]{2,1,0:T(8,128)(2,1)S(1)}, u32[]{:S(2)}) copy-start(bf16[32,24,576]{2,1,0:T(8,128)(2,1)S(1)} %slice.327) | copy-start | bytes 2654212
  116.8 4.6 collective-permute-start.11
  118.2 66.6 %collective-permute-start.14 = (bf16[8,240,768]{2,1,0:T(8,128)(2,1)}, bf16[8,240,768]{2,1,0:T(8,128)(2,1)}, u32[]{:S(2)}, u32[]{:S(2)}) collective-permute-start(bf16[8,240,768]{2,1,0:T(8,128)(2,1)} %bitcast.326), channel_id=1, source_target_pairs={{0,16},{16,0},{1,17},{17,1},{2,18},{18,2},{3,19},{19,3},{4,20},{20... | collective-permute-start | bytes 8847368 | tf_op jit(solution)/shard_map/ppermute | solution.py:28
  151.6 25.8 %all-to-all-start = ((bf16[8,192,192]{2,1,0:T(8,128)(2,1)}), bf16[8,192,192]{2,1,0:T(8,128)(2,1)S(1)}, u32[]{:S(2)}, u32[]{:S(2)}) async-start(bf16[8,192,192]{2,1,0:T(8,128)(2,1)} %bitcast.359), calls=%async_computation | async-start | bytes 1572864 | tf_op jit(solution)/shard_map/all_to_all | solution.py:365
  194.7 2.3 collective-permute-start.15
  197.0 26.1 %copy-start.7 = (bf16[16,96,768]{2,1,0:T(8,128)(2,1)}, bf16[16,96,768]{2,1,0:T(8,128)(2,1)S(1)}, u32[]{:S(2)}) copy-start(bf16[16,96,768]{2,1,0:T(8,128)(2,1)S(1)} %slice.346) | copy-start | bytes 7077892
  197.1 26.0 %copy-start.26 = (bf16[384,768]{1,0:T(8,128)(2,1)}, bf16[384,768]{1,0:T(8,128)(2,1)S(1)}, u32[]{:S(2)}) copy-start(bf16[384,768]{1,0:T(8,128)(2,1)S(1)} %collective-permute-done.15) | copy-start | bytes 1769476
  226.6 2.2 collective-permute-start.16
  233.8 5.3 %collective-permute-start.17 = (bf16[384,768]{1,0:T(8,128)(2,1)}, bf16[384,768]{1,0:T(8,128)(2,1)}, u32[]{:S(2)}, u32[]{:S(2)}) collective-permute-start(bf16[384,768]{1,0:T(8,128)(2,1)} %add_convert_fusion.3), channel_id=1, source_target_pairs={{0,1},{1,0},{2,3},{3,2},{4,5},{5,4},{6,7},{7,6},{8,9},{9,8},{10,11... | collective-permute-start | bytes 1769480 | tf_op jit(solution)/shard_map/ppermute | solution.py:28
  249.8 6.6 %collective-permute-start.18 = (bf16[384,768]{1,0:T(8,128)(2,1)}, bf16[384,768]{1,0:T(8,128)(2,1)}, u32[]{:S(2)}, u32[]{:S(2)}) collective-permute-start(bf16[384,768]{1,0:T(8,128)(2,1)} %slice.510), channel_id=1, source_target_pairs={{0,1},{1,0},{2,3},{3,2},{4,5},{5,4},{6,7},{7,6},{8,9},{9,8},{10,11... | collective-permute-start | bytes 1769480 | tf_op jit(solution)/shard_map/ppermute | solution.py:28
  252.6 1.9 collective-permute-start.31
  260.3 14.0 %collective-permute-start.32 = (bf16[384,768]{1,0:T(8,128)(2,1)S(1)}, bf16[384,768]{1,0:T(8,128)(2,1)S(1)}, u32[]{:S(2)}, u32[]{:S(2)}) collective-permute-start(bf16[384,768]{1,0:T(8,128)(2,1)S(1)} %get-tuple-element.44), channel_id=1, source_target_pairs={{0,1},{1,0},{2,3},{3,2},{4,5},{5,4},{6,7},{7,6},{8,9},{9,8},{10,11... | collective-permute-start | bytes 1769480 | tf_op jit(solution)/shard_map/ppermute | solution.py:28
  265.6 25.4 %all-to-all-start.1 = ((bf16[8,192,192]{2,1,0:T(8,128)(2,1)}), bf16[8,192,192]{2,1,0:T(8,128)(2,1)S(1)}, u32[]{:S(2)}, u32[]{:S(2)}) async-start(bf16[8,192,192]{2,1,0:T(8,128)(2,1)} %bitcast.69), calls=%async_computation.1 | async-start | bytes 1572864 | tf_op jit(solution)/shard_map/all_to_all | solution.py:365
  270.2 177.8 %reduce-scatter.2.cloned.1.call-start = ((), (), s32[]{:S(2)}) async-start(), calls=%async_computation.3 | async-start | bytes 3096576 | tf_op jit(solution)/shard_map/reduce_scatter | solution.py:422
  289.5 62.7 %collective-permute-start.33 = (bf16[8,1,224,768]{3,2,1,0:T(8,128)(2,1)}, bf16[8,1,224,768]{3,2,1,0:T(8,128)(2,1)}, u32[]{:S(2)}, u32[]{:S(2)}) collective-permute-start(bf16[8,1,224,768]{3,2,1,0:T(8,128)(2,1)} %constant_dynamic-slice_fusion.2), channel_id=1, source_target_pairs={{0,16},{16,0},{1,17},{17,1},{2,18},{18,2},{3,19},{19,3},{4,20},{20... | collective-permute-start | bytes 8257544 | tf_op jit(solution)/shard_map/ppermute | solution.py:28
  341.6 3.0 collective-permute-start.19
  352.1 12.4 %collective-permute-start.25 = (bf16[2,2,1,2,56,576]{5,4,3,1,0,2:T(8,128)(2,1)}, bf16[2,2,1,2,56,576]{5,4,3,1,0,2:T(8,128)(2,1)}, u32[]{:S(2)}, u32[]{:S(2)}) collective-permute-start(bf16[2,2,1,2,56,576]{5,4,3,1,0,2:T(8,128)(2,1)} %fusion.39), channel_id=1, source_target_pairs={{0,1},{1,0},{2,3},{3,2},{4,5},{5,4},{6,7},{7,6},{8,9},{9,8},{10,11... | collective-permute-start | bytes 1548296 | tf_op jit(solution)/shard_map/ppermute | solution.py:28
  360.7 38.0 %collective-permute-start.22 = (bf16[2,2,192,384]{3,2,1,0:T(8,128)(2,1)S(1)}, bf16[2,2,192,384]{3,2,1,0:T(8,128)(2,1)S(1)}, u32[]{:S(2)}, u32[]{:S(2)}) collective-permute-start(bf16[2,2,192,384]{3,2,1,0:T(8,128)(2,1)S(1)} %fusion.34), channel_id=1, source_target_pairs={{0,4},{1,5},{2,6},{3,7},{4,0},{5,1},{6,2},{7,3},{8,12},{9,13},{10,... | collective-permute-start | bytes 1769480 | tf_op jit(solution)/shard_map/ppermute | solution.py:28
  363.0 38.4 %collective-permute-start.20 = (bf16[2,2,192,384]{3,2,0,1:T(8,128)(2,1)S(1)}, bf16[2,2,192,384]{3,2,0,1:T(8,128)(2,1)S(1)}, u32[]{:S(2)}, u32[]{:S(2)}) collective-permute-start(bf16[2,2,192,384]{3,2,0,1:T(8,128)(2,1)S(1)} %fusion.33), channel_id=1, source_target_pairs={{0,2},{1,3},{2,0},{3,1},{4,6},{5,7},{6,4},{7,5},{8,10},{9,11},{10,... | collective-permute-start | bytes 1769480 | tf_op jit(solution)/shard_map/ppermute | solution.py:28
  365.8 35.9 %collective-permute-start.26 = (bf16[2,2,56,576]{3,2,1,0:T(8,128)(2,1)S(1)}, bf16[2,2,56,576]{3,2,1,0:T(8,128)(2,1)S(1)}, u32[]{:S(2)}, u32[]{:S(2)}) collective-permute-start(bf16[2,2,56,576]{3,2,1,0:T(8,128)(2,1)S(1)} %fusion.44), channel_id=1, source_target_pairs={{0,8},{1,9},{2,10},{3,11},{4,12},{5,13},{6,14},{7,15},{8,0},{9,1},... | collective-permute-start | bytes 774152 | tf_op jit(solution)/shard_map/ppermute | solution.py:28
  399.0 11.1 %collective-permute-start.23 = (bf16[2,192,384]{2,1,0:T(8,128)(2,1)S(1)}, bf16[2,192,384]{2,1,0:T(8,128)(2,1)S(1)}, u32[]{:S(2)}, u32[]{:S(2)}) collective-permute-start(bf16[2,192,384]{2,1,0:T(8,128)(2,1)S(1)} %fusion.42), channel_id=1, source_target_pairs={{0,2},{1,3},{2,0},{3,1},{4,6},{5,7},{6,4},{7,5},{8,10},{9,11},{10,... | collective-permute-start | bytes 884744 | tf_op jit(solution)/shard_map/ppermute | solution.py:28
  401.6 10.7 %collective-permute-start.21 = (bf16[2,192,384]{2,1,0:T(8,128)(2,1)S(1)}, bf16[2,192,384]{2,1,0:T(8,128)(2,1)S(1)}, u32[]{:S(2)}, u32[]{:S(2)}) collective-permute-start(bf16[2,192,384]{2,1,0:T(8,128)(2,1)S(1)} %fusion.41), channel_id=1, source_target_pairs={{0,4},{1,5},{2,6},{3,7},{4,0},{5,1},{6,2},{7,3},{8,12},{9,13},{10,... | collective-permute-start | bytes 884744 | tf_op jit(solution)/shard_map/ppermute | solution.py:28
  401.8 13.0 %collective-permute-start.27 = (bf16[2,2,56,576]{3,2,1,0:T(8,128)(2,1)S(1)}, bf16[2,2,56,576]{3,2,1,0:T(8,128)(2,1)S(1)}, u32[]{:S(2)}, u32[]{:S(2)}) collective-permute-start(bf16[2,2,56,576]{3,2,1,0:T(8,128)(2,1)S(1)} %fusion.58), channel_id=1, source_target_pairs={{0,16},{16,0},{1,17},{17,1},{2,18},{18,2},{3,19},{19,3},{4,20},{20... | collective-permute-start | bytes 774152 | tf_op jit(solution)/shard_map/ppermute | solution.py:28
  413.2 36.2 %collective-permute-start.24 = (bf16[192,768]{1,0:T(8,128)(2,1)}, bf16[192,768]{1,0:T(8,128)(2,1)}, u32[]{:S(2)}, u32[]{:S(2)}) collective-permute-start(bf16[192,768]{1,0:T(8,128)(2,1)} %fusion.43), channel_id=1, source_target_pairs={{0,8},{1,9},{2,10},{3,11},{4,12},{5,13},{6,14},{7,15},{8,0},{9,1},... | collective-permute-start | bytes 884744 | tf_op jit(solution)/shard_map/ppermute | solution.py:28
  415.0 7.1 %collective-permute-start.30 = (bf16[56,576]{1,0:T(8,128)(2,1)S(1)}, bf16[56,576]{1,0:T(8,128)(2,1)S(1)}, u32[]{:S(2)}, u32[]{:S(2)}) collective-permute-start(bf16[56,576]{1,0:T(8,128)(2,1)S(1)} %get-tuple-element.95), channel_id=1, source_target_pairs={{0,6},{1,7},{2,4},{3,5},{4,2},{5,3},{6,0},{7,1},{8,14},{9,15},{10,... | collective-permute-start | bytes 193544 | tf_op jit(solution)/shard_map/ppermute | solution.py:28
  418.6 5.0 %collective-permute-start.29 = (bf16[56,576]{1,0:T(8,128)(2,1)S(1)}, bf16[56,576]{1,0:T(8,128)(2,1)S(1)}, u32[]{:S(2)}, u32[]{:S(2)}) collective-permute-start(bf16[56,576]{1,0:T(8,128)(2,1)S(1)} %get-tuple-element.96), channel_id=1, source_target_pairs={{0,4},{1,5},{2,6},{3,7},{4,0},{5,1},{6,2},{7,3},{8,12},{9,13},{10,... | collective-permute-start | bytes 193544 | tf_op jit(solution)/shard_map/ppermute | solution.py:28
  418.6 4.9 %collective-permute-start.28 = (bf16[56,576]{1,0:T(8,128)(2,1)S(1)}, bf16[56,576]{1,0:T(8,128)(2,1)S(1)}, u32[]{:S(2)}, u32[]{:S(2)}) collective-permute-start(bf16[56,576]{1,0:T(8,128)(2,1)S(1)} %get-tuple-element.97), channel_id=1, source_target_pairs={{0,2},{1,3},{2,0},{3,1},{4,6},{5,7},{6,4},{7,5},{8,10},{9,11},{10,... | collective-permute-start | bytes 193544 | tf_op jit(solution)/shard_map/ppermute | solution.py:28
  424.1 26.3 %copy-start.5 = (f32[384,768]{1,0:T(8,128)S(1)}, f32[384,768]{1,0:T(8,128)}, u32[]{:S(2)}) copy-start(f32[384,768]{1,0:T(8,128)} %get-tuple-element.45) | copy-start | bytes 3538948
  447.9 8.7 %collective-permute-start.34 = (bf16[224,768]{1,0:T(8,128)(2,1)}, bf16[224,768]{1,0:T(8,128)(2,1)S(1)}, u32[]{:S(2)}, u32[]{:S(2)}) collective-permute-start(bf16[224,768]{1,0:T(8,128)(2,1)} %bitcast.367), channel_id=1, source_target_pairs={{0,16},{16,0},{1,17},{17,1},{2,18},{18,2},{3,19},{19,3},{4,20},{20... | collective-permute-start | bytes 1032200 | tf_op jit(solution)/shard_map/ppermute | solution.py:28
  458.1 1.5 collective-permute-start.35
  (29 other events, 109.2 us)
Sparse Core Ops, SparseCore 0:
  32.8 75.9 all-gather.2
  356.5 91.4 reduce-scatter.1

commit v5 on v4

--- a/solution.py
+++ b/solution.py
@@ -164,50 +164,63 @@
         out_shape=[jax.ShapeDtypeStruct((n,W),BF16),jax.ShapeDtypeStruct((L,2*W),F32)],
         scratch_shapes=[pltpu.VMEM((NH,128,n),BF16),pltpu.VMEM((NH,n,128),BF16),pltpu.VMEM((NH,128,n),BF16),pltpu.VMEM((NH,n,128),BF16),
             pltpu.VMEM((NH,HEAD,n),F32),pltpu.VMEM((NH,bk,128),F32),pltpu.VMEM((NH,bk,128),F32)],
-        cost_estimate=pl.CostEstimate(flops=32*n*L*W, transcendentals=NH*n*L, bytes_accessed=4*n*L),
         name="attend_backward",
     )(q,kv,kb,cf,st,dc)
 
 
-def weight_grads_body(y_ref, dz_ref, a_ref, do_ref, ctx_ref, da_ref, vec_ref, out_ref, *, chips):
+def outer_grads_body(a_ref, do_ref, out_ref, *, chips):
+    width = do_ref.shape[1]
+    r_out = a_ref.shape[1] // chips
+    half = chips // 2
+    for j in range(2):
+        grad = t_dot(a_ref[:, j * width : (j + 1) * width], do_ref[...]).astype(BF16)
+        for q in range(half):
+            out_ref[j * half + q] = grad[q * r_out : (q + 1) * r_out]
+
+
+def outer_grads(a, do, chips):
+    width = do.shape[1]
+    return pl.pallas_call(
+        partial(outer_grads_body, chips=chips),
+        out_shape=jax.ShapeDtypeStruct((chips, a.shape[1] // chips, width), BF16),
+        cost_estimate=pl.CostEstimate(
+            flops=2 * a.shape[0] * a.shape[1] * width, transcendentals=0, bytes_accessed=7 * width * width * 2
+        ),
+        name="outer_grads",
+    )(a, do)
+
+
+def inner_grads_body(y_ref, dz_ref, ctx_ref, da_ref, do_ref, vec_ref, out_ref, *, chips):
     width = y_ref.shape[1]
     r_in, r_ctx = width // chips, ctx_ref.shape[1] // chips
-    r_out = a_ref.shape[1] // chips
     for j in range(2):
         grad = t_dot(y_ref[...], dz_ref[:, j * width : (j + 1) * width]).astype(BF16)
         for q in range(chips):
             out_ref[q, j * r_in : (j + 1) * r_in] = grad[q * r_in : (q + 1) * r_in]
-        grad = t_dot(a_ref[:, j * width : (j + 1) * width], do_ref[...]).astype(BF16)
-        half = chips // 2
-        for q in range(half):
-            out_ref[j * half + q, 2 * r_in : 2 * r_in + r_out] = grad[q * r_out : (q + 1) * r_out]
-    first = 2 * r_in + r_out
+    first = 2 * r_in
     grad = t_dot(ctx_ref[...], da_ref[...]).astype(BF16)
     for q in range(chips):
         out_ref[q, first : first + r_ctx] = grad[q * r_ctx : (q + 1) * r_ctx]
-    own = vec_ref.shape[0]
-    n = da_ref.shape[0] // 2
+    n = do_ref.shape[0]
     ones = jnp.ones((16, y_ref.shape[0]), BF16)
-    sums = [dot(ones[:, :n], da_ref[:n])[:1], dot(ones[:, :n], do_ref[:n])[:1]]
+    sums = [dot(ones[:, :n], da_ref[:n])[:1], dot(ones[:, :n], do_ref[...])[:1]]
     sums += [dot(ones, dz_ref[:, j * width : (j + 1) * width])[:1] for j in range(2)]
     small = jnp.concatenate([vec_ref[...]] + sums, axis=0).astype(BF16)
     for q in range(chips):
-        out_ref[q, first + r_ctx : first + r_ctx + own + 4] = small
-        out_ref[q, first + r_ctx + own + 4 :] = jnp.zeros((out_ref.shape[1] - first - r_ctx - own - 4, width), BF16)
-
-
-def weight_grads(y, dz, a, do, ctx, da, vec, chips, parts):
+        out_ref[q, first + r_ctx :] = small
+
+
+def inner_grads(y, dz, ctx, da, do, vec, chips):
     width = y.shape[1]
-    total = 2 * width // chips + a.shape[1] // chips + ctx.shape[1] // chips + vec.shape[0] + 4
-    total = -(-total // (16 * parts)) * 16 * parts
+    total = 2 * width // chips + ctx.shape[1] // chips + vec.shape[0] + 4
     return pl.pallas_call(
-        partial(weight_grads_body, chips=chips),
+        partial(inner_grads_body, chips=chips),
         out_shape=jax.ShapeDtypeStruct((chips, total, width), BF16),
         cost_estimate=pl.CostEstimate(
-            flops=2 * width * (y.shape[0] * (2 * dz.shape[1] + ctx.shape[1])), transcendentals=0, bytes_accessed=15 * width * width * 2
+            flops=2 * width * y.shape[0] * (dz.shape[1] + ctx.shape[1]), transcendentals=0, bytes_accessed=8 * width * width * 2
         ),
-        name="weight_grads",
-    )(y, dz, a, do, ctx, da, vec)
+        name="inner_grads",
+    )(y, dz, ctx, da, do, vec)
 
 
 def per_device(
@@ -251,6 +264,20 @@
     def sflip(value, mask):
         return flip(value, "seq", seq_size, mask)
 
+    chips = seq_size // 2
+    x_mine = pick(tokens, z1)
+    x_sent = pick(tokens, 1 - z1)
+    half_width = width // 2
+    x_theirs = sflip(x_sent, HI)
+    x_pair = in_order(x_mine, x_theirs, z1)
+    xa, xb = x_pair[:, :, :half_width], x_pair[:, :, half_width:]
+    ra, rb = sflip(xa, YO), sflip(xb, ZO)
+    xa, xb = in_order(xa, ra, y0), in_order(xb, rb, z0)
+    ra, rb = sflip(xa, ZO), sflip(xb, YO)
+    xa, xb = in_order(xa, ra, z0), in_order(xb, rb, y0)
+    x_all = jnp.concatenate([xa.transpose(2, 0, 1, 3, 4), xb.transpose(2, 1, 0, 3, 4)], axis=-1)
+    x_all = x_all.reshape(8 * rows, width)
+
     core = me % 2
     chips = seq_size // 2
     piece = feed // seq_size
@@ -280,18 +307,6 @@
         theirs = flip(gathered, "grp", grp_size, 1 << b)
         gathered = in_order(gathered, theirs, (grp >> b) % 2).reshape((-1,) + packed.shape)
 
-    x_mine = pick(tokens, z1)
-    x_sent = pick(tokens, 1 - z1)
-    half_width = width // 2
-    x_pair = in_order(x_mine, sflip(x_sent, HI), z1)
-    xa, xb = x_pair[:, :, :half_width], x_pair[:, :, half_width:]
-    ra, rb = sflip(xa, YO), sflip(xb, ZO)
-    xa, xb = in_order(xa, ra, y0), in_order(xb, rb, z0)
-    ra, rb = sflip(xa, ZO), sflip(xb, YO)
-    xa, xb = in_order(xa, ra, z0), in_order(xb, rb, y0)
-    x_all = jnp.concatenate([xa.transpose(2, 0, 1, 3, 4), xb.transpose(2, 1, 0, 3, 4)], axis=-1)
-    x_all = x_all.reshape(8 * rows, width)
-
     smalls = jnp.concatenate(
         [query_bias, value_bias, output_bias, first_gain, first_shift, outer_bias, second_gain, second_shift, inner_bias]
     )
@@ -301,6 +316,7 @@
     small_block = jnp.zeros((small_rows * 3 * GROUP_WIDTH,), bf16).at[: smalls.shape[0]].set(smalls)
     small_block = jnp.broadcast_to(small_block.reshape(1, small_rows, -1), (HEAD_GROUPS, small_rows, 3 * GROUP_WIDTH))
     grouped = jnp.concatenate([grouped, small_block], axis=1)
+    grouped, _ = lax.optimization_barrier((grouped, x_theirs))
 
     def group_block(k):
         return lax.dynamic_index_in_dim(grouped, head_group ^ k, 0, keepdims=False)
@@ -397,6 +413,17 @@
     dhidden_two, dsecond_gain, dsecond_shift = norm_back_two(cotangent.astype(jnp.float32))
     douter = dhidden_two.astype(bf16)
     both_douter = jnp.concatenate([douter, sflip(douter, 1)], axis=0)
+
+    def over_chips(blocks):
+        return lax.psum_scatter(blocks, "seq", scatter_dimension=0, tiled=False, axis_index_groups=chip_groups)
+
+    def over_groups(blocks):
+        for b in range(log2_of(grp_size)):
+            blocks = (blocks.astype(jnp.float32) + flip(blocks, "grp", grp_size, 1 << b).astype(jnp.float32)).astype(bf16)
+        return blocks
+
+    outer_blocks, both_douter = lax.optimization_barrier((outer_grads(active, both_douter, chips), both_douter))
+    outer_sums = over_chips(outer_blocks)
     dinner = (dot_t(both_douter, outer_all) * slope).astype(bf16)
     dfirst_part = dot_t(dinner, inner_all)
     dfirst = dhidden_two + dfirst_part[:n_own] + sflip(dfirst_part[n_own:].astype(bf16), 1).astype(jnp.float32)
@@ -412,31 +439,9 @@
     both_ctx = jnp.concatenate([pick(ctx_split, core), sflip(pick(ctx_split, 1 - core), 1)], axis=0)
     both_dattend = jnp.concatenate([dattend, sflip(dattend, 1)], axis=0)
     vectors = jnp.stack([dfirst_gain, dfirst_shift, dsecond_gain, dsecond_shift])
-    grads = weight_grads(both_first, dinner, active, both_douter, both_ctx, both_dattend, vectors, chips, grp_size)
-    grads = grads.reshape(chips, grp_size, -1, width)
-    for b in reversed(range(log2_of(grp_size))):
-        bit = (grp >> b) % 2
-        n_half = grads.shape[1] // 2
-        kept, sent = (lax.dynamic_slice_in_dim(grads, n_half * i, n_half, axis=1) for i in (bit, 1 - bit))
-        grads = (kept.astype(jnp.float32) + flip(sent, "grp", grp_size, 1 << b).astype(jnp.float32)).astype(bf16)
-    grads = lax.psum_scatter(grads[:, 0], "seq", scatter_dimension=0, tiled=False, axis_index_groups=chip_groups)
-    for b in range(log2_of(grp_size)):
-        grads = in_order(grads, flip(grads, "grp", grp_size, 1 << b), (grp >> b) % 2).reshape(-1, width)
-    r1 = 4 * out_rows
-    r2 = r1 + piece
-    r3 = r2 + out_rows
-    inner_grad = grads[:r1].reshape(2, 2, out_rows, width)
-    inner_grad = [inner_grad[:, i] for i in range(2)]
-    far = sflip(jnp.concatenate([pick(inner_grad, 1 - core).reshape(2 * out_rows, width), grads[r3 : r3 + 8]], axis=0), 1)
-    dinner_weight = in_order(pick(inner_grad, core), far[: 2 * out_rows].reshape(2, out_rows, width), core)
-    dinner_weight = dinner_weight.transpose(2, 0, 1, 3).reshape(out_rows, 2, chips, piece).transpose(0, 2, 1, 3)
-    dinner_weight = dinner_weight.reshape(out_rows, feed).astype(jnp.float32)
-    douter_weight = grads[r1:r2].astype(jnp.float32)
-    doutput_weight = grads[r2:r3].astype(jnp.float32)
-    small = grads[r3 : r3 + 8].astype(jnp.float32)
-    both = lax.dynamic_slice_in_dim(small + far[2 * out_rows :].astype(jnp.float32), me * out_rows, out_rows, axis=1)
-    dfirst_gain, dfirst_shift, dsecond_gain, dsecond_shift, doutput_bias, douter_bias = (both[i] for i in range(6))
-    dinner_bias = lax.dynamic_slice_in_dim(small[6:8].reshape(half_feed), (me // 2) * piece, piece)
+    inner_blocks = inner_grads(both_first, dinner, both_ctx, both_dattend, douter, vectors, chips)
+    inner_blocks, dcontext = lax.optimization_barrier((inner_blocks, dcontext))
+    inner_sums = over_chips(inner_blocks)
 
     dqueries, dkv = attend_backward(queries, kv, key_tail, context_full, stats, dcontext)
     dkv = dkv.reshape(n_parts, 8 * rows, 2 * GROUP_WIDTH)
@@ -448,6 +453,8 @@
         dkv = jnp.where(bit == 0, low, high) + sflip(sent, b).astype(jnp.float32)
     dqkv = jnp.concatenate([dqueries, dkv[0].astype(bf16)], axis=1)
 
+    dqkv, outer_sums, inner_sums = lax.optimization_barrier((dqkv, outer_sums, inner_sums))
+
     dx = dot_t(dqkv, w_all).reshape(2, 2, 2, rows, width)
     da, db = dx[..., :half_width], dx[..., half_width:]
 
@@ -463,6 +470,22 @@
     mine = pick(dx, z1)
     theirs = sflip(pick(dx, 1 - z1).astype(bf16), HI).astype(jnp.float32)
     dtokens = dhidden_one.reshape(2, rows, width) + in_order(mine, theirs, z1)
+
+    grads = over_groups(inner_sums)
+    douter_weight = over_groups(outer_sums).astype(jnp.float32)
+    r1 = 4 * out_rows
+    r3 = r1 + out_rows
+    inner_grad = grads[:r1].reshape(2, 2, out_rows, width)
+    inner_grad = [inner_grad[:, i] for i in range(2)]
+    far = sflip(jnp.concatenate([pick(inner_grad, 1 - core).reshape(2 * out_rows, width), grads[r3 : r3 + 8]], axis=0), 1)
+    dinner_weight = in_order(pick(inner_grad, core), far[: 2 * out_rows].reshape(2, out_rows, width), core)
+    dinner_weight = dinner_weight.transpose(2, 0, 1, 3).reshape(out_rows, 2, chips, piece).transpose(0, 2, 1, 3)
+    dinner_weight = dinner_weight.reshape(out_rows, feed).astype(jnp.float32)
+    doutput_weight = grads[r1:r3].astype(jnp.float32)
+    small = grads[r3 : r3 + 8].astype(jnp.float32)
+    both = lax.dynamic_slice_in_dim(small + far[2 * out_rows :].astype(jnp.float32), me * out_rows, out_rows, axis=1)
+    dfirst_gain, dfirst_shift, dsecond_gain, dsecond_shift, doutput_bias, douter_bias = (both[i] for i in range(6))
+    dinner_bias = lax.dynamic_slice_in_dim(small[6:8].reshape(half_feed), (me // 2) * piece, piece)
 
     dw = t_dot(x_all, dqkv)
     dbias = column_sums(dqkv)

time: 475 us -> 449 us (0.945)
  waiting for transfers between devices: 169 us -> 156 us
  matrix products: 45.8 us -> 35.1 us
  local copies, waits for them, and re-layouts: 48.5 us -> 41.9 us
    ppermute x35, waiting for transfers between devices: 127 us -> 87.4 us  [flip(): return lax.ppermute(value, axis, [(i, i ^ mask) for i in range(size)])]
    reduce_scatter x1 -> x2, waiting for transfers between devices: 21.6 us -> 45.3 us  [over_chips(): lax.psum_scatter(blocks, 'seq', scatter_dimension=0, tiled=False, axis_in...]
    dot_general x4, matrix products: 30.4 us -> 20.5 us  [dot(): return jnp.dot(left, right, preferred_element_type=jnp.float32)]
    concatenate x1, local copies, waits for them, and re-layouts: 6.13 us -> 0.1 us  [per_device(): jnp.concatenate([query_bias, value_bias, output_bias, first_gain, first_s...]
    unnamed x74 -> x100, local copies, waits for them, and re-layouts: 6.07 us -> 9.82 us
    pallas_call x1 -> x2, Pallas kernels: 10.6 us -> 12.7 us  [the longest x1 7.23 us: inner_grads(): pl.pallas_call(partial(inner_grads_body, chips=chips), out_shape=jax.Shap...]
  transfers between devices with their start and end apart: 40 -> 41, of which waited for: 18 -> 24; matrix products, arithmetic and copies ran while one was open for 16% -> 19% of each run, Pallas kernels for 18% -> 19%
where the time goes in v5:
time: 449 us; the launch traced here: 440 us
  waiting for transfers between devices  156 us (35%)
  Pallas kernels  87.5 us (19%)
  other arithmetic  54.9 us (12%)
  starting transfers between devices  47.9 us (11%)
  local copies, waits for them, and re-layouts  41.9 us (9%)
  matrix products  35.1 us (8%)
  between operations  16.9 us (4%)
    ppermute x35, waiting for transfers between devices, flip(): return lax.ppermute(value, axis, [(i, i ^ mask) for i in range(size)])  87.4 us
    pallas_call x1, Pallas kernels, attend_backward(): pl.pallas_call(partial(bwd_body, bk=bk, nk=nk), grid=(nk, NH), in_specs=[...  46.5 us
    reduce_scatter x2, waiting for transfers between devices, over_chips(): lax.psum_scatter(blocks, 'seq', scatter_dimension=0, tiled=False, axis_in...  45.3 us
    ppermute x35, starting transfers between devices, flip(): return lax.ppermute(value, axis, [(i, i ^ mask) for i in range(size)])  38.1 us
    pallas_call x1, Pallas kernels, attend_forward(): pl.pallas_call(partial(fwd_body, bq=bq), grid=(n // bq, NH), in_specs=[pl...  28.3 us
    all_to_all x2, waiting for transfers between devices, exchange(): lax.all_to_all(blocks, 'seq', 0, 0, axis_index_groups=teams, tiled=True)  23.1 us
    dot_general x4, matrix products, dot(): return jnp.dot(left, right, preferred_element_type=jnp.float32)  20.5 us
    dot_general x4, matrix products, dot_t(): lax.dot_general(left, right, (((1,), (1,)), ((), ())), preferred_element_...  12.5 us
  transfers between devices with their start and end apart: 41, of which 24 were waited for; matrix products, arithmetic and copies ran while one was open for 19% of the time, Pallas kernels for 19%

profile of v5, /device:TPU:0, one launch (start us, length us, event | category | flops | bytes accessed | tf_op | source)
XLA Modules:
  0.0 440.0 jit_solution(4717149297684780606)
XLA Ops:
  10.8 3.6 collective-permute-start.12
  14.4 2.7 collective-permute-start
  22.1 8.5 %collective-permute-done = bf16[192,768]{1,0:T(8,128)(2,1)S(1)} collective-permute-done((bf16[192,768]{1,0:T(8,128)(2,1)S(1)}, bf16[192,768]{1,0:T(8,128)(2,1)S(1)}, u32[]{:S(2)}, u32[]{:S(2)}) %collective-permute-start) | collective-permute-done | bytes 294944 | tf_op jit(solution)/shard_map/ppermute | solution.py:28
  34.4 2.1 collective-permute-start.3
  37.9 2.4 collective-permute-done.6
  42.1 10.6 %collective-permute-done.8 = bf16[2,2,32,576]{3,2,1,0:T(8,128)(2,1)S(1)} collective-permute-done((bf16[2,2,32,576]{3,2,1,0:T(8,128)(2,1)S(1)}, bf16[2,2,32,576]{3,2,1,0:T(8,128)(2,1)S(1)}, u32[]{:S(2)}, u32[]{:S(2)}) %collective-permute-start.8) | collective-permute-done | bytes 147488 | tf_op jit(solution)/shard_map/ppermute | solution.py:28
  54.8 4.4 %collective-permute-start.2 = (bf16[2,2,192,384]{3,2,1,0:T(8,128)(2,1)S(1)}, bf16[2,2,192,384]{3,2,1,0:T(8,128)(2,1)S(1)}, u32[]{:S(2)}, u32[]{:S(2)}) collective-permute-start(bf16[2,2,192,384]{3,2,1,0:T(8,128)(2,1)S(1)} %maximum_select_fusion.9), channel_id=1, source_target_pairs={{0,4},{1,5},{2,6},{3,7},{4,0},{5,1},{6,2},{7,3},{8,12},{9,13},{10,... | collective-permute-start | bytes 1769480 | tf_op jit(solution)/shard_map/ppermute | solution.py:28
  62.3 24.5 %collective-permute-done.2 = bf16[2,2,192,384]{3,2,1,0:T(8,128)(2,1)S(1)} collective-permute-done((bf16[2,2,192,384]{3,2,1,0:T(8,128)(2,1)S(1)}, bf16[2,2,192,384]{3,2,1,0:T(8,128)(2,1)S(1)}, u32[]{:S(2)}, u32[]{:S(2)}) %collective-permute-start.2) | collective-permute-done | bytes 589856 | tf_op jit(solution)/shard_map/ppermute | solution.py:28
  92.3 3.2 convolution_add_fusion
  95.5 1.9 copy-done.19
  99.8 2.5 fusion.9.q_ref
  104.1 28.3 %attend_forward.1 = (bf16[1536,192]{1,0:T(8,128)(2,1)}, f32[1536,192]{1,0:T(8,128)}, f32[1536,128]{1,0:T(8,128)}) custom-call(bf16[1536,192]{1,0:T(8,128)(2,1)} %fusion.9.q_ref, bf16[3072,384]{1,0:T(8,128)(2,1)} %bitcast.309, bf16[3072,128]{1,0:T(8,128)(2,1)} %select_convert_fusion.1.kb_ref), custom_call_target="tpu_custom_call" | custom-call | flops 14495514624 | bytes 18874368 | tf_op jit(solution)/shard_map/attend_forward/pallas_call | solution.py:103
  132.4 4.3 all-to-all-start
  137.1 19.8 %all-to-all-done = bf16[8,192,192]{2,1,0:T(8,128)(2,1)S(1)} async-done(((bf16[8,192,192]{2,1,0:T(8,128)(2,1)}), bf16[8,192,192]{2,1,0:T(8,128)(2,1)S(1)}, u32[]{:S(2)}, u32[]{:S(2)}) %all-to-all-start) | async-done | bytes 589856 | tf_op jit(solution)/shard_map/all_to_all | solution.py:381
  158.1 7.8 %collective-permute-done.14 = bf16[8,240,768]{2,1,0:T(8,128)(2,1)} collective-permute-done((bf16[8,240,768]{2,1,0:T(8,128)(2,1)}, bf16[8,240,768]{2,1,0:T(8,128)(2,1)}, u32[]{:S(2)}, u32[]{:S(2)}) %collective-permute-start.14) | collective-permute-done | bytes 2949152 | tf_op jit(solution)/shard_map/ppermute | solution.py:28
  165.9 5.5 %maximum_select_fusion = bf16[2,8,240,768]{3,2,1,0:T(8,128)(2,1)S(1)} fusion(bf16[1,8,240,768]{3,2,1,0:T(8,128)(2,1)} %bitcast.58, bf16[1,8,240,768]{3,2,1,0:T(8,128)(2,1)} %bitcast.324, pred[]{:T(512)S(6)} %eq.41), kind=kLoop, calls=%fused_computation.1 | loop fusion | flops 8847360 | bytes 11796481 | tf_op jit(solution)/shard_map/jit(_where)/select_n | solution.py:32
  171.4 2.0 fusion.72
  177.1 2.0 slice.342
  179.4 14.6 %multiply_convert_fusion.1 = (bf16[768,1536]{1,0:T(8,128)(2,1)S(1)}, f32[768,1536]{1,0:T(8,128)}, f32[768,1536]{1,0:T(8,128)}) fusion(f32[1536]{0:T(1024)S(1)} %select_n.763, bf16[768,768]{1,0:T(8,128)(2,1)S(1)} %bitcast.335, bf16[768,768]{1,0:T(8,128)(2,1)S(1)} %bitcast.337, bf16[384,768]{1,0:T(8,128)(2,1)S(1)} %collective-permute-done.15, ...), kind=kOutput, calls=%fused_computation.4 | convolution fusion | flops 1896873984 | bytes 15341568 | tf_op jit(solution)/shard_map/dot_general | solution.py:46
  194.1 2.0 fusion.80
  207.2 5.4 %outer_grads.1 = bf16[8,192,768]{2,1,0:T(8,128)(2,1)} custom-call(bf16[768,1536]{1,0:T(8,128)(2,1)} %copy-done.49, bf16[768,768]{1,0:T(8,128)(2,1)} %pad_maximum_fusion.7.do_ref), custom_call_target="tpu_custom_call" | custom-call | flops 1811939328 | bytes 8257536 | tf_op jit(solution)/shard_map/outer_grads/pallas_call | solution.py:183
  212.7 7.8 %multiply_convert_fusion.dz_ref = bf16[768,1536]{1,0:T(8,128)(2,1)S(1)} fusion(f32[768,1536]{1,0:T(8,128)} %get-tuple-element.70, f32[768,1536]{1,0:T(8,128)} %get-tuple-element.128, bf16[768,768]{1,0:T(8,128)(2,1)} %pad_maximum_fusion.7.do_ref, bf16[1536,768]{1,0:T(8,128)(2,1)} %bitcast.326, f32[1536]{0:T(1024)S(1)} %select_n.763), kind=kOutput, calls=%fused_computation.3 | convolution fusion | flops 1827274752 | bytes 15341568 | tf_op jit(solution)/shard_map/dot_general | solution.py:50
  220.5 2.0 fusion.10
  224.5 1.9 copy.121
  226.4 3.2 reshape_reshape.3
  229.6 2.2 multiply_reduce_fusion
  236.3 3.7 all-to-all-start.1
  240.9 1.9 copy.122
  244.7 1.8 pad_maximum_fusion.10.ctx_ref
  248.3 2.2 pad_maximum_fusion.8.da_ref
  250.5 7.2 %inner_grads.1 = bf16[8,248,768]{2,1,0:T(8,128)(2,1)} custom-call(bf16[768,768]{1,0:T(8,128)(2,1)} %pad_maximum_fusion.6.y_ref, bf16[768,1536]{1,0:T(8,128)(2,1)} %copy-done.13, bf16[768,384]{1,0:T(8,128)(2,1)} %pad_maximum_fusion.10.ctx_ref, bf16[768,768]{1,0:T(8,128)(2,1)} %pad_maximum_fusion.8.da_ref, bf16[384,768]{1,0:T(8,128)(2,1)} %copy-done.8, ...), custom_call_target="tpu_custom_call" | custom-call | flops 2264924160 | bytes 9437184 | tf_op jit(solution)/shard_map/inner_grads/pallas_call | solution.py:216
  257.7 3.4 all-to-all-done.1
  261.9 46.5 %attend_backward.1 = (bf16[1536,192]{1,0:T(8,128)(2,1)}, f32[3072,384]{1,0:T(8,128)}) custom-call(bf16[1536,192]{1,0:T(8,128)(2,1)} %fusion.9.q_ref, bf16[3072,384]{1,0:T(8,128)(2,1)} %bitcast.310, bf16[3072,128]{1,0:T(8,128)(2,1)} %select_convert_fusion.1.kb_ref, f32[1536,192]{1,0:T(8,128)} %get-tuple-element.45.cf_ref, ...), custom_call_target="tpu_custom_call" | custom-call | tf_op jit(solution)/shard_map/attend_backward/pallas_call | solution.py:160
  308.4 3.9 fusion.14
  312.3 2.6 copy.136
  315.4 2.8 fusion.15
  319.1 45.2 %reduce-scatter.5.cloned.1.call-done = bf16[1,248,768]{2,1,0:T(8,128)(2,1)} async-done(((bf16[8,248,768]{2,1,0:T(8,128)(2,1)}), bf16[1,248,768]{2,1,0:T(8,128)(2,1)}) %reduce-scatter.5.cloned.1.call-update) | async-done | bytes 380944 | tf_op jit(solution)/shard_map/reduce_scatter | solution.py:418
  364.7 2.1 fusion.81
  370.7 2.0 fusion.7
  379.4 3.3 collective-permute-done.35
  383.6 4.9 %collective-permute-done.33 = bf16[248,768]{1,0:T(8,128)(2,1)S(1)} collective-permute-done((bf16[248,768]{1,0:T(8,128)(2,1)S(1)}, bf16[248,768]{1,0:T(8,128)(2,1)S(1)}, u32[]{:S(2)}, u32[]{:S(2)}) %collective-permute-start.33) | collective-permute-done | bytes 380960 | tf_op jit(solution)/shard_map/ppermute | solution.py:28
  391.7 2.2 collective-permute-start.28
  397.7 2.1 fusion.25
  403.4 4.8 %collective-permute-done.28 = bf16[2,2,56,576]{3,2,1,0:T(8,128)(2,1)S(1)} collective-permute-done((bf16[2,2,56,576]{3,2,1,0:T(8,128)(2,1)S(1)}, bf16[2,2,56,576]{3,2,1,0:T(8,128)(2,1)S(1)}, u32[]{:S(2)}, u32[]{:S(2)}) %collective-permute-start.28) | collective-permute-done | bytes 258080 | tf_op jit(solution)/shard_map/ppermute | solution.py:28
  409.9 4.5 %collective-permute-done.23 = bf16[2,192,384]{2,1,0:T(8,128)(2,1)S(1)} collective-permute-done((bf16[2,192,384]{2,1,0:T(8,128)(2,1)S(1)}, bf16[2,192,384]{2,1,0:T(8,128)(2,1)S(1)}, u32[]{:S(2)}, u32[]{:S(2)}) %collective-permute-start.23) | collective-permute-done | bytes 294944 | tf_op jit(solution)/shard_map/ppermute | solution.py:28
  416.8 2.3 collective-permute-start.32
  420.5 4.0 collective-permute-done.32
  428.2 2.9 collective-permute-done.26
  (333 shorter events, 91.7 us)
Async XLA Ops:
  7.2 12.0 %copy-start.47 = (bf16[24]{0:T(256)(128)(2,1)S(1)}, bf16[24]{0:T(256)(128)(2,1)}, u32[]{:S(2)}) copy-start(bf16[24]{0:T(256)(128)(2,1)} %param.36) | copy-start | bytes 148
  7.2 11.9 %copy-start.46 = (bf16[24]{0:T(256)(128)(2,1)S(1)}, bf16[24]{0:T(256)(128)(2,1)}, u32[]{:S(2)}) copy-start(bf16[24]{0:T(256)(128)(2,1)} %param.35) | copy-start | bytes 148
  7.2 11.9 %copy-start.45 = (bf16[24]{0:T(256)(128)(2,1)S(1)}, bf16[24]{0:T(256)(128)(2,1)}, u32[]{:S(2)}) copy-start(bf16[24]{0:T(256)(128)(2,1)} %param.34) | copy-start | bytes 148
  7.3 12.1 %copy-start.36 = (bf16[24,768]{1,0:T(8,128)(2,1)S(1)}, bf16[24,768]{1,0:T(8,128)(2,1)}, u32[]{:S(2)}) copy-start(bf16[24,768]{1,0:T(8,128)(2,1)} %param.22) | copy-start | bytes 110596
  7.3 92.0 %all-gather.3.cloned.1.call-start = ((), (), s32[]{:S(2)}) async-start(), calls=%async_computation.6 | async-start | bytes 3317760 | tf_op jit(solution)/shard_map/all_gather | solution.py:305
  7.4 13.9 %collective-permute-start.13 = (bf16[96,768]{1,0:T(8,128)(2,1)}, bf16[96,768]{1,0:T(8,128)(2,1)S(1)}, u32[]{:S(2)}, u32[]{:S(2)}) collective-permute-start(bf16[96,768]{1,0:T(8,128)(2,1)} %param.33), channel_id=1, source_target_pairs={{0,0},{1,2},{2,1},{3,3},{4,4},{5,6},{6,5},{7,7},{8,8},{9,10},{10,9... | collective-permute-start | bytes 442376 | tf_op jit(solution)/shard_map/ppermute | solution.py:290
  10.8 10.1 %collective-permute-start.12 = (bf16[72,768]{1,0:T(8,128)(2,1)S(1)}, bf16[72,768]{1,0:T(8,128)(2,1)S(1)}, u32[]{:S(2)}, u32[]{:S(2)}) collective-permute-start(bf16[72,768]{1,0:T(8,128)(2,1)S(1)} %pad_maximum_fusion.14), channel_id=1, source_target_pairs={{0,1},{1,0},{2,3},{3,2},{4,5},{5,4},{6,7},{7,6},{8,9},{9,8},{10,11... | collective-permute-start | bytes 331784 | tf_op jit(solution)/shard_map/ppermute | solution.py:28
  14.4 16.2 %collective-permute-start = (bf16[192,768]{1,0:T(8,128)(2,1)S(1)}, bf16[192,768]{1,0:T(8,128)(2,1)S(1)}, u32[]{:S(2)}, u32[]{:S(2)}) collective-permute-start(bf16[192,768]{1,0:T(8,128)(2,1)S(1)} %get-tuple-element.86), channel_id=1, source_target_pairs={{0,8},{1,9},{2,10},{3,11},{4,12},{5,13},{6,14},{7,15},{8,0},{9,1},... | collective-permute-start | bytes 884744 | tf_op jit(solution)/shard_map/ppermute | solution.py:28
  30.6 7.2 %collective-permute-start.7 = (bf16[32,576]{1,0:T(8,128)(2,1)S(1)}, bf16[32,576]{1,0:T(8,128)(2,1)S(1)}, u32[]{:S(2)}, u32[]{:S(2)}) collective-permute-start(bf16[32,576]{1,0:T(8,128)(2,1)S(1)} %get-tuple-element.115), channel_id=1, source_target_pairs={{0,6},{1,7},{2,4},{3,5},{4,2},{5,3},{6,0},{7,1},{8,14},{9,15},{10,... | collective-permute-start | bytes 110600 | tf_op jit(solution)/shard_map/ppermute | solution.py:28
  31.2 9.1 %collective-permute-start.6 = (bf16[32,576]{1,0:T(8,128)(2,1)S(1)}, bf16[32,576]{1,0:T(8,128)(2,1)S(1)}, u32[]{:S(2)}, u32[]{:S(2)}) collective-permute-start(bf16[32,576]{1,0:T(8,128)(2,1)S(1)} %get-tuple-element.116), channel_id=1, source_target_pairs={{0,4},{1,5},{2,6},{3,7},{4,0},{5,1},{6,2},{7,3},{8,12},{9,13},{10,... | collective-permute-start | bytes 110600 | tf_op jit(solution)/shard_map/ppermute | solution.py:28
  32.8 4.2 collective-permute-start.5
  34.4 24.7 %collective-permute-start.3 = (bf16[2,192,384]{2,1,0:T(8,128)(2,1)S(1)}, bf16[2,192,384]{2,1,0:T(8,128)(2,1)S(1)}, u32[]{:S(2)}, u32[]{:S(2)}) collective-permute-start(bf16[2,192,384]{2,1,0:T(8,128)(2,1)S(1)} %get-tuple-element.83), channel_id=1, source_target_pairs={{0,4},{1,5},{2,6},{3,7},{4,0},{5,1},{6,2},{7,3},{8,12},{9,13},{10,... | collective-permute-start | bytes 884744 | tf_op jit(solution)/shard_map/ppermute | solution.py:28
  36.5 18.1 %collective-permute-start.1 = (bf16[2,192,384]{2,1,0:T(8,128)(2,1)S(1)}, bf16[2,192,384]{2,1,0:T(8,128)(2,1)S(1)}, u32[]{:S(2)}, u32[]{:S(2)}) collective-permute-start(bf16[2,192,384]{2,1,0:T(8,128)(2,1)S(1)} %get-tuple-element.84), channel_id=1, source_target_pairs={{0,2},{1,3},{2,0},{3,1},{4,6},{5,7},{6,4},{7,5},{8,10},{9,11},{10,... | collective-permute-start | bytes 884744 | tf_op jit(solution)/shard_map/ppermute | solution.py:28
  40.3 12.3 %collective-permute-start.8 = (bf16[2,2,32,576]{3,2,1,0:T(8,128)(2,1)S(1)}, bf16[2,2,32,576]{3,2,1,0:T(8,128)(2,1)S(1)}, u32[]{:S(2)}, u32[]{:S(2)}) collective-permute-start(bf16[2,2,32,576]{3,2,1,0:T(8,128)(2,1)S(1)} %maximum_select_fusion.16), channel_id=1, source_target_pairs={{0,8},{1,9},{2,10},{3,11},{4,12},{5,13},{6,14},{7,15},{8,0},{9,1},... | collective-permute-start | bytes 442376 | tf_op jit(solution)/shard_map/ppermute | solution.py:28
  52.7 9.0 %collective-permute-start.9 = (bf16[2,2,2,32,576]{4,3,2,1,0:T(8,128)(2,1)S(1)}, bf16[2,2,2,32,576]{4,3,2,1,0:T(8,128)(2,1)S(1)}, u32[]{:S(2)}, u32[]{:S(2)}) collective-permute-start(bf16[2,2,2,32,576]{4,3,2,1,0:T(8,128)(2,1)S(1)} %maximum_select_fusion.13), channel_id=1, source_target_pairs={{0,16},{16,0},{1,17},{17,1},{2,18},{18,2},{3,19},{19,3},{4,20},{20... | collective-permute-start | bytes 884744 | tf_op jit(solution)/shard_map/ppermute | solution.py:28
  54.8 32.0 %collective-permute-start.2 = (bf16[2,2,192,384]{3,2,1,0:T(8,128)(2,1)S(1)}, bf16[2,2,192,384]{3,2,1,0:T(8,128)(2,1)S(1)}, u32[]{:S(2)}, u32[]{:S(2)}) collective-permute-start(bf16[2,2,192,384]{3,2,1,0:T(8,128)(2,1)S(1)} %maximum_select_fusion.9), channel_id=1, source_target_pairs={{0,4},{1,5},{2,6},{3,7},{4,0},{5,1},{6,2},{7,3},{8,12},{9,13},{10,... | collective-permute-start | bytes 1769480 | tf_op jit(solution)/shard_map/ppermute | solution.py:28
  59.3 28.3 %collective-permute-start.4 = (bf16[2,2,192,384]{3,2,1,0:T(8,128)(2,1)S(1)}, bf16[2,2,192,384]{3,2,1,0:T(8,128)(2,1)S(1)}, u32[]{:S(2)}, u32[]{:S(2)}) collective-permute-start(bf16[2,2,192,384]{3,2,1,0:T(8,128)(2,1)S(1)} %maximum_select_fusion.11), channel_id=1, source_target_pairs={{0,2},{1,3},{2,0},{3,1},{4,6},{5,7},{6,4},{7,5},{8,10},{9,11},{10,... | collective-permute-start | bytes 1769480 | tf_op jit(solution)/shard_map/ppermute | solution.py:28
  61.9 26.3 %collective-permute-start.10 = (bf16[2,2,2,2,32,576]{5,4,3,2,1,0:T(8,128)(2,1)S(1)}, bf16[2,2,2,2,32,576]{5,4,3,2,1,0:T(8,128)(2,1)S(1)}, u32[]{:S(2)}, u32[]{:S(2)}) collective-permute-start(bf16[2,2,2,2,32,576]{5,4,3,2,1,0:T(8,128)(2,1)S(1)} %maximum_select_fusion.7), channel_id=1, source_target_pairs={{0,1},{1,0},{2,3},{3,2},{4,5},{5,4},{6,7},{7,6},{8,9},{9,8},{10,11... | collective-permute-start | bytes 1769480 | tf_op jit(solution)/shard_map/ppermute | solution.py:28
  97.9 4.4 %collective-permute-start.11 = (bf16[1,1536,384]{2,1,0:T(8,128)(2,1)S(1)}, bf16[1,1536,384]{2,1,0:T(8,128)(2,1)S(1)}, u32[]{:S(2)}, u32[]{:S(2)}) collective-permute-start(bf16[1,1536,384]{2,1,0:T(8,128)(2,1)S(1)} %fusion.16), channel_id=1, source_target_pairs={{0,1},{1,0},{2,3},{3,2},{4,5},{5,4},{6,7},{7,6},{8,9},{9,8},{10,11... | collective-permute-start | bytes 3538952 | tf_op jit(solution)/shard_map/ppermute | solution.py:28
  99.3 66.6 %collective-permute-start.14 = (bf16[8,240,768]{2,1,0:T(8,128)(2,1)}, bf16[8,240,768]{2,1,0:T(8,128)(2,1)}, u32[]{:S(2)}, u32[]{:S(2)}) collective-permute-start(bf16[8,240,768]{2,1,0:T(8,128)(2,1)} %bitcast.323), channel_id=1, source_target_pairs={{0,16},{16,0},{1,17},{17,1},{2,18},{18,2},{3,19},{19,3},{4,20},{20... | collective-permute-start | bytes 8847368 | tf_op jit(solution)/shard_map/ppermute | solution.py:28
  132.4 24.4 %all-to-all-start = ((bf16[8,192,192]{2,1,0:T(8,128)(2,1)}), bf16[8,192,192]{2,1,0:T(8,128)(2,1)S(1)}, u32[]{:S(2)}, u32[]{:S(2)}) async-start(bf16[8,192,192]{2,1,0:T(8,128)(2,1)} %bitcast.349), calls=%async_computation | async-start | bytes 1572864 | tf_op jit(solution)/shard_map/all_to_all | solution.py:381
  136.8 182.3 %reduce-scatter.3.cloned.1.call-start = ((), (), s32[]{:S(2)}) async-start(), calls=%async_computation.4 | async-start | bytes 2654208 | tf_op jit(solution)/shard_map/reduce_scatter | solution.py:418
  176.0 3.1 collective-permute-start.15
  179.0 15.0 %copy-start.14 = (bf16[16,96,768]{2,1,0:T(8,128)(2,1)}, bf16[16,96,768]{2,1,0:T(8,128)(2,1)S(1)}, u32[]{:S(2)}) copy-start(bf16[16,96,768]{2,1,0:T(8,128)(2,1)S(1)} %slice.342) | copy-start | bytes 7077892
  179.1 15.0 %copy-start.31 = (bf16[384,768]{1,0:T(8,128)(2,1)}, bf16[384,768]{1,0:T(8,128)(2,1)S(1)}, u32[]{:S(2)}) copy-start(bf16[384,768]{1,0:T(8,128)(2,1)S(1)} %collective-permute-done.15) | copy-start | bytes 1769476
  197.6 2.1 collective-permute-start.16
  203.9 2.1 collective-permute-start.17
  224.1 5.5 %collective-permute-start.18 = (bf16[384,768]{1,0:T(8,128)(2,1)}, bf16[384,768]{1,0:T(8,128)(2,1)}, u32[]{:S(2)}, u32[]{:S(2)}) collective-permute-start(bf16[384,768]{1,0:T(8,128)(2,1)} %slice.504), channel_id=1, source_target_pairs={{0,1},{1,0},{2,3},{3,2},{4,5},{5,4},{6,7},{7,6},{8,9},{9,8},{10,11... | collective-permute-start | bytes 1769480 | tf_op jit(solution)/shard_map/ppermute | solution.py:28
  236.3 24.7 %all-to-all-start.1 = ((bf16[8,192,192]{2,1,0:T(8,128)(2,1)}), bf16[8,192,192]{2,1,0:T(8,128)(2,1)S(1)}, u32[]{:S(2)}, u32[]{:S(2)}) async-start(bf16[8,192,192]{2,1,0:T(8,128)(2,1)} %bitcast.72), calls=%async_computation.1 | async-start | bytes 1572864 | tf_op jit(solution)/shard_map/all_to_all | solution.py:381
  240.0 124.3 %reduce-scatter.5.cloned.1.call-start = ((), (), s32[]{:S(2)}) async-start(), calls=%async_computation.5 | async-start | bytes 3428352 | tf_op jit(solution)/shard_map/reduce_scatter | solution.py:418
  242.8 1.9 collective-permute-start.19
  242.9 5.4 %collective-permute-start.20 = (bf16[384,768]{1,0:T(8,128)(2,1)S(1)}, bf16[384,768]{1,0:T(8,128)(2,1)}, u32[]{:S(2)}, u32[]{:S(2)}) collective-permute-start(bf16[384,768]{1,0:T(8,128)(2,1)S(1)} %get-tuple-element.60), channel_id=1, source_target_pairs={{0,1},{1,0},{2,3},{3,2},{4,5},{5,4},{6,7},{7,6},{8,9},{9,8},{10,11... | collective-permute-start | bytes 1769480 | tf_op jit(solution)/shard_map/ppermute | solution.py:28
  312.3 3.1 collective-permute-start.21
  319.1 45.7 %copy-start.28 = (bf16[32,24,576]{2,1,0:T(8,128)(2,1)S(1)}, bf16[32,24,576]{2,1,0:T(8,128)(2,1)}, u32[]{:S(2)}) copy-start(bf16[32,24,576]{2,1,0:T(8,128)(2,1)} %slice.323) | copy-start | bytes 2654212
  372.7 9.9 %collective-permute-start.35 = (bf16[192,768]{1,0:T(8,128)(2,1)S(1)}, bf16[192,768]{1,0:T(8,128)(2,1)S(1)}, u32[]{:S(2)}, u32[]{:S(2)}) collective-permute-start(bf16[192,768]{1,0:T(8,128)(2,1)S(1)} %bitcast.365), channel_id=1, source_target_pairs={{0,16},{16,0},{1,17},{17,1},{2,18},{18,2},{3,19},{19,3},{4,20},{20... | collective-permute-start | bytes 884744 | tf_op jit(solution)/shard_map/ppermute | solution.py:28
  374.3 14.2 %collective-permute-start.33 = (bf16[248,768]{1,0:T(8,128)(2,1)S(1)}, bf16[248,768]{1,0:T(8,128)(2,1)S(1)}, u32[]{:S(2)}, u32[]{:S(2)}) collective-permute-start(bf16[248,768]{1,0:T(8,128)(2,1)S(1)} %bitcast.358), channel_id=1, source_target_pairs={{0,16},{16,0},{1,17},{17,1},{2,18},{18,2},{3,19},{19,3},{4,20},{20... | collective-permute-start | bytes 1142792 | tf_op jit(solution)/shard_map/ppermute | solution.py:28
  375.9 14.5 %collective-permute-start.27 = (bf16[2,2,1,2,56,576]{5,4,3,1,0,2:T(8,128)(2,1)}, bf16[2,2,1,2,56,576]{5,4,3,1,0,2:T(8,128)(2,1)}, u32[]{:S(2)}, u32[]{:S(2)}) collective-permute-start(bf16[2,2,1,2,56,576]{5,4,3,1,0,2:T(8,128)(2,1)} %fusion.38), channel_id=1, source_target_pairs={{0,1},{1,0},{2,3},{3,2},{4,5},{5,4},{6,7},{7,6},{8,9},{9,8},{10,11... | collective-permute-start | bytes 1548296 | tf_op jit(solution)/shard_map/ppermute | solution.py:28
  375.9 21.8 %collective-permute-start.24 = (bf16[2,2,192,384]{3,2,1,0:T(8,128)(2,1)}, bf16[2,2,192,384]{3,2,1,0:T(8,128)(2,1)}, u32[]{:S(2)}, u32[]{:S(2)}) collective-permute-start(bf16[2,2,192,384]{3,2,1,0:T(8,128)(2,1)} %fusion.33), channel_id=1, source_target_pairs={{0,4},{1,5},{2,6},{3,7},{4,0},{5,1},{6,2},{7,3},{8,12},{9,13},{10,... | collective-permute-start | bytes 1769480 | tf_op jit(solution)/shard_map/ppermute | solution.py:28
  377.8 22.8 %collective-permute-start.22 = (bf16[2,2,192,384]{3,2,0,1:T(8,128)(2,1)}, bf16[2,2,192,384]{3,2,0,1:T(8,128)(2,1)}, u32[]{:S(2)}, u32[]{:S(2)}) collective-permute-start(bf16[2,2,192,384]{3,2,0,1:T(8,128)(2,1)} %fusion.32), channel_id=1, source_target_pairs={{0,2},{1,3},{2,0},{3,1},{4,6},{5,7},{6,4},{7,5},{8,10},{9,11},{10,... | collective-permute-start | bytes 1769480 | tf_op jit(solution)/shard_map/ppermute | solution.py:28
  389.1 4.9 %collective-permute-start.34 = (bf16[104,768]{1,0:T(8,128)(2,1)S(1)}, bf16[104,768]{1,0:T(8,128)(2,1)S(1)}, u32[]{:S(2)}, u32[]{:S(2)}) collective-permute-start(bf16[104,768]{1,0:T(8,128)(2,1)S(1)} %pad_maximum_fusion.13), channel_id=1, source_target_pairs={{0,1},{1,0},{2,3},{3,2},{4,5},{5,4},{6,7},{7,6},{8,9},{9,8},{10,11... | collective-permute-start | bytes 479240 | tf_op jit(solution)/shard_map/ppermute | solution.py:28
  391.7 16.4 %collective-permute-start.28 = (bf16[2,2,56,576]{3,2,1,0:T(8,128)(2,1)S(1)}, bf16[2,2,56,576]{3,2,1,0:T(8,128)(2,1)S(1)}, u32[]{:S(2)}, u32[]{:S(2)}) collective-permute-start(bf16[2,2,56,576]{3,2,1,0:T(8,128)(2,1)S(1)} %fusion.44), channel_id=1, source_target_pairs={{0,8},{1,9},{2,10},{3,11},{4,12},{5,13},{6,14},{7,15},{8,0},{9,1},... | collective-permute-start | bytes 774152 | tf_op jit(solution)/shard_map/ppermute | solution.py:28
  399.9 9.9 %collective-permute-start.25 = (bf16[2,192,384]{2,1,0:T(8,128)(2,1)S(1)}, bf16[2,192,384]{2,1,0:T(8,128)(2,1)S(1)}, u32[]{:S(2)}, u32[]{:S(2)}) collective-permute-start(bf16[2,192,384]{2,1,0:T(8,128)(2,1)S(1)} %fusion.41), channel_id=1, source_target_pairs={{0,2},{1,3},{2,0},{3,1},{4,6},{5,7},{6,4},{7,5},{8,10},{9,11},{10,... | collective-permute-start | bytes 884744 | tf_op jit(solution)/shard_map/ppermute | solution.py:28
  402.0 12.3 %collective-permute-start.23 = (bf16[2,192,384]{2,1,0:T(8,128)(2,1)S(1)}, bf16[2,192,384]{2,1,0:T(8,128)(2,1)S(1)}, u32[]{:S(2)}, u32[]{:S(2)}) collective-permute-start(bf16[2,192,384]{2,1,0:T(8,128)(2,1)S(1)} %fusion.40), channel_id=1, source_target_pairs={{0,4},{1,5},{2,6},{3,7},{4,0},{5,1},{6,2},{7,3},{8,12},{9,13},{10,... | collective-permute-start | bytes 884744 | tf_op jit(solution)/shard_map/ppermute | solution.py:28
  408.2 8.4 %collective-permute-start.29 = (bf16[2,2,56,576]{3,2,1,0:T(8,128)(2,1)S(1)}, bf16[2,2,56,576]{3,2,1,0:T(8,128)(2,1)S(1)}, u32[]{:S(2)}, u32[]{:S(2)}) collective-permute-start(bf16[2,2,56,576]{3,2,1,0:T(8,128)(2,1)S(1)} %fusion.50), channel_id=1, source_target_pairs={{0,16},{16,0},{1,17},{17,1},{2,18},{18,2},{3,19},{19,3},{4,20},{20... | collective-permute-start | bytes 774152 | tf_op jit(solution)/shard_map/ppermute | solution.py:28
  415.3 15.8 %collective-permute-start.26 = (bf16[192,768]{1,0:T(8,128)(2,1)}, bf16[192,768]{1,0:T(8,128)(2,1)}, u32[]{:S(2)}, u32[]{:S(2)}) collective-permute-start(bf16[192,768]{1,0:T(8,128)(2,1)} %fusion.42), channel_id=1, source_target_pairs={{0,8},{1,9},{2,10},{3,11},{4,12},{5,13},{6,14},{7,15},{8,0},{9,1},... | collective-permute-start | bytes 884744 | tf_op jit(solution)/shard_map/ppermute | solution.py:28
  416.8 7.8 %collective-permute-start.32 = (bf16[56,576]{1,0:T(8,128)(2,1)S(1)}, bf16[56,576]{1,0:T(8,128)(2,1)S(1)}, u32[]{:S(2)}, u32[]{:S(2)}) collective-permute-start(bf16[56,576]{1,0:T(8,128)(2,1)S(1)} %get-tuple-element.109), channel_id=1, source_target_pairs={{0,6},{1,7},{2,4},{3,5},{4,2},{5,3},{6,0},{7,1},{8,14},{9,15},{10,... | collective-permute-start | bytes 193544 | tf_op jit(solution)/shard_map/ppermute | solution.py:28
  419.1 6.2 %collective-permute-start.31 = (bf16[56,576]{1,0:T(8,128)(2,1)S(1)}, bf16[56,576]{1,0:T(8,128)(2,1)S(1)}, u32[]{:S(2)}, u32[]{:S(2)}) collective-permute-start(bf16[56,576]{1,0:T(8,128)(2,1)S(1)} %get-tuple-element.110), channel_id=1, source_target_pairs={{0,4},{1,5},{2,6},{3,7},{4,0},{5,1},{6,2},{7,3},{8,12},{9,13},{10,... | collective-permute-start | bytes 193544 | tf_op jit(solution)/shard_map/ppermute | solution.py:28
  420.5 4.9 %collective-permute-start.30 = (bf16[56,576]{1,0:T(8,128)(2,1)S(1)}, bf16[56,576]{1,0:T(8,128)(2,1)S(1)}, u32[]{:S(2)}, u32[]{:S(2)}) collective-permute-start(bf16[56,576]{1,0:T(8,128)(2,1)S(1)} %get-tuple-element.111), channel_id=1, source_target_pairs={{0,2},{1,3},{2,0},{3,1},{4,6},{5,7},{6,4},{7,5},{8,10},{9,11},{10,... | collective-permute-start | bytes 193544 | tf_op jit(solution)/shard_map/ppermute | solution.py:28
  (43 other events, 231.2 us)
Sparse Core Ops, SparseCore 0:
  22.2 76.4 all-gather.2
  212.8 74.8 reduce-scatter.2
  291.4 72.9 reduce-scatter.4
